TPU v7x, 32 devices: a whole 2x2x4 slice. The times are simulated.
32 devices in a mesh: shard: 2 (over y), context: 4 (over z), tensor: 4 (over x, core).
Axes of the slice: x: 2, y: 2, z: 4, core: 2. Of those that a mesh axis runs over, the one named last changes fastest.
Arguments:
- hidden_in: bfloat16 [8192, 1024], P(('shard', 'context')), may hold values from -6 to 6
- segment_ids: int32 [2, 4096], P('shard', 'context'), may hold values from 0 to 15, never falling along the last dimension, each value on 1 to 2048 neighbouring positions
- cotangent: bfloat16 [8192, 1024], P(('shard', 'context')), may hold values from -6 to 6
- qkv_weight: bfloat16 [2, 1024, 3, 1024], P(None, 'shard', None, 'tensor'), may hold values from -0.1875 to 0.1875
- merge_weight: bfloat16 [2, 1024, 1024], P(None, 'tensor', 'shard'), may hold values from -0.75 to 0.75
- up_weight: bfloat16 [2, 1024, 4096], P(None, 'shard', 'tensor'), may hold values from -0.1875 to 0.1875
- down_weight: bfloat16 [2, 4096, 1024], P(None, 'tensor', 'shard'), may hold values from -0.1875 to 0.1875
- row_gains: bfloat16 [2, 2, 1024], P(None, None, 'shard'), may hold values from 0.5 to 1.5
- row_bias: bfloat16 [2, 4, 1024], P(None, None, 'shard'), may hold values from -4 to 4
- head_bias: bfloat16 [2, 2, 1024], P(None, None, 'tensor'), may hold values from -4 to 4
- up_bias: bfloat16 [2, 4096], P(None, 'tensor'), may hold values from -6 to 6
Outputs:
- hidden_out: bfloat16 [8192, 1024], P(('shard', 'context'))
- input_grad: float32 [8192, 1024], P(('shard', 'context'))
- grad_qkv: float32 [2, 1024, 3, 1024], P(None, 'shard', None, 'tensor')
- grad_merge: float32 [2, 1024, 1024], P(None, 'tensor', 'shard')
- grad_up: float32 [2, 1024, 4096], P(None, 'shard', 'tensor')
- grad_down: float32 [2, 4096, 1024], P(None, 'tensor', 'shard')
- grad_gains: float32 [2, 2, 1024], P(None, None, 'shard')
- grad_shifts: float32 [2, 4, 1024], P(None, None, 'shard')
- grad_heads: float32 [2, 2, 1024], P(None, None, 'tensor')
- grad_hidden: float32 [2, 4096], P(None, 'tensor')
Inputs may be any that keep to these rules, and one draw needn't show every extreme that they name: `segment_ids`: in each sequence the document numbers never fall and take every value of 0 to 15; each document has 1 to 2048 tokens, and one has exactly 2048.
All inputs are finite; a program needn't handle non-finite values.
Results may differ from a plain program's by a relative error of at most 0.035.
Values may be sent and summed in bfloat16 or wider, within the bound.
No kernel may reach another device: no remote copies, remote signals or barrier semaphores. Data moves between devices by JAX's collectives and lax.ppermute only.
A program may use at most 320 MiB of HBM per device.

v0:
```python
import jax
import jax.numpy as jnp
from jax import lax
from jax.sharding import PartitionSpec as P

HEAD_DIM = 64


HIGH_NEG = -1e30
EPSILON = 1e-05


def layer_norm(value, gain, shift):
    center = value - jnp.mean(value, axis=-1, keepdims=True)
    spread = jnp.mean(center * center, axis=-1, keepdims=True)
    return center * lax.rsqrt(spread + EPSILON) * gain + shift


def exact_gelu(value):
    return jax.nn.gelu(value, approximate=False)


def fetch_layer(qkv_weight, up_weight, merge_weight, down_weight, row_gains, row_bias, layer):
    return (
        lax.all_gather(qkv_weight[layer], "shard", axis=0, tiled=True),
        lax.all_gather(up_weight[layer], "shard", axis=0, tiled=True),
        lax.all_gather(merge_weight[layer], "shard", axis=1, tiled=True),
        lax.all_gather(down_weight[layer], "shard", axis=1, tiled=True),
        lax.all_gather(row_gains[layer], "shard", axis=1, tiled=True),
        lax.all_gather(row_bias[layer], "shard", axis=1, tiled=True),
    )


def forward_total(partial_sum):
    return lax.psum(partial_sum.astype(jnp.bfloat16), "tensor").astype(jnp.float32)


def backward_total(partial_sum):
    return lax.psum(partial_sum.astype(jnp.bfloat16), "tensor").astype(jnp.float32)


def norm_totals(g_gains, g_shifts):
    return (g_gains, g_shifts)


def shard_total(grads):
    return (
        lax.psum_scatter(
            grads[0].astype(jnp.bfloat16), "shard", scatter_dimension=0, tiled=True
        ).astype(jnp.float32),
        lax.psum_scatter(
            grads[1].astype(jnp.bfloat16), "shard", scatter_dimension=0, tiled=True
        ).astype(jnp.float32),
        lax.psum_scatter(
            grads[2].astype(jnp.bfloat16), "shard", scatter_dimension=1, tiled=True
        ).astype(jnp.float32),
        lax.psum_scatter(
            grads[3].astype(jnp.bfloat16), "shard", scatter_dimension=1, tiled=True
        ).astype(jnp.float32),
        lax.psum_scatter(
            grads[4].astype(jnp.bfloat16), "shard", scatter_dimension=1, tiled=True
        ).astype(jnp.float32),
        lax.psum_scatter(
            grads[5].astype(jnp.bfloat16), "shard", scatter_dimension=1, tiled=True
        ).astype(jnp.float32),
    )


def context_total(grads):
    return (
        lax.psum(grads[0].astype(jnp.bfloat16), "context").astype(jnp.float32),
        lax.psum(grads[1].astype(jnp.bfloat16), "context").astype(jnp.float32),
        lax.psum(grads[2].astype(jnp.bfloat16), "context").astype(jnp.float32),
        lax.psum(grads[3].astype(jnp.bfloat16), "context").astype(jnp.float32),
        lax.psum(grads[4].astype(jnp.bfloat16), "context").astype(jnp.float32),
        lax.psum(grads[5].astype(jnp.bfloat16), "context").astype(jnp.float32),
    )


def split_blocks(array, block):
    return array.reshape((array.shape[0] // block, block) + array.shape[1:])


def masked_scores(q_block, seg_block, key_heads, seg_all):
    scores = jnp.einsum("qhd,khd->hqk", q_block, key_heads, preferred_element_type=jnp.float32)
    same = seg_block[:, None] == seg_all[None, :]
    return jnp.where(same[None], scores, HIGH_NEG)


def attend_forward(query, key_heads, value_heads, seg_rows, seg_all):
    rows, heads, width = query.shape
    block = min(512, rows)

    def one_block(args):
        q_block, seg_block = args
        scores = masked_scores(q_block, seg_block, key_heads, seg_all)
        top = jnp.max(scores, axis=-1, keepdims=True)
        weights = jnp.exp(scores - top)
        total = jnp.sum(weights, axis=-1, keepdims=True)
        probs = (weights / total).astype(jnp.bfloat16)
        context = jnp.einsum("hqk,khd->qhd", probs, value_heads, preferred_element_type=jnp.float32)
        return (context.astype(jnp.bfloat16), top[..., 0] + jnp.log(total[..., 0]))

    context, lse = lax.map(one_block, (split_blocks(query, block), split_blocks(seg_rows, block)))
    return (context.reshape(rows, heads * width), lse)


def attend_backward(query, key_heads, value_heads, seg_rows, seg_all, lse, d_context):
    rows, heads, width = query.shape
    block = min(512, rows)

    def one_block(carry, args):
        key_sum, value_sum = carry
        q_block, seg_block, lse_block, d_block = args
        scores = masked_scores(q_block, seg_block, key_heads, seg_all)
        probs = jnp.exp(scores - lse_block[..., None])
        d_probs = jnp.einsum(
            "qhd,khd->hqk", d_block, value_heads, preferred_element_type=jnp.float32
        )
        delta = jnp.sum(probs * d_probs, axis=-1, keepdims=True)
        d_scores = (probs * (d_probs - delta)).astype(jnp.bfloat16)
        d_query = jnp.einsum(
            "hqk,khd->qhd", d_scores, key_heads, preferred_element_type=jnp.float32
        )
        key_sum = key_sum + jnp.einsum(
            "hqk,qhd->khd", d_scores, q_block, preferred_element_type=jnp.float32
        )
        value_sum = value_sum + jnp.einsum(
            "hqk,qhd->khd", probs.astype(jnp.bfloat16), d_block, preferred_element_type=jnp.float32
        )
        return ((key_sum, value_sum), d_query)

    empty = jnp.zeros(key_heads.shape, jnp.float32)
    shaped_grad = d_context.reshape(rows, heads, width)
    (key_sum, value_sum), d_query = lax.scan(
        one_block,
        (empty, empty),
        (
            split_blocks(query, block),
            split_blocks(seg_rows, block),
            lse,
            split_blocks(shaped_grad, block),
        ),
    )
    total_rows = key_heads.shape[0]
    return (
        d_query.reshape(rows, heads * width),
        key_sum.reshape(total_rows, heads * width),
        value_sum.reshape(total_rows, heads * width),
    )


def shards(
    hidden_in,
    segment_ids,
    cotangent,
    qkv_weight,
    merge_weight,
    up_weight,
    down_weight,
    row_gains,
    row_bias,
    head_bias,
    up_bias,
):
    layers = qkv_weight.shape[0]
    scale = HEAD_DIM ** (-0.5)
    rows = hidden_in.shape[0]
    seg_rows = segment_ids[0]
    x_value = hidden_in.astype(jnp.float32)
    x_low = hidden_in
    saved = []
    for layer in range(layers):
        gathered = fetch_layer(
            qkv_weight, up_weight, merge_weight, down_weight, row_gains, row_bias, layer
        )
        w_qkv, w_up, w_merge, w_down = (gathered[0], gathered[1], gathered[2], gathered[3])
        gains = gathered[4].astype(jnp.float32)
        biases = gathered[5].astype(jnp.float32)
        bias_heads = head_bias[layer].astype(jnp.float32)
        projected = jnp.einsum("rd,dcj->rcj", x_low, w_qkv, preferred_element_type=jnp.float32)
        query = ((projected[:, 0] + bias_heads[0]) * scale).astype(jnp.bfloat16)
        key = projected[:, 1].astype(jnp.bfloat16)
        value = (projected[:, 2] + bias_heads[1]).astype(jnp.bfloat16)
        key_all, value_all, seg_all = (
            lax.all_gather(key, "context", axis=0, tiled=True),
            lax.all_gather(value, "context", axis=0, tiled=True),
            lax.all_gather(segment_ids, "context", axis=1, tiled=True),
        )
        heads = key.shape[1] // HEAD_DIM
        shaped_query = query.reshape(rows, heads, HEAD_DIM)
        key_heads = key_all.reshape(-1, heads, HEAD_DIM)
        value_heads = value_all.reshape(-1, heads, HEAD_DIM)
        context, lse = attend_forward(shaped_query, key_heads, value_heads, seg_rows, seg_all[0])
        mixed = (
            x_value
            + forward_total(jnp.dot(context, w_merge, preferred_element_type=jnp.float32))
            + biases[0]
        )
        normed = layer_norm(mixed, gains[0], biases[1])
        normed_low = normed.astype(jnp.bfloat16)
        pre = jnp.dot(normed_low, w_up, preferred_element_type=jnp.float32) + up_bias[layer].astype(
            jnp.float32
        )
        act = exact_gelu(pre).astype(jnp.bfloat16)
        summed = (
            normed
            + forward_total(jnp.dot(act, w_down, preferred_element_type=jnp.float32))
            + biases[2]
        )
        output = layer_norm(summed, gains[1], biases[3])
        kept = None
        saved.append(
            (
                x_low,
                shaped_query,
                key_heads,
                value_heads,
                seg_all[0],
                lse,
                context,
                mixed,
                normed_low,
                pre,
                act,
                summed,
                kept,
            )
        )
        x_value = output
        x_low = output.astype(jnp.bfloat16)
    hidden_out = x_low
    d_out = cotangent.astype(jnp.float32)
    reduced_all = [None] * layers
    bias_all = [None] * layers
    for layer in reversed(range(layers)):
        (
            x_low,
            shaped_query,
            key_heads,
            value_heads,
            seg_all,
            lse,
            context,
            mixed,
            normed_low,
            pre,
            act,
            summed,
            kept,
        ) = saved[layer]
        gathered = fetch_layer(
            qkv_weight, up_weight, merge_weight, down_weight, row_gains, row_bias, layer
        )
        w_qkv, w_up, w_merge, w_down = (gathered[0], gathered[1], gathered[2], gathered[3])
        gains = gathered[4].astype(jnp.float32)
        biases = gathered[5].astype(jnp.float32)
        _, second_back = jax.vjp(layer_norm, summed, gains[1], biases[3])
        d_summed, d_gain_two, d_shift_four = second_back(d_out)
        d_down_low = d_summed.astype(jnp.bfloat16)
        g_down = jnp.einsum("rf,rd->fd", act, d_down_low, preferred_element_type=jnp.float32)
        d_act = jnp.einsum("rd,fd->rf", d_down_low, w_down, preferred_element_type=jnp.float32)
        _, gelu_back = jax.vjp(exact_gelu, pre)
        d_pre = gelu_back(d_act)[0].astype(jnp.bfloat16)
        g_up = jnp.einsum("rd,rf->df", normed_low, d_pre, preferred_element_type=jnp.float32)
        g_hidden = jnp.sum(d_pre.astype(jnp.float32), axis=0)
        d_normed = d_summed + backward_total(
            jnp.einsum("rf,df->rd", d_pre, w_up, preferred_element_type=jnp.float32)
        )
        _, first_back = jax.vjp(layer_norm, mixed, gains[0], biases[1])
        d_mixed, d_gain_one, d_shift_two = first_back(d_normed)
        d_mixed_low = d_mixed.astype(jnp.bfloat16)
        g_merge = jnp.einsum("rj,rd->jd", context, d_mixed_low, preferred_element_type=jnp.float32)
        d_context = jnp.einsum(
            "rd,jd->rj", d_mixed_low, w_merge, preferred_element_type=jnp.float32
        ).astype(jnp.bfloat16)
        d_query, key_sum, value_sum = attend_backward(
            shaped_query, key_heads, value_heads, seg_rows, seg_all, lse, d_context
        )
        d_key, d_value = (
            lax.psum_scatter(
                key_sum.astype(jnp.bfloat16), "context", scatter_dimension=0, tiled=True
            ).astype(jnp.float32),
            lax.psum_scatter(
                value_sum.astype(jnp.bfloat16), "context", scatter_dimension=0, tiled=True
            ).astype(jnp.float32),
        )
        d_proj = jnp.stack(
            [
                d_query.astype(jnp.bfloat16) * scale,
                d_key.astype(jnp.bfloat16),
                d_value.astype(jnp.bfloat16),
            ],
            axis=1,
        )
        g_qkv = jnp.einsum("rd,rcj->dcj", x_low, d_proj, preferred_element_type=jnp.float32)
        g_heads = jnp.stack(
            [
                jnp.sum(d_proj[:, 0].astype(jnp.float32), axis=0),
                jnp.sum(d_proj[:, 2].astype(jnp.float32), axis=0),
            ]
        )
        g_gains, g_shifts = norm_totals(
            jnp.stack([d_gain_one, d_gain_two]),
            jnp.stack(
                [jnp.sum(d_mixed, axis=0), d_shift_two, jnp.sum(d_summed, axis=0), d_shift_four]
            ),
        )
        d_out = d_mixed + backward_total(
            jnp.einsum("rcj,dcj->rd", d_proj, w_qkv, preferred_element_type=jnp.float32)
        )
        local_grads = (g_qkv, g_up, g_merge, g_down, g_gains, g_shifts)
        reduced = context_total(shard_total(local_grads))
        reduced_all[layer] = reduced
        bias_all[layer] = lax.psum((g_heads, g_hidden), ("shard", "context"))
    grad_qkv = jnp.stack([item[0] for item in reduced_all])
    grad_up = jnp.stack([item[1] for item in reduced_all])
    grad_merge = jnp.stack([item[2] for item in reduced_all])
    grad_down = jnp.stack([item[3] for item in reduced_all])
    grad_gains = jnp.stack([item[4] for item in reduced_all])
    grad_shifts = jnp.stack([item[5] for item in reduced_all])
    grad_heads = jnp.stack([item[0] for item in bias_all])
    grad_hidden = jnp.stack([item[1] for item in bias_all])
    return (
        hidden_out,
        d_out,
        grad_qkv,
        grad_merge,
        grad_up,
        grad_down,
        grad_gains,
        grad_shifts,
        grad_heads,
        grad_hidden,
    )


def solution(mesh):
    return jax.shard_map(
        shards,
        mesh=mesh,
        in_specs=(
            P(("shard", "context"), None),
            P("shard", "context"),
            P(("shard", "context"), None),
            P(None, "shard", None, "tensor"),
            P(None, "tensor", "shard"),
            P(None, "shard", "tensor"),
            P(None, "tensor", "shard"),
            P(None, None, "shard"),
            P(None, None, "shard"),
            P(None, None, "tensor"),
            P(None, "tensor"),
        ),
        out_specs=(
            P(("shard", "context"), None),
            P(("shard", "context"), None),
            P(None, "shard", None, "tensor"),
            P(None, "tensor", "shard"),
            P(None, "shard", "tensor"),
            P(None, "tensor", "shard"),
            P(None, None, "shard"),
            P(None, None, "shard"),
            P(None, None, "tensor"),
            P(None, "tensor"),
        ),
        check_vma=False,
    )
```

profile of v0, /device:TPU:0, one launch (start us, length us, event | category | flops | bytes accessed | tf_op | source)
XLA Modules:
  0.0 2251.2 jit_solution(4304272434515088384)
XLA Ops:
  95.5 42.7 %all-gather.31.cloned.1.call-done = bf16[4096,1,256]{2,0,1:T(8,128)(2,1)} async-done(((bf16[1024,1,256]{2,0,1:T(8,128)(2,1)}), bf16[4096,1,256]{2,0,1:T(8,128)(2,1)}) %all-gather.31.cloned.1.call-update) | async-done | bytes 2097168 | tf_op jit(solution)/shard_map/all_gather | solution.py:186
  142.3 93.0 %while.54 = (s32[]{:T(128)}, bf16[2,512,4,64]{1,3,2,0:T(8,128)(2,1)S(1)}, f32[2,4,512]{2,1,0:T(4,128)S(1)}, s32[2,512]{1,0:T(2,128)S(1)}, s32[1,4096]{1,0:T(1,12...) while((s32[]{:T(128)}, ...), condition=%wide.region_3.4_spmd, body=%wide.region_0.3_spmd.sunk | while | flops 2225207296 | bytes 113858672 | solution.py:104
  255.1 34.6 %all-reduce.13.cloned.1.call-done = bf16[1024,1024]{1,0:T(8,128)(2,1)} async-done(((bf16[1024,1024]{1,0:T(8,128)(2,1)}), bf16[1024,1024]{1,0:T(8,128)(2,1)}) %all-reduce.13.cloned.1.call-update) | async-done | bytes 2097168 | tf_op jit(solution)/shard_map/psum | solution.py:35
  366.9 50.7 %all-reduce.15.cloned.1.call-done = bf16[1024,1024]{1,0:T(8,128)(2,1)} async-done(((bf16[1024,1024]{1,0:T(8,128)(2,1)}), bf16[1024,1024]{1,0:T(8,128)(2,1)}) %all-reduce.15.cloned.1.call-update) | async-done | bytes 2097168 | tf_op jit(solution)/shard_map/psum | solution.py:35
  465.4 33.0 %all-gather.27.cloned.1.call-done = bf16[4096,256]{1,0:T(8,128)(2,1)} async-done(((bf16[1024,256]{1,0:T(8,128)(2,1)}), bf16[4096,256]{1,0:T(8,128)(2,1)}) %all-gather.27.cloned.1.call-update) | async-done | bytes 2097168 | tf_op jit(solution)/shard_map/all_gather | solution.py:187
  502.9 42.2 %all-gather.39.cloned.1.call-done = bf16[4096,1,256]{2,0,1:T(8,128)(2,1)} async-done(((bf16[1024,1,256]{2,0,1:T(8,128)(2,1)}), bf16[4096,1,256]{2,0,1:T(8,128)(2,1)}) %all-gather.39.cloned.1.call-update) | async-done | bytes 2097168 | tf_op jit(solution)/shard_map/all_gather | solution.py:186
  549.2 93.0 %while.55 = (s32[]{:T(128)}, bf16[2,512,4,64]{1,3,2,0:T(8,128)(2,1)S(1)}, f32[2,4,512]{2,1,0:T(4,128)S(1)}, s32[2,512]{1,0:T(2,128)S(1)}, s32[1,4096]{1,0:T(1,12...) while((s32[]{:T(128)}, ...), condition=%wide.region_13.14_spmd, body=%wide.region_10.13_spmd.sunk | while | flops 2225207296 | bytes 113858672 | solution.py:104
  656.3 40.1 %all-reduce.17.cloned.1.call-done = bf16[1024,1024]{1,0:T(8,128)(2,1)} async-done(((bf16[1024,1024]{1,0:T(8,128)(2,1)}), bf16[1024,1024]{1,0:T(8,128)(2,1)}) %all-reduce.17.cloned.1.call-update) | async-done | bytes 2097168 | tf_op jit(solution)/shard_map/psum | solution.py:35
  771.2 51.5 %all-reduce.19.cloned.1.call-done = bf16[1024,1024]{1,0:T(8,128)(2,1)} async-done(((bf16[1024,1024]{1,0:T(8,128)(2,1)}), bf16[1024,1024]{1,0:T(8,128)(2,1)}) %all-reduce.19.cloned.1.call-update) | async-done | bytes 2097168 | tf_op jit(solution)/shard_map/psum | solution.py:35
  847.2 51.5 %all-reduce.21.cloned.1.call-done = bf16[1024,1024]{1,0:T(8,128)(2,1)} async-done(((bf16[1024,1024]{1,0:T(8,128)(2,1)}), bf16[1024,1024]{1,0:T(8,128)(2,1)}) %all-reduce.21.cloned.1.call-update) | async-done | bytes 2097168 | tf_op jit(solution)/shard_map/psum | solution.py:39
  912.8 208.2 %while.56 = (s32[]{:T(128)}, f32[4096,4,64]{0,2,1:T(8,128)}, f32[4096,4,64]{0,2,1:T(8,128)}, bf16[2,512,4,64]{1,3,2,0:T(8,128)(2,1)}, bf16[2,512,4,64]{1,3,2,0:T...) while((s32[]{:T(128)}, f32[4096,4,64]{0,2,1:T(8,128)}, ...), condition=%wide.region_27.28_spmd.clone, body=%wide.region_25.27_spmd.clone.sunk | while | flops 5475661824 | bytes 351877312 | solution.py:135
  1133.2 36.8 %reduce-scatter.25.cloned.1.call-done = bf16[1024,256]{1,0:T(8,128)(2,1)} async-done(((bf16[4096,256]{1,0:T(8,128)(2,1)}), bf16[1024,256]{1,0:T(8,128)(2,1)}) %reduce-scatter.25.cloned.1.call-update) | async-done | bytes 524304 | tf_op jit(solution)/shard_map/reduce_scatter | solution.py:281
  1170.0 45.9 %reduce-scatter.27.cloned.1.call-done = bf16[1024,256]{1,0:T(8,128)(2,1)} async-done(((bf16[4096,256]{1,0:T(8,128)(2,1)}), bf16[1024,256]{1,0:T(8,128)(2,1)}) %reduce-scatter.27.cloned.1.call-update) | async-done | bytes 524304 | tf_op jit(solution)/shard_map/reduce_scatter | solution.py:284
  1221.0 50.8 %all-reduce.23.cloned.1.call-done = bf16[1024,1024]{1,0:T(8,128)(2,1)} async-done(((bf16[1024,1024]{1,0:T(8,128)(2,1)}), bf16[1024,1024]{1,0:T(8,128)(2,1)}) %all-reduce.23.cloned.1.call-update) | async-done | bytes 2097168 | tf_op jit(solution)/shard_map/psum | solution.py:39
  1294.3 51.5 %all-reduce.25.cloned.1.call-done = bf16[1024,1024]{1,0:T(8,128)(2,1)} async-done(((bf16[1024,1024]{1,0:T(8,128)(2,1)}), bf16[1024,1024]{1,0:T(8,128)(2,1)}) %all-reduce.25.cloned.1.call-update) | async-done | bytes 2097168 | tf_op jit(solution)/shard_map/psum | solution.py:39
  1359.9 208.3 %while.57 = (s32[]{:T(128)}, f32[4096,4,64]{0,2,1:T(8,128)}, f32[4096,4,64]{0,2,1:T(8,128)}, bf16[2,512,4,64]{1,3,2,0:T(8,128)(2,1)}, bf16[2,512,4,64]{1,3,2,0:T...) while((s32[]{:T(128)}, f32[4096,4,64]{0,2,1:T(8,128)}, ...), condition=%wide.region_38.39_spmd.clone, body=%wide.region_36.38_spmd.clone.sunk | while | flops 5475661824 | bytes 351877312 | solution.py:135
  1579.8 37.4 %reduce-scatter.29.cloned.1.call-done = bf16[1024,256]{1,0:T(8,128)(2,1)} async-done(((bf16[4096,256]{1,0:T(8,128)(2,1)}), bf16[1024,256]{1,0:T(8,128)(2,1)}) %reduce-scatter.29.cloned.1.call-update) | async-done | bytes 524304 | tf_op jit(solution)/shard_map/reduce_scatter | solution.py:281
  1617.2 46.1 %reduce-scatter.31.cloned.1.call-done = bf16[1024,256]{1,0:T(8,128)(2,1)} async-done(((bf16[4096,256]{1,0:T(8,128)(2,1)}), bf16[1024,256]{1,0:T(8,128)(2,1)}) %reduce-scatter.31.cloned.1.call-update) | async-done | bytes 524304 | tf_op jit(solution)/shard_map/reduce_scatter | solution.py:284
  1736.6 34.0 %reduce-scatter.47.cloned.1.call-done = bf16[1024,512]{1,0:T(8,128)(2,1)} async-done(((bf16[1024,1024]{1,0:T(8,128)(2,1)}), bf16[1024,512]{1,0:T(8,128)(2,1)}) %reduce-scatter.47.cloned.1.call-update) | async-done | bytes 1048592 | tf_op jit(solution)/shard_map/reduce_scatter | solution.py:57
  1770.6 34.7 %reduce-scatter.43.cloned.1.call-done = bf16[512,1024]{1,0:T(8,128)(2,1)} async-done(((bf16[1024,1024]{1,0:T(8,128)(2,1)}), bf16[512,1024]{1,0:T(8,128)(2,1)}) %reduce-scatter.43.cloned.1.call-update) | async-done | bytes 1048592 | tf_op jit(solution)/shard_map/reduce_scatter | solution.py:51
  1850.3 34.2 %reduce-scatter.45.cloned.1.call-done = bf16[1024,512]{1,0:T(8,128)(2,1)} async-done(((bf16[1024,1024]{1,0:T(8,128)(2,1)}), bf16[1024,512]{1,0:T(8,128)(2,1)}) %reduce-scatter.45.cloned.1.call-update) | async-done | bytes 1048592 | tf_op jit(solution)/shard_map/reduce_scatter | solution.py:57
  1884.5 34.1 %reduce-scatter.41.cloned.1.call-done = bf16[512,1024]{1,0:T(8,128)(2,1)} async-done(((bf16[1024,1024]{1,0:T(8,128)(2,1)}), bf16[512,1024]{1,0:T(8,128)(2,1)}) %reduce-scatter.41.cloned.1.call-update) | async-done | bytes 1048592 | tf_op jit(solution)/shard_map/reduce_scatter | solution.py:51
  1989.8 37.9 %all-reduce = (f32[1,2,256]{2,1,0:T(2,128)S(1)}, f32[1,2,256]{2,1,0:T(2,128)S(1)}, f32[1,1024]{1,0:T(1,128)S(1)}, f32[1,1024]{1,0:T(1,128)S(1)}) all-reduce(f32[1,2,256]{2,1,0:T(2,128)S(1)} %maximum_bitcast_fusion.1, f32[1,2,256]{2,1,0:T(2,128)S(1)} %maximum_bitcast_fusion, ...), channel_id=1, replica_groups=mesh['shard'=2,'context'=4,'tensor'=4] {'shard','context'}, use_global_device_ids=true, to_apply=%region_83.84 | all-reduce | flops 3072 | bytes 24576 | tf_op jit(solution)/shard_map/psum | solution.py:315
  2047.3 184.9 %all-reduce.29.cloned.1.call-done = (bf16[1,512,3,256]{1,3,2,0:T(8,128)(2,1)}, bf16[1,512,3,256]{1,3,2,0:T(8,128)(2,1)}, bf16[1,256,512]{2,1,0:T(8,128)(2,1)}, b...) async-done(((bf16[1,512,3,256]{1,3,2,0:T(8,128)(2,1)}, ...) | async-done | bytes 6291472 | tf_op jit(solution)/shard_map/psum | solution.py:71
  (585 shorter events, 1258.7 us)
Async XLA Ops:
  45.9 243.8 %all-reduce.13.cloned.1.call-start = ((), (), s32[]{:S(2)}) async-start(), calls=%async_computation.17 | async-start | bytes 4194304 | tf_op jit(solution)/shard_map/psum | solution.py:35
  241.1 119.1 %all-gather.35.cloned.1.call-start = ((), (), s32[]{:S(2)}) async-start(), calls=%async_computation.41 | async-start | bytes 3145728 | tf_op jit(solution)/shard_map/all_gather | solution.py:28
  244.3 173.3 %all-reduce.15.cloned.1.call-start = ((), (), s32[]{:S(2)}) async-start(), calls=%async_computation.18 | async-start | bytes 4194304 | tf_op jit(solution)/shard_map/psum | solution.py:35
  366.8 131.5 %all-gather.27.cloned.1.call-start = ((), (), s32[]{:S(2)}) async-start(), calls=%async_computation.19 | async-start | bytes 2621440 | tf_op jit(solution)/shard_map/all_gather | solution.py:187
  453.3 243.2 %all-reduce.17.cloned.1.call-start = ((), (), s32[]{:S(2)}) async-start(), calls=%async_computation.20 | async-start | bytes 4194304 | tf_op jit(solution)/shard_map/psum | solution.py:35
  646.8 119.1 %all-gather.43.cloned.1.call-start = ((), (), s32[]{:S(2)}) async-start(), calls=%async_computation.45 | async-start | bytes 3145728 | tf_op jit(solution)/shard_map/all_gather | solution.py:28
  647.5 175.2 %all-reduce.19.cloned.1.call-start = ((), (), s32[]{:S(2)}) async-start(), calls=%async_computation.21 | async-start | bytes 4194304 | tf_op jit(solution)/shard_map/psum | solution.py:35
  771.2 127.5 %all-reduce.21.cloned.1.call-start = ((), (), s32[]{:S(2)}) async-start(), calls=%async_computation.22 | async-start | bytes 4194304 | tf_op jit(solution)/shard_map/psum | solution.py:39
  847.1 323.0 %reduce-scatter.25.cloned.1.call-start = ((), (), s32[]{:S(2)}) async-start(), calls=%async_computation.23 | async-start | bytes 2621440 | tf_op jit(solution)/shard_map/reduce_scatter | solution.py:281
  1131.0 140.8 %all-reduce.23.cloned.1.call-start = ((), (), s32[]{:S(2)}) async-start(), calls=%async_computation.25 | async-start | bytes 4194304 | tf_op jit(solution)/shard_map/psum | solution.py:39
  1220.9 125.0 %all-reduce.25.cloned.1.call-start = ((), (), s32[]{:S(2)}) async-start(), calls=%async_computation.26 | async-start | bytes 4194304 | tf_op jit(solution)/shard_map/psum | solution.py:39
  1294.3 322.9 %reduce-scatter.29.cloned.1.call-start = ((), (), s32[]{:S(2)}) async-start(), calls=%async_computation.27 | async-start | bytes 2621440 | tf_op jit(solution)/shard_map/reduce_scatter | solution.py:281
  1578.1 141.0 %all-reduce.27.cloned.1.call-start = ((), (), s32[]{:S(2)}) async-start(), calls=%async_computation.29 | async-start | bytes 4194304 | tf_op jit(solution)/shard_map/psum | solution.py:39
  1679.3 126.1 %reduce-scatter.43.cloned.1.call-start = ((), (), s32[]{:S(2)}) async-start(), calls=%async_computation.35 | async-start | bytes 3145728 | tf_op jit(solution)/shard_map/reduce_scatter | solution.py:51
  1686.4 147.2 %reduce-scatter.35.cloned.1.call-start = ((), (), s32[]{:S(2)}) async-start(), calls=%async_computation.31 | async-start | bytes 2359296 | tf_op jit(solution)/shard_map/reduce_scatter | solution.py:48
  1692.0 158.2 %reduce-scatter.37.cloned.1.call-start = ((), (), s32[]{:S(2)}) async-start(), calls=%async_computation.32 | async-start | bytes 786432 | tf_op jit(solution)/shard_map/reduce_scatter | solution.py:54
  1696.2 188.3 %reduce-scatter.45.cloned.1.call-start = ((), (), s32[]{:S(2)}) async-start(), calls=%async_computation.36 | async-start | bytes 3145728 | tf_op jit(solution)/shard_map/reduce_scatter | solution.py:57
  1703.1 215.5 %reduce-scatter.41.cloned.1.call-start = ((), (), s32[]{:S(2)}) async-start(), calls=%async_computation.34 | async-start | bytes 3145728 | tf_op jit(solution)/shard_map/reduce_scatter | solution.py:51
  1709.7 237.2 %reduce-scatter.33.cloned.1.call-start = ((), (), s32[]{:S(2)}) async-start(), calls=%async_computation.30 | async-start | bytes 2359296 | tf_op jit(solution)/shard_map/reduce_scatter | solution.py:48
  1714.0 246.9 %reduce-scatter.51.cloned.1.call-start = ((), (), s32[]{:S(2)}) async-start(), calls=%async_computation.47 | async-start | bytes 393216
  1717.0 257.8 %reduce-scatter.55.cloned.1.call-start = ((), (), s32[]{:S(2)}) async-start(), calls=%async_computation.49 | async-start | bytes 393216
  1718.1 270.6 %reduce-scatter.49.cloned.1.call-start = ((), (), s32[]{:S(2)}) async-start(), calls=%async_computation.46 | async-start | bytes 393216
  1719.1 309.8 %reduce-scatter.53.cloned.1.call-start = ((), (), s32[]{:S(2)}) async-start(), calls=%async_computation.48 | async-start | bytes 393216
  1725.6 506.6 %all-reduce.29.cloned.1.call-start = ((), (), s32[]{:S(2)}) async-start(), calls=%async_computation.50 | async-start | bytes 12582912 | tf_op jit(solution)/shard_map/psum | solution.py:71
  (144 other events, 5835.8 us)
Sparse Core Ops, SparseCore 0:
  45.0 46.2 all-gather.24
  93.4 44.6 all-gather.30
  239.6 50.0 all-reduce.12
  291.7 33.1 all-gather.32
  327.0 33.1 all-gather.34
  366.2 51.3 all-reduce.14
  452.4 45.9 all-gather.26
  500.4 44.6 all-gather.38
  646.3 50.0 all-reduce.16
  697.9 33.1 all-gather.40
  732.8 33.1 all-gather.42
  771.3 51.3 all-reduce.18
  847.2 51.4 all-reduce.20
  1126.1 43.9 reduce-scatter.24
  1172.8 43.1 reduce-scatter.26
  1221.0 50.6 all-reduce.22
  1294.4 51.4 all-reduce.24
  1573.2 43.9 reduce-scatter.28
  1620.1 43.1 reduce-scatter.30
  1668.4 50.6 all-reduce.26
  1773.5 31.8 reduce-scatter.42
  1852.6 31.8 reduce-scatter.44
  1886.7 31.8 reduce-scatter.40
  2006.2 226.0 all-reduce.28
  (11 shorter events, 216.3 us)
where the time goes:
time: 2260 us; the launch traced here: 2250 us
  waiting for transfers between devices  1230 us (54%)
  matrix products  547 us (24%)
  other arithmetic  263 us (12%)
  blocking collectives  101 us (4%)
  local copies, waits for them, and re-layouts  89.3 us (4%)
    psum x1, waiting for transfers between devices, context_total(): lax.psum(grads[0].astype(jnp.bfloat16), 'context').astype(jnp.float32)  185 us
    psum x4, waiting for transfers between devices, forward_total(): lax.psum(partial_sum.astype(jnp.bfloat16), 'tensor').astype(jnp.float32)  177 us
    psum x4, waiting for transfers between devices, backward_total(): lax.psum(partial_sum.astype(jnp.bfloat16), 'tensor').astype(jnp.float32)  154 us
    dot_general x8, matrix products, masked_scores(): jnp.einsum('qhd,khd->hqk', q_block, key_heads, preferred_element_type=jnp...  120 us
    convert_element_type x4, other arithmetic, one_block(): d_scores = (probs * (d_probs - delta)).astype(jnp.bfloat16)  111 us
    dot_general x4, matrix products, one_block(): jnp.einsum('qhd,khd->hqk', d_block, value_heads, preferred_element_type=j...  100 us
    reduce_scatter x2, waiting for transfers between devices, shards(): lax.psum_scatter(value_sum.astype(jnp.bfloat16), 'context', scatter_dimen...  92 us
    all_gather x2, waiting for transfers between devices, shards(): lax.all_gather(key, 'context', axis=0, tiled=True)  84.8 us
  transfers between devices with their start and end apart: 35, of which 33 were waited for; matrix products, arithmetic and copies ran while one was open for 7% of the time, Pallas kernels for 0%

commit v1 on v0

v1 whole, which is shorter than its diff:
```python
import functools
import math

import jax
import jax.numpy as jnp
from jax import lax
from jax.experimental import pallas as pl
from jax.experimental.pallas import tpu as pltpu
from jax.sharding import PartitionSpec as P

HEAD_DIM = 64
DOCS = 16
NEG = -1e30
EPSILON = 1e-05
CALM = 75.0
FAR = 1 << 24
F32 = jnp.float32
BF16 = jnp.bfloat16
SHARD = "shard"
CONTEXT = "context"
VMEM = pl.BlockSpec(memory_space=pltpu.VMEM)


def dot(a, b, ca, cb):
    return lax.dot_general(a, b, (((ca,), (cb,)), ((), ())), preferred_element_type=F32)


def params(mib=56):
    return pltpu.CompilerParams(vmem_limit_bytes=mib << 20)


def cost(flops, nbytes, trans=0):
    return pl.CostEstimate(flops=1, bytes_accessed=1, transcendentals=0)


def qkv_kernel(perm, cols, *refs, n_x, n_w):
    xs, bias_ref = refs[:n_x], refs[n_x]
    w_refs = refs[n_x + 1 : n_x + 1 + n_w]
    out_ref = refs[n_x + 1 + n_w]
    x_ref = xs[0]
    if n_x > 1:
        x_ref = refs[n_x + 2 + n_w]
        for i in range(n_x):

            @pl.when(pl.program_id(0) == i)
            def _():
                x_ref[...] = xs[i][...]

    scale = HEAD_DIM ** (-0.5)
    width = w_refs[0].shape[-1]
    for c in range(3):
        acc = None
        k = 0
        for w_ref in w_refs:
            deep = w_ref.shape[2]
            for i in range(w_ref.shape[0]):
                off = pl.multiple_of(cols[k] * deep, 128)
                part = dot(x_ref[:, pl.ds(off, deep)], w_ref[i, c], 1, 0)
                acc = part if acc is None else acc + part
                k += 1
        if c == 0:
            acc = (acc + bias_ref[0:1, :].astype(F32)) * scale
        if c == 2:
            acc = acc + bias_ref[1:2, :].astype(F32)
        turned = acc.T.astype(BF16)
        for h in range(width // HEAD_DIM):
            out_ref[h, c] = turned[h * HEAD_DIM : (h + 1) * HEAD_DIM]


def project(xs, weights, cols, bias, perm, piece):
    width = xs[0].shape[1]
    rows = sum(x.shape[0] for x in xs)
    hw = weights[0].shape[-1]
    heads = hw // HEAD_DIM
    out_shape = [jax.ShapeDtypeStruct((heads, 3, HEAD_DIM, rows), BF16)]
    out_specs = [pl.BlockSpec((heads, 3, HEAD_DIM, piece), lambda r, p, c: (0, 0, 0, p[r]))]
    x_specs = [pl.BlockSpec((piece, width), lambda r, p, c: (r, 0))]
    if len(xs) > 1:
        x_specs = [pl.BlockSpec((piece, width), lambda r, p, c: (0, 0))] * len(xs)
        out_shape.append(jax.ShapeDtypeStruct((rows, width), BF16))
        out_specs.append(pl.BlockSpec((piece, width), lambda r, p, c: (p[r], 0)))
    return pl.pallas_call(
        functools.partial(qkv_kernel, n_x=len(xs), n_w=len(weights)),
        grid_spec=pltpu.PrefetchScalarGridSpec(
            num_scalar_prefetch=2,
            grid=(rows // piece,),
            in_specs=x_specs
            + [pl.BlockSpec(bias.shape, lambda r, p, c: (0, 0))]
            + [pl.BlockSpec(w.shape, lambda r, p, c: (0, 0, 0, 0)) for w in weights],
            out_specs=out_specs,
        ),
        out_shape=out_shape,
        compiler_params=params(),
        cost_estimate=cost(2 * rows * width * 3 * hw, 2 * rows * width * 2 + 6 * width * hw),
        name="project",
    )(perm, cols, *xs, bias, *weights)


def back_kernel(perm, cols, *refs, n_w):
    d_ref = refs[0]
    w_refs = refs[1 : 1 + n_w]
    out_refs = refs[1 + n_w : -2]
    proj_ref, sum_ref = refs[-2:]
    heads = d_ref.shape[0]
    r = pl.program_id(0)
    first = r == 0

    @pl.when(first)
    def _():
        sum_ref[...] = jnp.zeros_like(sum_ref)

    parts = []
    for c in range(3):
        flat = jnp.concatenate([d_ref[h, c] for h in range(heads)], axis=0)
        turned = flat.astype(F32).T
        if c != 1:
            row = c // 2
            sum_ref[row : row + 1, :] += jnp.sum(turned, axis=0, keepdims=True)
        turned = turned.astype(BF16)
        proj_ref[c] = turned
        parts.append(turned)
    k = 0
    for w_ref in w_refs:
        deep = w_ref.shape[2]
        for i in range(w_ref.shape[0]):
            acc = dot(parts[0], w_ref[i, 0], 1, 1)
            acc = acc + dot(parts[1], w_ref[i, 1], 1, 1)
            acc = acc + dot(parts[2], w_ref[i, 2], 1, 1)
            off = pl.multiple_of(cols[k] * deep, 128)
            low = acc.astype(BF16)
            for n, out_ref in enumerate(out_refs):

                @pl.when(r == n)
                def _():
                    out_ref[:, pl.ds(off, deep)] = low

            k += 1


def project_back(d_heads, weights, cols, perm, piece, width):
    heads, _, _, rows = d_heads.shape
    blocks = rows // piece
    hw = heads * HEAD_DIM
    return pl.pallas_call(
        functools.partial(back_kernel, n_w=len(weights)),
        grid_spec=pltpu.PrefetchScalarGridSpec(
            num_scalar_prefetch=2,
            grid=(blocks,),
            in_specs=[pl.BlockSpec((heads, 3, HEAD_DIM, piece), lambda r, p, c: (0, 0, 0, p[r]))]
            + [pl.BlockSpec(w.shape, lambda r, p, c: (0, 0, 0, 0)) for w in weights],
            out_specs=[pl.BlockSpec((piece, width), lambda r, p, c: (0, 0))] * blocks
            + [
                pl.BlockSpec((3, piece, hw), lambda r, p, c: (0, p[r], 0)),
                pl.BlockSpec((2, hw), lambda r, p, c: (0, 0)),
            ],
        ),
        out_shape=[jax.ShapeDtypeStruct((piece, width), BF16)] * blocks
        + [
            jax.ShapeDtypeStruct((3, rows, hw), BF16),
            jax.ShapeDtypeStruct((2, hw), F32),
        ],
        compiler_params=params(),
        cost_estimate=cost(2 * rows * width * 3 * hw, 2 * rows * width * 2 + 6 * width * hw),
        name="project_back",
    )(perm, cols, d_heads, *weights)


def tile_kernel_index(tiles, t, size, bq, bk, chunk):
    q0 = pl.multiple_of(tiles[1 + t] * bq, bq)
    k0 = pl.multiple_of(tiles[1 + size + t] * bk, bk)
    cj, kj = q0 // chunk, k0 // chunk
    off = pl.multiple_of(q0 - cj * chunk, bq)
    ko = pl.multiple_of(k0 - kj * chunk, bk)
    return q0, k0, cj, off, kj, ko, tiles[1 + 2 * size + t]


def inside(spot, pos, start, length):
    place = (spot + (pos - start)).astype(jnp.uint32)
    return place < length.astype(jnp.uint32)


def attend_kernel(
    tiles,
    qkv,
    start,
    length,
    low,
    high,
    lse,
    keys,
    acc,
    total,
    top,
    *,
    bq,
    bk,
    seq,
    chunk,
    piece,
    unroll,
    size,
):
    n_chunks = seq // chunk
    q_most = jnp.zeros((1, chunk), F32)
    k_most = jnp.zeros((1, chunk), F32)
    for j in range(n_chunks):
        q = qkv[j, 0].astype(F32)
        k = qkv[j, 1].astype(F32)
        q_most = jnp.maximum(q_most, jnp.sum(q * q, axis=0, keepdims=True))
        k_most = jnp.maximum(k_most, jnp.sum(k * k, axis=0, keepdims=True))
        keys[j * chunk : (j + 1) * chunk, :] = k.T.astype(BF16)
    calm = jnp.max(q_most) * jnp.max(k_most) < CALM * CALM
    acc[...] = jnp.zeros_like(acc)
    total[...] = jnp.zeros_like(total)
    spot = lax.broadcasted_iota(jnp.int32, (bk, bq), 0)

    def tile(t):
        q0, k0, cj, off, kj, ko, pos = tile_kernel_index(tiles, t, size, bq, bk, chunk)
        s = dot(keys[pl.ds(k0, bk), :], qkv[cj, 0, :, pl.ds(off, bq)], 1, 0)
        ok = inside(spot, pos, start[:, pl.ds(q0, bq)], length[:, pl.ds(q0, bq)])
        return q0, kj, ko, s, ok

    @pl.when(calm)
    def _():
        top[...] = jnp.zeros_like(top)

        def step(i, _):
            group = [tile(i * unroll + u) for u in range(unroll)]
            for q0, kj, ko, s, ok in group:
                p = jnp.where(ok, jnp.exp(s), 0.0)
                total[:, pl.ds(q0, bq)] += jnp.sum(p, axis=0, keepdims=True)
                value = qkv[kj, 2, :, pl.ds(ko, bk)]
                acc[:, pl.ds(q0, bq)] += dot(value, p.astype(BF16), 1, 0)
            return 0

        lax.fori_loop(0, tiles[0], step, 0)

    @pl.when(jnp.logical_not(calm))
    def _():
        top[...] = jnp.full_like(top, NEG)

        def step(i, _):
            q0, kj, ko, s, ok = tile(i)
            s = jnp.where(ok, s, NEG)
            here = pl.ds(q0, bq)
            new = jnp.maximum(top[:, here], jnp.max(s, axis=0, keepdims=True))
            p = jnp.where(ok, jnp.exp(s - new), 0.0)
            fade = jnp.exp(top[:, here] - new)
            total[:, here] = total[:, here] * fade + jnp.sum(p, axis=0, keepdims=True)
            value = qkv[kj, 2, :, pl.ds(ko, bk)]
            acc[:, here] = acc[:, here] * fade + dot(value, p.astype(BF16), 1, 0)
            top[:, here] = new
            return 0

        lax.fori_loop(0, tiles[0] * unroll, step, 0)

    lse[...] = top[...] + jnp.log(total[...])
    for z in range(n_chunks):
        for t in range(chunk // piece):
            base = z * chunk + t * piece
            out = acc[:, base : base + piece] / total[:, base : base + piece]
            low[t * n_chunks + z] = out.astype(BF16)
            high[t * n_chunks + z] = out


def attend(qkv, doc, tiles, piece, bq, bk, unroll):
    n_chunks, _, hd, chunk = qkv.shape
    seq = n_chunks * chunk
    start, end = doc
    pieces = seq // piece
    return pl.pallas_call(
        functools.partial(
            attend_kernel,
            bq=bq,
            bk=bk,
            seq=seq,
            chunk=chunk,
            piece=piece,
            unroll=unroll,
            size=(tiles.shape[0] - 1) // 3,
        ),
        grid_spec=pltpu.PrefetchScalarGridSpec(
            num_scalar_prefetch=1,
            grid=(),
            in_specs=[VMEM] * 3,
            out_specs=[VMEM] * 3,
            scratch_shapes=[
                pltpu.VMEM((seq, hd), BF16),
                pltpu.VMEM((hd, seq), F32),
                pltpu.VMEM((1, seq), F32),
                pltpu.VMEM((1, seq), F32),
            ],
        ),
        out_shape=[
            jax.ShapeDtypeStruct((pieces, hd, piece), BF16),
            jax.ShapeDtypeStruct((pieces, hd, piece), F32),
            jax.ShapeDtypeStruct((1, seq), F32),
        ],
        compiler_params=params(40),
        cost_estimate=cost(2 * seq * seq * hd, 8 * seq * hd, seq * seq // 4),
        name="attend",
    )(tiles, qkv, start[None], (end - start)[None])


def attend_back_kernel(
    tiles,
    qkv,
    start,
    length,
    lse,
    ctx,
    d_ctx,
    out,
    keys,
    values,
    queries,
    grads,
    d_keys,
    d_values,
    d_queries,
    delta,
    d_turned,
    *,
    bq,
    bk,
    seq,
    chunk,
    piece,
    unroll,
    size,
):
    n_chunks = seq // chunk
    for j in range(n_chunks):
        sl = slice(j * chunk, (j + 1) * chunk)
        queries[sl, :] = qkv[j, 0].astype(F32).T.astype(BF16)
        keys[sl, :] = qkv[j, 1].astype(F32).T.astype(BF16)
        values[sl, :] = qkv[j, 2].astype(F32).T.astype(BF16)
    for at in range(seq // piece):
        t, z = at // n_chunks, at % n_chunks
        base = z * chunk + t * piece
        part = d_ctx[at].astype(F32)
        d_turned[:, base : base + piece] = d_ctx[at]
        grads[base : base + piece, :] = part.T.astype(BF16)
        delta[:, base : base + piece] = jnp.sum(part * ctx[at], axis=0, keepdims=True)
    d_queries[...] = jnp.zeros_like(d_queries)
    d_keys[...] = jnp.zeros_like(d_keys)
    d_values[...] = jnp.zeros_like(d_values)
    spot = lax.broadcasted_iota(jnp.int32, (bk, bq), 0)

    def tile(t):
        q0, k0, cj, off, kj, ko, pos = tile_kernel_index(tiles, t, size, bq, bk, chunk)
        s = dot(keys[pl.ds(k0, bk), :], qkv[cj, 0, :, pl.ds(off, bq)], 1, 0)
        dp = dot(values[pl.ds(k0, bk), :], d_turned[:, pl.ds(q0, bq)], 1, 0)
        ok = inside(spot, pos, start[:, pl.ds(q0, bq)], length[:, pl.ds(q0, bq)])
        return q0, k0, kj, ko, s, dp, ok

    def step(i, _):
        group = [tile(i * unroll + u) for u in range(unroll)]
        for q0, k0, kj, ko, s, dp, ok in group:
            here = pl.ds(q0, bq)
            there = pl.ds(k0, bk)
            p = jnp.where(ok, jnp.exp(s - lse[:, here]), 0.0)
            ds = (p * (dp - delta[:, here])).astype(BF16)
            d_values[there, :] += dot(p.astype(BF16), grads[here, :], 1, 0)
            d_keys[there, :] += dot(ds, queries[here, :], 1, 0)
            d_queries[:, here] += dot(qkv[kj, 1, :, pl.ds(ko, bk)], ds, 1, 0)
        return 0

    lax.fori_loop(0, tiles[0], step, 0)
    scale = HEAD_DIM ** (-0.5)
    for j in range(n_chunks):
        sl = slice(j * chunk, (j + 1) * chunk)
        out[j, 0] = (d_queries[:, sl].astype(BF16).astype(F32) * scale).astype(BF16)
        out[j, 1] = d_keys[sl, :].T.astype(BF16)
        out[j, 2] = d_values[sl, :].T.astype(BF16)


def attend_back(qkv, doc, tiles, lse, ctx, d_ctx, piece, bq, bk, unroll):
    n_chunks, _, hd, chunk = qkv.shape
    seq = n_chunks * chunk
    start, end = doc
    return pl.pallas_call(
        functools.partial(
            attend_back_kernel,
            bq=bq,
            bk=bk,
            seq=seq,
            chunk=chunk,
            piece=piece,
            unroll=unroll,
            size=(tiles.shape[0] - 1) // 3,
        ),
        grid_spec=pltpu.PrefetchScalarGridSpec(
            num_scalar_prefetch=1,
            grid=(),
            in_specs=[VMEM] * 6,
            out_specs=VMEM,
            scratch_shapes=[pltpu.VMEM((seq, hd), BF16)] * 4
            + [pltpu.VMEM((seq, hd), F32)] * 2
            + [
                pltpu.VMEM((hd, seq), F32),
                pltpu.VMEM((1, seq), F32),
                pltpu.VMEM((hd, seq), BF16),
            ],
        ),
        out_shape=jax.ShapeDtypeStruct((n_chunks, 3, hd, chunk), BF16),
        compiler_params=params(48),
        cost_estimate=cost(4 * seq * seq * hd, 16 * seq * hd, seq * seq // 4),
        name="attend_back",
    )(tiles, qkv, start[None], (end - start)[None], lse, ctx, d_ctx)


def document_bounds(seg):
    ids = jnp.arange(DOCS, dtype=jnp.int32)[:, None]
    below = jnp.sum((seg[None] < ids).astype(jnp.int32), axis=1, keepdims=True)
    upto = jnp.sum((seg[None] <= ids).astype(jnp.int32), axis=1, keepdims=True)
    mine = seg[None] == ids
    start = jnp.sum(jnp.where(mine, below, 0), axis=0)
    end = jnp.sum(jnp.where(mine, upto, 0), axis=0)
    return start, end


def tile_list(start, end, bq, bk, unroll):
    n, m = start.shape[0] // bq, start.shape[0] // bk
    low = start.reshape(n, bq)[:, 0] // bk
    high = (end.reshape(n, bq)[:, -1] + bk - 1) // bk
    count = high - low
    order = jnp.arange(n)
    upto = jnp.sum(jnp.where(order[:, None] <= order[None], count[:, None], 0), axis=0)
    total = upto[-1]
    t = jnp.arange(n * m + unroll, dtype=jnp.int32)
    mine = jnp.minimum(jnp.sum((t[:, None] >= upto[None]).astype(jnp.int32), axis=1), n - 1)
    base = jnp.sum(jnp.where(mine[:, None] == order[None], (high - upto)[None], 0), axis=1)
    real = t < total
    key = jnp.where(real, base + t, 0)
    pos = jnp.where(real, key * bk, FAR)
    steps = (total + unroll - 1) // unroll
    return jnp.concatenate([steps[None], mine, key, pos]).astype(jnp.int32)


def norm_stats(value):
    center = value - jnp.mean(value, axis=-1, keepdims=True)
    rstd = lax.rsqrt(jnp.mean(center * center, axis=-1, keepdims=True) + EPSILON)
    return center * rstd, rstd


def norm_back(xhat, rstd, d_out, gain):
    scaled = d_out * gain
    m1 = jnp.mean(scaled, axis=-1, keepdims=True)
    m2 = jnp.mean(scaled * xhat, axis=-1, keepdims=True)
    return (scaled - m1 - xhat * m2) * rstd


def column(value):
    return jnp.sum(value, axis=0, keepdims=True)


def merge_kernel(perm, cols, ctx, x, vec, *refs):
    ws = refs[:-3]
    mixed_ref, normed_ref, low_ref = refs[-3:]
    halves, deep, wide = ws[0].shape
    parts = []
    for r in range(len(ws)):
        rows = pl.ds(pl.multiple_of(perm[r] * deep, deep), deep)
        parts.append(ctx[rows, :].astype(F32).T.astype(BF16))
    for s in range(halves):
        acc = dot(parts[0], ws[0][s], 1, 0)
        for r in range(1, len(ws)):
            acc = acc + dot(parts[r], ws[r][s], 1, 0)
        sl = pl.ds(pl.multiple_of(cols[s] * wide, 128), wide)
        mixed_ref[:, sl] = x[:, sl] + acc + vec[2:3, sl]
    xhat, _ = norm_stats(mixed_ref[...])
    normed = xhat * vec[0:1, :] + vec[3:4, :]
    normed_ref[...] = normed
    low_ref[...] = normed.astype(BF16)


def merge_specs(ws, layer):
    shape = ws[0].shape
    spec = pl.BlockSpec((shape[0], None) + shape[2:], lambda *_: (0, layer, 0, 0))
    return [spec] * len(ws)


def merge_norm(ctx, ws, layer, x, vec, perm, cols):
    rows, width = x.shape
    big = jax.ShapeDtypeStruct((rows, width), F32)
    return pl.pallas_call(
        merge_kernel,
        grid_spec=pltpu.PrefetchScalarGridSpec(
            num_scalar_prefetch=2,
            grid=(1,),
            in_specs=[VMEM] * 3 + merge_specs(ws, layer),
            out_specs=[VMEM] * 3,
        ),
        out_shape=[big, big, jax.ShapeDtypeStruct((rows, width), BF16)],
        compiler_params=params(),
        cost_estimate=cost(2 * rows * width * width, 2 * width * width + 16 * rows * width),
        name="merge_norm",
    )(perm, cols, ctx, x, vec, *ws)


def add_up(refs):
    total = refs[0][...].astype(F32)
    for ref in refs[1:]:
        total = total + ref[...].astype(F32)
    return total


def norm_kernel(vec, *refs, n_in):
    summed_ref, out_ref, low_ref = refs[n_in:]
    summed = add_up(refs[:n_in]) + vec[4:5, :]
    summed_ref[...] = summed
    xhat, _ = norm_stats(summed)
    out = xhat * vec[1:2, :] + vec[5:6, :]
    out_ref[...] = out
    low_ref[...] = out.astype(BF16)


def second_norm(vec, terms):
    shape = terms[0].shape
    big = jax.ShapeDtypeStruct(shape, F32)
    return pl.pallas_call(
        functools.partial(norm_kernel, n_in=len(terms)),
        in_specs=[VMEM] * (1 + len(terms)),
        out_specs=[VMEM] * 3,
        out_shape=[big, big, jax.ShapeDtypeStruct(shape, BF16)],
        compiler_params=params(),
        cost_estimate=cost(20 * shape[0] * shape[1], 20 * shape[0] * shape[1]),
        name="second_norm",
    )(vec, *terms)


def second_back_math(vec, summed, d_out, d_ref, low_ref, sum_ref):
    xhat, rstd = norm_stats(summed)
    d_summed = norm_back(xhat, rstd, d_out, vec[1:2, :])
    d_ref[...] = d_summed
    low_ref[...] = d_summed.astype(BF16)
    sum_ref[0:1, :] = column(d_out * xhat)
    sum_ref[1:2, :] = column(d_out)
    sum_ref[2:3, :] = column(d_summed)
    return xhat


def last_kernel(vec, d_out_ref, *refs, n_in):
    out_ref, d_ref, low_ref, sum_ref = refs[n_in:]
    summed = add_up(refs[:n_in]) + vec[4:5, :]
    d_out = d_out_ref[...].astype(F32)
    xhat = second_back_math(vec, summed, d_out, d_ref, low_ref, sum_ref)
    out_ref[...] = (xhat * vec[1:2, :] + vec[5:6, :]).astype(BF16)


def last_norm(vec, d_out, terms):
    rows, width = terms[0].shape
    low = jax.ShapeDtypeStruct((rows, width), BF16)
    return pl.pallas_call(
        functools.partial(last_kernel, n_in=len(terms)),
        in_specs=[VMEM] * (2 + len(terms)),
        out_specs=[VMEM] * 4,
        out_shape=[
            low,
            jax.ShapeDtypeStruct((rows, width), F32),
            low,
            jax.ShapeDtypeStruct((3, width), F32),
        ],
        compiler_params=params(),
        cost_estimate=cost(40 * rows * width, 20 * rows * width),
        name="last_norm",
    )(vec, d_out, *terms)


def second_back_kernel(vec, summed_ref, *refs, n_in):
    d_ref, low_ref, sum_ref = refs[n_in:]
    second_back_math(vec, summed_ref[...], add_up(refs[:n_in]), d_ref, low_ref, sum_ref)


def second_back(vec, summed, terms):
    rows, width = summed.shape
    return pl.pallas_call(
        functools.partial(second_back_kernel, n_in=len(terms)),
        in_specs=[VMEM] * (2 + len(terms)),
        out_specs=[VMEM] * 3,
        out_shape=[
            jax.ShapeDtypeStruct((rows, width), F32),
            jax.ShapeDtypeStruct((rows, width), BF16),
            jax.ShapeDtypeStruct((3, width), F32),
        ],
        compiler_params=params(),
        cost_estimate=cost(40 * rows * width, 20 * rows * width),
        name="second_back",
    )(vec, summed, *terms)


def first_back_kernel(perm, cols, vec, mixed_ref, *refs, n_w, n_in):
    ws = refs[:n_w]
    d_ref, low_ref, sum_ref, ctx_ref = refs[n_w + n_in :]
    d_out = add_up(refs[n_w : n_w + n_in])
    xhat, rstd = norm_stats(mixed_ref[...])
    d_mixed = norm_back(xhat, rstd, d_out, vec[0:1, :])
    d_ref[...] = d_mixed
    low_ref[...] = d_mixed.astype(BF16)
    sum_ref[0:1, :] = column(d_out * xhat)
    sum_ref[1:2, :] = column(d_out)
    sum_ref[2:3, :] = column(d_mixed)
    halves, deep, wide = ws[0].shape
    parts = []
    for s in range(halves):
        parts.append(low_ref[:, pl.ds(pl.multiple_of(cols[s] * wide, 128), wide)])
    for r in range(n_w):
        acc = dot(ws[r][0], parts[0], 1, 1)
        for s in range(1, halves):
            acc = acc + dot(ws[r][s], parts[s], 1, 1)
        rows = pl.ds(pl.multiple_of(perm[r] * deep, deep), deep)
        ctx_ref[rows, :] = acc.astype(BF16)


def first_back(vec, mixed, ws, layer, terms, perm, cols):
    rows, width = mixed.shape
    return pl.pallas_call(
        functools.partial(first_back_kernel, n_w=len(ws), n_in=len(terms)),
        grid_spec=pltpu.PrefetchScalarGridSpec(
            num_scalar_prefetch=2,
            grid=(1,),
            in_specs=[VMEM] * 2 + merge_specs(ws, layer) + [VMEM] * len(terms),
            out_specs=[VMEM] * 4,
        ),
        out_shape=[
            jax.ShapeDtypeStruct((rows, width), F32),
            jax.ShapeDtypeStruct((rows, width), BF16),
            jax.ShapeDtypeStruct((3, width), F32),
            jax.ShapeDtypeStruct((width, rows), BF16),
        ],
        compiler_params=params(),
        cost_estimate=cost(2 * rows * width * width, 2 * width * width + 20 * rows * width),
        name="first_back",
    )(perm, cols, vec, mixed, *ws, *terms)


ERF_TOP = (
    -2.72614225801306e-10,
    2.77068142495902e-08,
    -2.10102402082508e-06,
    -5.69250639462346e-05,
    -7.34990630326855e-04,
    -2.95459980854025e-03,
    -1.60960333262415e-02,
)
ERF_BOTTOM = (
    -1.45660718464996e-05,
    -2.13374055278905e-04,
    -1.68282697438203e-03,
    -7.37332916720468e-03,
    -1.42647390514189e-02,
)


def erf(value):
    x = jnp.clip(value, -4.0, 4.0)
    sq = x * x
    top = jnp.full_like(x, ERF_TOP[0])
    for c in ERF_TOP[1:]:
        top = top * sq + c
    bottom = jnp.full_like(x, ERF_BOTTOM[0])
    for c in ERF_BOTTOM[1:]:
        bottom = bottom * sq + c
    return x * top / bottom


def up_kernel(*refs, n, fc):
    xs = refs[:n]
    up, bias, down = refs[n : n + 3]
    outs = refs[n + 3 : 2 * n + 3]
    cat_ref, act_ref, slope_ref = refs[2 * n + 3 :]
    r = pl.program_id(0)
    for i in range(n):

        @pl.when(r == i)
        def _():
            cat_ref[...] = xs[i][...]

    halves, deep, hidden = up.shape
    for f in range(0, hidden, fc):
        fs = slice(f, f + fc)
        u = dot(cat_ref[:, :deep], up[0, :, fs], 1, 0)
        for s in range(1, halves):
            u = u + dot(cat_ref[:, s * deep : (s + 1) * deep], up[s, :, fs], 1, 0)
        u = u + bias[:, fs].astype(F32)
        phi = 0.5 + 0.5 * erf(u * (0.5**0.5))
        act_ref[:, fs] = (u * phi).astype(BF16)
        slope = phi + u * (jnp.exp(-0.5 * u * u) * 0.3989422804014327)
        slope_ref[:, fs] = slope.astype(BF16)
    out = [dot(act_ref[...], down[s], 1, 0).astype(BF16) for s in range(halves)]
    for i in range(n):

        @pl.when(r == i)
        def _():
            for s in range(halves):
                outs[i][:, s * deep : (s + 1) * deep] = out[s]


def ff_specs(n, piece, width, hidden):
    whole = pl.BlockSpec((piece, width), lambda r: (0, 0))
    flat = pl.BlockSpec((piece, width), lambda r: (r, 0))
    tall = pl.BlockSpec((piece, hidden), lambda r: (r, 0))
    shapes = [jax.ShapeDtypeStruct((piece, width), BF16)] * n
    shapes += [jax.ShapeDtypeStruct((n * piece, w), BF16) for w in (width, hidden)]
    return whole, flat, tall, shapes


def feed_forward(xs, up, bias, down, fc):
    n = len(xs)
    piece, width = xs[0].shape
    hidden = up.shape[2]
    whole, flat, tall, shapes = ff_specs(n, piece, width, hidden)
    got = pl.pallas_call(
        functools.partial(up_kernel, n=n, fc=fc),
        grid=(n,),
        in_specs=[whole] * n
        + [
            pl.BlockSpec(up.shape, lambda r: (0, 0, 0)),
            pl.BlockSpec((1, hidden), lambda r: (0, 0)),
            pl.BlockSpec(down.shape, lambda r: (0, 0, 0)),
        ],
        out_specs=[whole] * n + [flat, tall, tall],
        out_shape=shapes + [shapes[-1]],
        compiler_params=params(),
        cost_estimate=cost(
            4 * n * piece * width * hidden, 12 * n * piece * width + 4 * width * hidden
        ),
        name="feed_forward",
    )(*xs, up, bias, down)
    return got[:n], got[n], got[n + 1], got[n + 2]


def down_kernel(*refs, n, fc):
    ds = refs[:n]
    slope_ref, up, down = refs[n : n + 3]
    outs = refs[n + 3 : 2 * n + 3]
    cat_ref, du_ref, sum_ref = refs[2 * n + 3 :]
    r = pl.program_id(0)
    for i in range(n):

        @pl.when(r == i)
        def _():
            cat_ref[...] = ds[i][...]

    halves, deep, hidden = up.shape

    @pl.when(r == 0)
    def _():
        sum_ref[...] = jnp.zeros_like(sum_ref)

    for f in range(0, hidden, fc):
        fs = slice(f, f + fc)
        d = dot(cat_ref[:, :deep], down[0, fs, :], 1, 1)
        for s in range(1, halves):
            d = d + dot(cat_ref[:, s * deep : (s + 1) * deep], down[s, fs, :], 1, 1)
        du = (d * slope_ref[:, fs].astype(F32)).astype(BF16)
        du_ref[:, fs] = du
        sum_ref[:, fs] += column(du.astype(F32))
    out = [dot(du_ref[...], up[s], 1, 1).astype(BF16) for s in range(halves)]
    for i in range(n):

        @pl.when(r == i)
        def _():
            for s in range(halves):
                outs[i][:, s * deep : (s + 1) * deep] = out[s]


def feed_back(ds, slope, up, down, fc):
    n = len(ds)
    piece, width = ds[0].shape
    hidden = up.shape[2]
    whole, flat, tall, shapes = ff_specs(n, piece, width, hidden)
    got = pl.pallas_call(
        functools.partial(down_kernel, n=n, fc=fc),
        grid=(n,),
        in_specs=[whole] * n
        + [
            tall,
            pl.BlockSpec(up.shape, lambda r: (0, 0, 0)),
            pl.BlockSpec(down.shape, lambda r: (0, 0, 0)),
        ],
        out_specs=[whole] * n + [flat, tall, pl.BlockSpec((1, hidden), lambda r: (0, 0))],
        out_shape=shapes + [jax.ShapeDtypeStruct((1, hidden), F32)],
        compiler_params=params(),
        cost_estimate=cost(
            4 * n * piece * width * hidden, 12 * n * piece * width + 4 * width * hidden
        ),
        name="feed_back",
    )(*ds, slope, up, down)
    return got[:n], got[n], got[n + 1], got[n + 2]


def place_kernel(perm, *refs):
    out = refs[-1]
    for i, ref in enumerate(refs[:-1]):

        @pl.when(pl.program_id(0) == i)
        def _():
            out[...] = ref[...].astype(out.dtype)


def place(blocks, perm, dtype):
    piece, width = blocks[0].shape
    n = len(blocks)
    return pl.pallas_call(
        place_kernel,
        grid_spec=pltpu.PrefetchScalarGridSpec(
            num_scalar_prefetch=1,
            grid=(n,),
            in_specs=[pl.BlockSpec((piece, width), lambda r, p: (0, 0))] * n,
            out_specs=pl.BlockSpec((piece, width), lambda r, p: (p[r], 0)),
        ),
        out_shape=jax.ShapeDtypeStruct((n * piece, width), dtype),
        compiler_params=params(),
        cost_estimate=cost(n * piece * width, 6 * n * piece * width),
        name="place",
    )(perm, *blocks)


def store_kernel(*refs):
    refs[-1][...] = refs[-2][...].astype(F32)


def store(buffer, joined, first, rows, width, layer, layers):
    chunk = joined.shape[1]
    block = math.gcd(math.gcd(rows, 256), first)
    ins = [
        pl.BlockSpec((block, chunk), lambda i, j: ((first + j * rows) // block + i, 0)),
    ]
    args = [joined]
    alias = {}
    if buffer is not None:
        ins = [pl.BlockSpec(memory_space=pl.ANY)] + ins
        args = [buffer] + args
        alias = {0: 0}
    return pl.pallas_call(
        store_kernel,
        grid=(rows // block, width // chunk),
        in_specs=ins,
        out_specs=pl.BlockSpec((None, block, chunk), lambda i, j: (layer, i, j)),
        out_shape=jax.ShapeDtypeStruct((layers, rows, width), F32),
        input_output_aliases=alias,
        compiler_params=params(32),
        cost_estimate=cost(rows * width, 6 * rows * width),
        name="store",
    )(*args)


def swap(value, axis, count, bit):
    return lax.ppermute(value, axis, [(i, i ^ bit) for i in range(count)])


def spread(own, count):
    one = swap(own, "tensor", count, 1)
    two = swap(own, "tensor", count, 2)
    return [own, one, two, swap(two, "tensor", count, 1)]


def collect(blocks, count):
    three = swap(blocks[3], "tensor", count, 1)
    far = (blocks[2].astype(F32) + three.astype(F32)).astype(BF16)
    two = swap(far, "tensor", count, 2)
    return [blocks[0], swap(blocks[1], "tensor", count, 1), two]


def ordered(parts, index, bits):
    for bit in bits:
        flip = (index & bit) != 0
        parts = [jnp.where(flip, parts[i ^ bit], parts[i]) for i in range(len(parts))]
    return parts


def sum_all(value, axis, count):
    bit = 1
    while bit < count:
        value = value + swap(value, axis, count, bit)
        bit *= 2
    return value


BQ, BK, UNROLL = 256, 512, 4
BQ_BACK, BK_BACK, UNROLL_BACK = 256, 256, 4


def build(n_shard, n_context, n_tensor):
    def shards(
        hidden_in,
        segment_ids,
        cotangent,
        qkv_weight,
        merge_weight,
        up_weight,
        down_weight,
        row_gains,
        row_bias,
        head_bias,
        up_bias,
    ):
        layers = qkv_weight.shape[0]
        rows, width = hidden_in.shape
        piece = rows // n_tensor
        deep = width // n_shard
        me_s = lax.axis_index(SHARD)
        me_t = lax.axis_index("tensor")
        order = jnp.arange(n_tensor, dtype=jnp.int32)
        relative = order ^ me_t.astype(jnp.int32)
        cols_all = jnp.arange(n_shard, dtype=jnp.int32)
        cols_rel = cols_all ^ me_s.astype(jnp.int32)

        w_in = jnp.transpose(qkv_weight, (0, 2, 1, 3))
        first = [w_in[0:1]]
        for bit in range(1, n_shard):
            first.append(swap(w_in[0:1], SHARD, n_shard, bit))
        segs = [segment_ids[0]]
        for bit in range(1, n_context):
            segs.append(swap(segment_ids[0], CONTEXT, n_context, bit))
        tables = jnp.concatenate([row_gains, row_bias], axis=1)
        w_in = [w_in[layer] for layer in range(layers)]
        up_weight = [up_weight[layer] for layer in range(layers)]
        down_weight = [down_weight[layer] for layer in range(layers)]
        first, segs, tables, merge_weight, up_weight, down_weight, w_in = (
            lax.optimization_barrier(
                (first, segs, tables, merge_weight, up_weight, down_weight, w_in)
            )
        )
        parts = [merge_weight]
        tabs = [tables]
        for bit in range(1, n_shard):
            parts.append(swap(merge_weight, SHARD, n_shard, bit))
            tabs.append(swap(tables, SHARD, n_shard, bit))
        bits = [1 << i for i in range(n_context.bit_length() - 1)]
        seg = jnp.concatenate(ordered(segs, lax.axis_index(CONTEXT), bits))
        doc = document_bounds(seg)
        tiles = tile_list(*doc, BQ, BK, UNROLL)
        tiles_back = tile_list(*doc, BQ_BACK, BK_BACK, UNROLL_BACK)
        w_qkv, cols = [first], [cols_rel]
        x_own = lax.dynamic_slice_in_dim(hidden_in, me_t * piece, piece, 0).astype(F32)
        d_last = lax.dynamic_slice_in_dim(cotangent, me_t * piece, piece, 0)
        xs = [hidden_in]
        x_nat = hidden_in
        saved = []
        for layer in range(layers):
            perm = order if layer == 0 else relative
            got = list(project(xs, w_qkv[layer], cols[layer], head_bias[layer], perm, piece))
            if layer == 0:
                got[0], parts, tabs, up_weight, down_weight, w_in = lax.optimization_barrier(
                    (got[0], parts, tabs, up_weight, down_weight, w_in)
                )
                pair = jnp.stack(parts)
                far = swap(pair, "tensor", n_tensor, 2)
                bits = [1 << i for i in range(n_shard.bit_length() - 1)]
                vec = jnp.concatenate(ordered(tabs, me_s, bits), axis=2).astype(F32)
                w_up, w_down = [], []
                for i in range(layers):
                    if i > 0:
                        w_qkv.append([lax.all_gather(w_in[i], SHARD, axis=0, tiled=False)])
                        cols.append(cols_all)
                    w_up.append(lax.all_gather(up_weight[i], SHARD, axis=0, tiled=False))
                    w_down.append(lax.all_gather(down_weight[i], SHARD, axis=0, tiled=False))
            else:
                x_nat = got[1]
            qkv = lax.all_to_all(got[0], CONTEXT, 0, 0, tiled=True)
            ctx_low, ctx, lse = attend(qkv, doc, tiles, piece, BQ, BK, UNROLL)
            if layer == 0:
                ctx_low, far, pair = lax.optimization_barrier((ctx_low, far, pair))
                w_merge = [pair, swap(pair, "tensor", n_tensor, 1)]
                w_merge += [far, swap(far, "tensor", n_tensor, 1)]
            mine = lax.all_to_all(ctx_low, ("tensor", CONTEXT), 0, 0, tiled=True)
            mine = mine.reshape(width, piece)
            mixed, normed, low = merge_norm(
                mine, w_merge, layer, x_own, vec[layer], relative, cols_rel
            )
            blocks, x1, act, slope = feed_forward(
                spread(low, n_tensor), w_up[layer], up_bias[layer : layer + 1], w_down[layer], 512
            )
            terms = [normed] + collect(blocks, n_tensor)
            keep = [x_nat, qkv, ctx, lse, mine, mixed, x1, act, slope]
            if layer + 1 < layers:
                summed, x_own, x_low = second_norm(vec[layer], terms)
                xs = spread(x_low, n_tensor)
                keep.append(summed)
            else:
                out_low, d_summed, d_low, sums = last_norm(vec[layer], d_last, terms)
            saved.append(keep)

        def send_parts(make):
            return [make(me_s ^ bit).astype(BF16) for bit in range(1, n_shard)]

        def exchange(parts):
            return [swap(p, SHARD, n_shard, i + 1) for i, p in enumerate(parts)]

        def settle(make, got):
            total = make(me_s)
            for part in got:
                total = total + part.astype(F32)
            return total.astype(BF16)

        def context_scatter(value):
            return lax.psum_scatter(value, CONTEXT, scatter_dimension=0, tiled=True)

        def context_gather(value):
            return lax.all_gather(value, CONTEXT, axis=0, tiled=True)

        def chunks(value, wide):
            return [value[:, i : i + wide] for i in range(0, value.shape[1], wide)]

        def join_wide(g_down, g_up):
            return jnp.concatenate([g_down] + chunks(g_up, g_down.shape[1]), axis=0)

        def join_narrow(g_qkv, g_merge):
            flat = g_qkv.reshape(-1, g_qkv.shape[2])
            wide = min(flat.shape[1], g_merge.shape[1])
            return jnp.concatenate(chunks(flat, wide) + chunks(g_merge, wide), axis=0)

        tie = lax.optimization_barrier
        grads = [None] * layers
        rowsums, sides = [None] * layers, [None] * layers
        terms = None
        hidden_out = None
        deep_t = width // n_tensor
        late, wide, narrow = (), (), ()
        for layer in reversed(range(layers)):
            last = layer + 1 == layers
            x_nat, qkv, ctx, lse, mine, mixed, x1, act, slope = saved[layer][:9]
            if not last:
                d_summed, d_low, sums = second_back(vec[layer], saved[layer][9], terms)
            blocks, wide = tie((spread(d_low, n_tensor), wide))
            if not last:
                wide = context_gather(wide)
            blocks, dy, du, g_hidden = feed_back(blocks, slope, w_up[layer], w_down[layer], 512)

            def down_part(i, act=act, dy=dy):
                return dot(act, lax.dynamic_slice_in_dim(dy, i * deep, deep, 1), 0, 0)

            def up_part(i, x1=x1, du=du):
                return dot(lax.dynamic_slice_in_dim(x1, i * deep, deep, 1), du, 0, 0)

            terms = [d_summed] + collect(blocks, n_tensor)
            down_send, up_send = send_parts(down_part), send_parts(up_part)
            terms, down_send, up_send, late, wide = tie((terms, down_send, up_send, late, wide))
            down_got, up_got = exchange(down_send), exchange(up_send)
            d_mixed, d_low, sums_one, d_mine = first_back(
                vec[layer], mixed, w_merge, layer, terms, relative, cols_rel
            )
            if not last:
                narrow = join_narrow(settle(makers[0], late[0]), settle(makers[1], late[1]))
                narrow = context_scatter(narrow)
            pieces = d_mine.reshape(n_tensor * n_context, HEAD_DIM, piece)
            d_ctx = lax.all_to_all(pieces, ("tensor", CONTEXT), 0, 0, tiled=True)
            g_blocks = []
            for r in range(n_tensor):
                part = lax.dynamic_slice_in_dim(mine, relative[r] * deep_t, deep_t, 0)
                g_blocks.append(dot(part, d_low, 1, 0).astype(BF16))
            d_ctx, g_blocks, narrow, down_got, out_low = tie(
                (d_ctx, g_blocks, narrow, down_got, out_low)
            )
            if last:
                out_low = [out_low, swap(out_low, "tensor", n_tensor, 2)]
            else:
                narrow = context_gather(narrow)
            d_heads = attend_back(
                qkv, doc, tiles_back, lse, ctx, d_ctx, piece, BQ_BACK, BK_BACK, UNROLL_BACK
            )
            d_heads, down_got, up_got, g_blocks, out_low, narrow = tie(
                (d_heads, down_got, up_got, g_blocks, out_low, narrow)
            )
            d_heads = lax.all_to_all(d_heads, CONTEXT, 0, 0, tiled=True)
            g_terms = collect(g_blocks, n_tensor)
            g_merge = sum(term.astype(F32) for term in g_terms).astype(BF16)
            new_wide = join_wide(settle(down_part, down_got), settle(up_part, up_got))
            if last:
                near = [swap(v, "tensor", n_tensor, 1) for v in out_low]
                out_low = [out_low[0], near[0], out_low[1], near[1]]
                hidden_out = place(out_low, relative, BF16)
            d_heads, new_wide, g_merge, narrow, hidden_out = tie(
                (d_heads, new_wide, g_merge, narrow, hidden_out)
            )
            new_wide = context_scatter(new_wide)
            got = project_back(d_heads, w_qkv[layer], cols[layer], relative, piece, width)
            d_x, d_proj, g_heads = got[:n_tensor], got[n_tensor], got[n_tensor + 1]

            def merge_part(i, g_merge=g_merge):
                return lax.dynamic_slice_in_dim(g_merge, i * deep, deep, 1).astype(F32)

            def qkv_part(i, x_nat=x_nat, d_proj=d_proj):
                d = lax.dynamic_slice_in_dim(x_nat, i * deep, deep, 1)
                return jnp.einsum("rd,crj->cdj", d, d_proj, preferred_element_type=F32)

            qkv_send, merge_send = send_parts(qkv_part), send_parts(merge_part)
            terms = [d_mixed] + collect(d_x, n_tensor)
            terms, qkv_send, merge_send = tie((terms, qkv_send, merge_send))
            if not last:
                grads[layer + 1] = (wide, narrow)
            late = (exchange(qkv_send), exchange(merge_send))
            makers = (qkv_part, merge_part)
            wide, narrow = new_wide, ()
            rowsums[layer] = jnp.concatenate([sums_one, sums], axis=0)
            sides[layer] = jnp.concatenate([g_heads.reshape(-1), g_hidden.reshape(-1)])
        total = terms[0]
        for term in terms[1:]:
            total = total + term.astype(F32)
        blocks, wide = tie((spread(total.astype(BF16), n_tensor), wide))
        narrow = join_narrow(settle(makers[0], late[0]), settle(makers[1], late[1]))
        wide, narrow = tie((wide, narrow))
        grads[0] = (context_gather(wide), context_gather(context_scatter(narrow)))
        input_grad = place(blocks, relative, F32)
        hw = width // n_tensor
        hidden = up_bias.shape[1]
        g_down = g_up = g_qkv = g_merge = None
        for layer in reversed(range(layers)):
            wide, narrow = grads[layer]
            g_down = store(g_down, wide, 0, hidden, deep, layer, layers)
            g_up = store(g_up, wide, hidden, deep, hidden, layer, layers)
            g_qkv = store(g_qkv, narrow, 0, 3 * deep, hw, layer, layers)
            g_merge = store(
                g_merge, narrow, narrow.shape[0] - hw * deep // narrow.shape[1], hw, deep, layer, layers
            )
        g_qkv = g_qkv.reshape(layers, 3, deep, -1)

        table = sum_all(jnp.concatenate(rowsums, axis=0), "tensor", n_tensor)
        side = jnp.concatenate(sides).reshape(-1, width)
        packed = jnp.concatenate([table, side], axis=0)
        packed = sum_all(packed, SHARD, n_shard)
        packed = sum_all(packed, CONTEXT, n_context)
        table = packed[: layers * 6].reshape(layers, 6, width)
        table = lax.dynamic_slice_in_dim(table, me_s * deep, deep, 2)
        side = packed[layers * 6 :].reshape(layers, -1)
        head_count = 2 * head_bias.shape[2]
        grad_gains = table[:, 0::3]
        grad_shifts = table[:, jnp.array([2, 1, 5, 4])]
        grad_heads = side[:, :head_count].reshape(head_bias.shape)
        grad_hidden = side[:, head_count:]
        return (
            hidden_out,
            input_grad,
            jnp.transpose(g_qkv, (0, 2, 1, 3)),
            g_merge,
            g_up,
            g_down,
            grad_gains,
            grad_shifts,
            grad_heads,
            grad_hidden,
        )

    return shards


def solution(mesh):
    tokens = (SHARD, CONTEXT)
    weights = (
        P(None, SHARD, None, "tensor"),
        P(None, "tensor", SHARD),
        P(None, SHARD, "tensor"),
        P(None, "tensor", SHARD),
        P(None, None, SHARD),
        P(None, None, SHARD),
        P(None, None, "tensor"),
        P(None, "tensor"),
    )
    return jax.shard_map(
        build(mesh.shape[SHARD], mesh.shape[CONTEXT], mesh.shape["tensor"]),
        mesh=mesh,
        in_specs=(P(tokens, None), P(*tokens), P(tokens, None)) + weights,
        out_specs=(P(tokens, None), P(tokens, None)) + weights,
        check_vma=False,
    )
```

time: 2260 us -> 881 us (0.39)
  waiting for transfers between devices: 1230 us -> 414 us
  matrix products: 547 us -> 48.7 us
  Pallas kernels: 0 us -> 240 us
  other arithmetic: 263 us -> 26.9 us
  blocking collectives: 101 us -> 19.1 us
  starting transfers between devices: 1.66 us -> 75.6 us
  local copies, waits for them, and re-layouts: 89.3 us -> 26.8 us
    psum x9 -> x0, waiting for transfers between devices: 516 us -> none  [the longest x1 185 us: context_total(): lax.psum(grads[0].astype(jnp.bfloat16), 'context').astype(jnp.float32)]
    dot_general x52 -> x20, matrix products: 547 us -> 48.7 us  [the longest x16 41.8 us: dot(): lax.dot_general(a, b, (((ca,), (cb,)), ((), ())), preferred_element_type=...]
    reduce_scatter x12 -> x4, waiting for transfers between devices: 387 us -> 25.2 us  [context_scatter(): return lax.psum_scatter(value, CONTEXT, scatter_dimension=0, tiled=True)]
    all_gather x10 -> x9, waiting for transfers between devices: 286 us -> 40.8 us  [the longest x4 40.8 us: context_gather(): return lax.all_gather(value, CONTEXT, axis=0, tiled=True)]
    pallas_call x0 -> x29, Pallas kernels: none -> 240 us  [the longest x2 54 us: attend_back(): pl.pallas_call(functools.partial(attend_back_kernel, bq=bq, bk=bk, seq=se...]
    ppermute x0 -> x67, waiting for transfers between devices: none -> 217 us  [swap(): return lax.ppermute(value, axis, [(i, i ^ bit) for i in range(count)])]
    all_to_all x0 -> x7, waiting for transfers between devices: none -> 128 us  [the longest x2 65.5 us: shards(): qkv = lax.all_to_all(got[0], CONTEXT, 0, 0, tiled=True)]
    reduce_sum x26 -> x8, other arithmetic: 115 us -> 0.87 us  [the longest x2 0.18 us: tile_list(): jnp.sum(jnp.where(mine[:, None] == order[None], (high - upto)[None], 0),...]
  transfers between devices with their start and end apart: 35 -> 87, of which waited for: 33 -> 43; matrix products, arithmetic and copies ran while one was open for 7% -> 10% of each run, Pallas kernels for 0% -> 21%
where the time goes in v1:
time: 881 us; the launch traced here: 871 us
  waiting for transfers between devices  414 us (47%)
  Pallas kernels  240 us (27%)
  starting transfers between devices  75.6 us (9%)
  matrix products  48.7 us (6%)
  other arithmetic  26.9 us (3%)
  local copies, waits for them, and re-layouts  26.8 us (3%)
  between operations  19.4 us (2%)
  blocking collectives  19.1 us (2%)
    ppermute x67, waiting for transfers between devices, swap(): return lax.ppermute(value, axis, [(i, i ^ bit) for i in range(count)])  217 us
    all_to_all x2, waiting for transfers between devices, shards(): qkv = lax.all_to_all(got[0], CONTEXT, 0, 0, tiled=True)  65.5 us
    pallas_call x2, Pallas kernels, attend_back(): pl.pallas_call(functools.partial(attend_back_kernel, bq=bq, bk=bk, seq=se...  54 us
    pallas_call x2, Pallas kernels, attend(): pl.pallas_call(functools.partial(attend_kernel, bq=bq, bk=bk, seq=seq, ch...  50.6 us
    ppermute x67, starting transfers between devices, swap(): return lax.ppermute(value, axis, [(i, i ^ bit) for i in range(count)])  44.8 us
    dot_general x16, matrix products, dot(): lax.dot_general(a, b, (((ca,), (cb,)), ((), ())), preferred_element_type=...  41.8 us
    all_gather x4, waiting for transfers between devices, context_gather(): return lax.all_gather(value, CONTEXT, axis=0, tiled=True)  40.8 us
    pallas_call x2, Pallas kernels, feed_forward(): pl.pallas_call(functools.partial(up_kernel, n=n, fc=fc), grid=(n,), in_sp...  30.3 us
  transfers between devices with their start and end apart: 87, of which 43 were waited for; matrix products, arithmetic and copies ran while one was open for 10% of the time, Pallas kernels for 21%

profile of v1, /device:TPU:0, one launch (start us, length us, event | category | flops | bytes accessed | tf_op | source)
XLA Modules:
  0.0 870.6 jit_solution(728280339021259243)
XLA Ops:
  55.8 29.0 %all-to-all-done.qkv = bf16[4,3,64,1024]{3,2,1,0:T(8,128)(2,1)} async-done(((bf16[4,3,64,1024]{3,2,1,0:T(8,128)(2,1)}), bf16[4,3,64,1024]{3,2,1,0:T(8,128)(2,1)}, u32[]{:S(2)}, u32[]{:S(2)}) %all-to-all-start) | async-done | bytes 1572896 | tf_op jit(solution)/shard_map/all_to_all | solution.py:963
  84.8 35.2 %attend.2 = (bf16[16,64,256]{2,1,0:T(8,128)(2,1)S(1)}, f32[16,64,256]{2,1,0:T(8,128)S(1)}, f32[1,4096]{1,0:T(1,128)S(1)}) custom-call(s32[397]{0:T(512)S(1)} %pad_add_fusion.2.tiles, bf16[4,3,64,1024]{3,2,1,0:T(8,128)(2,1)} %all-to-all-done.qkv, s32[1,4096]{1,0:T(1,128)S(1)} %bitcast.99, s32[1,4096]{1,0:T(1,128)S(1)} %sub.94.length), custom_call_target="tpu_custom_call" | custom-call | flops 1 | bytes 1 | tf_op jit(solution)/shard_map/attend/pallas_call | solution.py:271
  129.0 12.3 %all-to-all-done.1 = bf16[16,64,256]{2,1,0:T(8,128)(2,1)} async-done(((bf16[16,64,256]{2,1,0:T(8,128)(2,1)}), bf16[16,64,256]{2,1,0:T(8,128)(2,1)}, u32[]{:S(2)}, u32[]{:S(2)}) %all-to-all-start.1) | async-done | bytes 524320 | tf_op jit(solution)/shard_map/all_to_all | solution.py:969
  147.0 13.2 %collective-permute-done.10.refs_2_ = bf16[256,1024]{1,0:T(8,128)(2,1)} collective-permute-done((bf16[256,1024]{1,0:T(8,128)(2,1)}, bf16[256,1024]{1,0:T(8,128)(2,1)}, u32[]{:S(2)}, u32[]{:S(2)}) %collective-permute-start.10) | collective-permute-done | bytes 524320 | tf_op jit(solution)/shard_map/ppermute | solution.py:851
  162.5 15.2 %feed_forward.2 = (bf16[256,1024]{1,0:T(8,128)(2,1)}, bf16[256,1024]{1,0:T(8,128)(2,1)}, bf16[256,1024]{1,0:T(8,128)(2,1)}, bf16[256,1024]{1,0:T(8,128)(2,1)}, b...) custom-call(bf16[256,1024]{1,0:T(8,128)(2,1)} %get-tuple-element.217.refs_0_, ...), custom_call_target="tpu_custom_call" | custom-call | flops 1 | bytes 1 | tf_op jit(solution)/shard_map/feed_forward/pallas_call | solution.py:714
  183.1 13.0 %collective-permute-done.14.refs_3_ = bf16[256,1024]{1,0:T(8,128)(2,1)} collective-permute-done((bf16[256,1024]{1,0:T(8,128)(2,1)}, bf16[256,1024]{1,0:T(8,128)(2,1)}, u32[]{:S(2)}, u32[]{:S(2)}) %collective-permute-start.14) | collective-permute-done | bytes 524320 | tf_op jit(solution)/shard_map/ppermute | solution.py:851
  200.8 12.2 %collective-permute-done.16.refs_2_ = bf16[256,1024]{1,0:T(8,128)(2,1)} collective-permute-done((bf16[256,1024]{1,0:T(8,128)(2,1)}, bf16[256,1024]{1,0:T(8,128)(2,1)}, u32[]{:S(2)}, u32[]{:S(2)}) %collective-permute-start.16) | collective-permute-done | bytes 524320 | tf_op jit(solution)/shard_map/ppermute | solution.py:851
  227.9 36.4 %all-to-all-done.2.qkv = bf16[4,3,64,1024]{3,2,1,0:T(8,128)(2,1)} async-done(((bf16[4,3,64,1024]{3,2,1,0:T(8,128)(2,1)}), bf16[4,3,64,1024]{3,2,1,0:T(8,128)(2,1)}, u32[]{:S(2)}, u32[]{:S(2)}) %all-to-all-start.2) | async-done | bytes 1572896 | tf_op jit(solution)/shard_map/all_to_all | solution.py:963
  264.3 15.4 %attend.3 = (bf16[16,64,256]{2,1,0:T(8,128)(2,1)S(1)}, f32[16,64,256]{2,1,0:T(8,128)S(1)}, f32[1,4096]{1,0:T(1,128)S(1)}) custom-call(s32[397]{0:T(512)S(1)} %pad_add_fusion.2.tiles, bf16[4,3,64,1024]{3,2,1,0:T(8,128)(2,1)} %all-to-all-done.2.qkv, s32[1,4096]{1,0:T(1,128)S(1)} %bitcast.100, s32[1,4096]{1,0:T(1,128)S(1)} %sub.94.length), custom_call_target="tpu_custom_call" | custom-call | flops 1 | bytes 1 | tf_op jit(solution)/shard_map/attend/pallas_call | solution.py:271
  280.8 19.1 %all_to_all.40 = bf16[16,64,256]{2,1,0:T(8,128)(2,1)} all-to-all(bf16[16,64,256]{2,1,0:T(8,128)(2,1)S(1)} %get-tuple-element.228), channel_id=1, replica_groups=mesh['shard'=2,'context'=4,'tensor'=4] {'tensor','context'}, dimensions={0} | all-to-all | bytes 1048576 | tf_op jit(solution)/shard_map/all_to_all | solution.py:969
  305.4 13.3 %collective-permute-done.19.refs_2_ = bf16[256,1024]{1,0:T(8,128)(2,1)} collective-permute-done((bf16[256,1024]{1,0:T(8,128)(2,1)}, bf16[256,1024]{1,0:T(8,128)(2,1)}, u32[]{:S(2)}, u32[]{:S(2)}) %collective-permute-start.19) | collective-permute-done | bytes 524320 | tf_op jit(solution)/shard_map/ppermute | solution.py:851
  320.9 15.2 %feed_forward.3 = (bf16[256,1024]{1,0:T(8,128)(2,1)}, bf16[256,1024]{1,0:T(8,128)(2,1)}, bf16[256,1024]{1,0:T(8,128)(2,1)}, bf16[256,1024]{1,0:T(8,128)(2,1)}, b...) custom-call(bf16[256,1024]{1,0:T(8,128)(2,1)} %get-tuple-element.232.refs_0_, ...), custom_call_target="tpu_custom_call" | custom-call | flops 1 | bytes 1 | tf_op jit(solution)/shard_map/feed_forward/pallas_call | solution.py:714
  359.6 12.2 %collective-permute-done.25.refs_2_ = bf16[256,1024]{1,0:T(8,128)(2,1)S(1)} collective-permute-done((bf16[256,1024]{1,0:T(8,128)(2,1)}, bf16[256,1024]{1,0:T(8,128)(2,1)S(1)}, u32[]{:S(2)}, u32[]{:S(2)}) %collective-permute-start.25) | collective-permute-done | bytes 524320 | tf_op jit(solution)/shard_map/ppermute | solution.py:851
  434.2 27.0 %attend_back.2 = bf16[4,3,64,1024]{3,2,1,0:T(8,128)(2,1)} custom-call(s32[781]{0:T(1024)S(1)} %pad_add_fusion.1.tiles, bf16[4,3,64,1024]{3,2,1,0:T(8,128)(2,1)} %all-to-all-done.2.qkv, s32[1,4096]{1,0:T(1,128)S(1)} %bitcast.101, s32[1,4096]{1,0:T(1,128)S(1)} %sub.94.length, f32[1,4096]{1,0:T(1,128)S(1)} %get-tuple-element.259.lse, ...), custom_call_target="tpu_custom_call" | custom-call | flops 1 | bytes 1 | tf_op jit(solution)/shard_map/attend_back/pallas_call | solution.py:382
  488.4 14.0 %all-to-all-done.5.refs_0_ = bf16[4,3,64,1024]{3,2,1,0:T(8,128)(2,1)} async-done(((bf16[4,3,64,1024]{3,2,1,0:T(8,128)(2,1)}), bf16[4,3,64,1024]{3,2,1,0:T(8,128)(2,1)}, u32[]{:S(2)}, u32[]{:S(2)}) %all-to-all-start.5) | async-done | bytes 1572896 | tf_op jit(solution)/shard_map/all_to_all | solution.py:1068
  533.9 12.5 %collective-permute-done.42.refs_2_ = bf16[256,1024]{1,0:T(8,128)(2,1)S(1)} collective-permute-done((bf16[256,1024]{1,0:T(8,128)(2,1)}, bf16[256,1024]{1,0:T(8,128)(2,1)S(1)}, u32[]{:S(2)}, u32[]{:S(2)}) %collective-permute-start.42) | collective-permute-done | bytes 524320 | tf_op jit(solution)/shard_map/ppermute | solution.py:851
  570.6 14.8 %collective-permute-done.48 = bf16[256,512]{1,0:T(8,128)(2,1)S(1)} collective-permute-done((bf16[256,512]{1,0:T(8,128)(2,1)S(1)}, bf16[256,512]{1,0:T(8,128)(2,1)S(1)}, u32[]{:S(2)}, u32[]{:S(2)}) %collective-permute-start.48) | collective-permute-done | bytes 262176 | tf_op jit(solution)/shard_map/ppermute | solution.py:851
  617.0 16.7 %all-to-all-done.6.d_ctx = bf16[16,64,256]{2,1,0:T(8,128)(2,1)S(1)} async-done(((bf16[16,64,256]{2,1,0:T(8,128)(2,1)}), bf16[16,64,256]{2,1,0:T(8,128)(2,1)S(1)}, u32[]{:S(2)}, u32[]{:S(2)}) %all-to-all-start.6) | async-done | bytes 524320 | tf_op jit(solution)/shard_map/all_to_all | solution.py:1050
  635.3 27.0 %attend_back.3 = bf16[4,3,64,1024]{3,2,1,0:T(8,128)(2,1)} custom-call(s32[781]{0:T(1024)S(1)} %pad_add_fusion.1.tiles, bf16[4,3,64,1024]{3,2,1,0:T(8,128)(2,1)} %all-to-all-done.qkv, s32[1,4096]{1,0:T(1,128)S(1)} %bitcast.102, s32[1,4096]{1,0:T(1,128)S(1)} %sub.94.length, f32[1,4096]{1,0:T(1,128)S(1)} %get-tuple-element.205.lse, ...), custom_call_target="tpu_custom_call" | custom-call | flops 1 | bytes 1 | tf_op jit(solution)/shard_map/attend_back/pallas_call | solution.py:382
  689.3 13.6 %all-to-all-done.7.refs_0_ = bf16[4,3,64,1024]{3,2,1,0:T(8,128)(2,1)} async-done(((bf16[4,3,64,1024]{3,2,1,0:T(8,128)(2,1)}), bf16[4,3,64,1024]{3,2,1,0:T(8,128)(2,1)}, u32[]{:S(2)}, u32[]{:S(2)}) %all-to-all-start.7) | async-done | bytes 1572896 | tf_op jit(solution)/shard_map/all_to_all | solution.py:1068
  733.5 19.2 %collective-permute-done.61 = bf16[256,512]{1,0:T(8,128)(2,1)S(1)} collective-permute-done((bf16[256,512]{1,0:T(8,128)(2,1)S(1)}, bf16[256,512]{1,0:T(8,128)(2,1)S(1)}, u32[]{:S(2)}, u32[]{:S(2)}) %collective-permute-start.61) | collective-permute-done | bytes 262176 | tf_op jit(solution)/shard_map/ppermute | solution.py:851
  756.8 25.2 %reduce-scatter.11.cloned.1.call-done = bf16[512,256]{1,0:T(8,128)(2,1)} async-done(((bf16[2048,256]{1,0:T(8,128)(2,1)}), bf16[512,256]{1,0:T(8,128)(2,1)}) %reduce-scatter.11.cloned.1.call-update) | async-done | bytes 262160 | tf_op jit(solution)/shard_map/reduce_scatter | solution.py:1000
  818.8 12.1 %all-gather.21.cloned.1.call-done.refs_1_ = bf16[2048,512]{1,0:T(8,128)(2,1)} async-done(((bf16[512,512]{1,0:T(8,128)(2,1)}), bf16[2048,512]{1,0:T(8,128)(2,1)}) %all-gather.21.cloned.1.call-update) | async-done | bytes 2097168 | tf_op jit(solution)/shard_map/all_gather | solution.py:1003
  836.2 23.2 %all-gather.19.cloned.1.call-done.refs_1_ = bf16[2048,256]{1,0:T(8,128)(2,1)} async-done(((bf16[512,256]{1,0:T(8,128)(2,1)}), bf16[2048,256]{1,0:T(8,128)(2,1)}) %all-gather.19.cloned.1.call-update) | async-done | bytes 1048592 | tf_op jit(solution)/shard_map/all_gather | solution.py:1003
  (447 shorter events, 404.2 us)
Async XLA Ops:
  44.6 40.2 %all-to-all-start = ((bf16[4,3,64,1024]{3,2,1,0:T(8,128)(2,1)}), bf16[4,3,64,1024]{3,2,1,0:T(8,128)(2,1)}, u32[]{:S(2)}, u32[]{:S(2)}) async-start(bf16[4,3,64,1024]{3,2,1,0:T(8,128)(2,1)} %project.2), calls=%async_computation | async-start | bytes 3145728 | tf_op jit(solution)/shard_map/all_to_all | solution.py:963
  49.4 111.5 %all-gather.23.cloned.1.call-start = ((), (), s32[]{:S(2)}) async-start(), calls=%async_computation.20 | async-start | bytes 3145728 | tf_op jit(solution)/shard_map/all_gather | solution.py:959
  50.1 110.7 %all-gather.25.cloned.1.call-start = ((), (), s32[]{:S(2)}) async-start(), calls=%async_computation.21 | async-start | bytes 3145728 | tf_op jit(solution)/shard_map/all_gather | solution.py:960
  52.0 68.9 %collective-permute-start.6 = (bf16[2,2,256,512]{3,2,1,0:T(8,128)(2,1)}, bf16[2,2,256,512]{3,2,1,0:T(8,128)(2,1)}, u32[]{:S(2)}, u32[]{:S(2)}) collective-permute-start(bf16[2,2,256,512]{3,2,1,0:T(8,128)(2,1)} %pad_maximum_fusion.2.refs_0_), channel_id=1, source_target_pairs={{0,2},{1,3},{2,0},{3,1},{4,6},{5,7},{6,4},{7,5},{8,10},{9,11},{10,... | collective-permute-start | bytes 3145736 | tf_op jit(solution)/shard_map/ppermute | solution.py:851
  125.6 87.4 %all-gather.27.cloned.1.call-start = ((), (), s32[]{:S(2)}) async-start(), calls=%async_computation.22 | async-start | bytes 2359296 | tf_op jit(solution)/shard_map/all_gather | solution.py:957
  222.3 41.9 %all-to-all-start.2 = ((bf16[4,3,64,1024]{3,2,1,0:T(8,128)(2,1)}), bf16[4,3,64,1024]{3,2,1,0:T(8,128)(2,1)}, u32[]{:S(2)}, u32[]{:S(2)}) async-start(bf16[4,3,64,1024]{3,2,1,0:T(8,128)(2,1)} %get-tuple-element.227), calls=%async_computation.2 | async-start | bytes 3145728 | tf_op jit(solution)/shard_map/all_to_all | solution.py:963
  226.7 91.9 %all-gather.29.cloned.1.call-start = ((), (), s32[]{:S(2)}) async-start(), calls=%async_computation.23 | async-start | bytes 3145728 | tf_op jit(solution)/shard_map/all_gather | solution.py:959
  227.3 91.4 %all-gather.31.cloned.1.call-start = ((), (), s32[]{:S(2)}) async-start(), calls=%async_computation.24 | async-start | bytes 3145728 | tf_op jit(solution)/shard_map/all_gather | solution.py:960
  404.6 26.4 %collective-permute-start.30 = (bf16[1024,512]{1,0:T(8,128)(2,1)}, bf16[1024,512]{1,0:T(8,128)(2,1)}, u32[]{:S(2)}, u32[]{:S(2)}) collective-permute-start(bf16[1024,512]{1,0:T(8,128)(2,1)} %convolution_convert_fusion.3), channel_id=1, source_target_pairs={{0,16},{16,0},{1,17},{17,1},{2,18},{18,2},{3,19},{19,3},{4,20},{20... | collective-permute-start | bytes 3145736 | tf_op jit(solution)/shard_map/ppermute | solution.py:851
  415.1 46.1 %collective-permute-start.31 = (bf16[512,1024]{1,0:T(8,128)(2,1)}, bf16[512,1024]{1,0:T(8,128)(2,1)}, u32[]{:S(2)}, u32[]{:S(2)}) collective-permute-start(bf16[512,1024]{1,0:T(8,128)(2,1)} %convolution_convert_fusion.2), channel_id=1, source_target_pairs={{0,16},{16,0},{1,17},{17,1},{2,18},{18,2},{3,19},{19,3},{4,20},{20... | collective-permute-start | bytes 3145736 | tf_op jit(solution)/shard_map/ppermute | solution.py:851
  431.0 30.3 %collective-permute-start.32 = (bf16[256,1024]{1,0:T(8,128)(2,1)}, bf16[256,1024]{1,0:T(8,128)(2,1)S(1)}, u32[]{:S(2)}, u32[]{:S(2)}) collective-permute-start(bf16[256,1024]{1,0:T(8,128)(2,1)} %get-tuple-element.280.refs_0_), channel_id=1, source_target_pairs={{0,2},{1,3},{2,0},{3,1},{4,6},{5,7},{6,4},{7,5},{8,10},{9,11},{10,... | collective-permute-start | bytes 1572872 | tf_op jit(solution)/shard_map/ppermute | solution.py:851
  461.2 41.1 %all-to-all-start.5 = ((bf16[4,3,64,1024]{3,2,1,0:T(8,128)(2,1)}), bf16[4,3,64,1024]{3,2,1,0:T(8,128)(2,1)}, u32[]{:S(2)}, u32[]{:S(2)}) async-start(bf16[4,3,64,1024]{3,2,1,0:T(8,128)(2,1)} %attend_back.2), calls=%async_computation.5 | async-start | bytes 3145728 | tf_op jit(solution)/shard_map/all_to_all | solution.py:1068
  465.6 82.7 %reduce-scatter.5.cloned.1.call-start = ((), (), s32[]{:S(2)}) async-start(), calls=%async_computation.12 | async-start | bytes 2621440 | tf_op jit(solution)/shard_map/reduce_scatter | solution.py:1000
  502.4 90.2 %all-gather.15.cloned.1.call-start = ((), (), s32[]{:S(2)}) async-start(), calls=%async_computation.13 | async-start | bytes 2621440 | tf_op jit(solution)/shard_map/all_gather | solution.py:1003
  548.3 85.4 %reduce-scatter.7.cloned.1.call-start = ((), (), s32[]{:S(2)}) async-start(), calls=%async_computation.14 | async-start | bytes 1310720 | tf_op jit(solution)/shard_map/reduce_scatter | solution.py:1000
  597.6 36.2 %collective-permute-start.49 = (bf16[1024,512]{1,0:T(8,128)(2,1)S(1)}, bf16[1024,512]{1,0:T(8,128)(2,1)}, u32[]{:S(2)}, u32[]{:S(2)}) collective-permute-start(bf16[1024,512]{1,0:T(8,128)(2,1)S(1)} %copy-done.68), channel_id=1, source_target_pairs={{0,16},{16,0},{1,17},{17,1},{2,18},{18,2},{3,19},{19,3},{4,20},{20... | collective-permute-start | bytes 3145736 | tf_op jit(solution)/shard_map/ppermute | solution.py:851
  605.0 28.8 %all-to-all-start.6 = ((bf16[16,64,256]{2,1,0:T(8,128)(2,1)}), bf16[16,64,256]{2,1,0:T(8,128)(2,1)S(1)}, u32[]{:S(2)}, u32[]{:S(2)}) async-start(bf16[16,64,256]{2,1,0:T(8,128)(2,1)} %bitcast.122), calls=%async_computation.7 | async-start | bytes 1048576 | tf_op jit(solution)/shard_map/all_to_all | solution.py:1050
  608.7 53.6 %all-gather.17.cloned.1.call-start = ((), (), s32[]{:S(2)}) async-start(), calls=%async_computation.15 | async-start | bytes 1310720 | tf_op jit(solution)/shard_map/all_gather | solution.py:1003
  633.8 28.5 %collective-permute-start.50 = (bf16[512,1024]{1,0:T(8,128)(2,1)}, bf16[512,1024]{1,0:T(8,128)(2,1)}, u32[]{:S(2)}, u32[]{:S(2)}) collective-permute-start(bf16[512,1024]{1,0:T(8,128)(2,1)} %convolution_convert_fusion), channel_id=1, source_target_pairs={{0,16},{16,0},{1,17},{17,1},{2,18},{18,2},{3,19},{19,3},{4,20},{20... | collective-permute-start | bytes 3145736 | tf_op jit(solution)/shard_map/ppermute | solution.py:851
  662.3 40.7 %all-to-all-start.7 = ((bf16[4,3,64,1024]{3,2,1,0:T(8,128)(2,1)}), bf16[4,3,64,1024]{3,2,1,0:T(8,128)(2,1)}, u32[]{:S(2)}, u32[]{:S(2)}) async-start(bf16[4,3,64,1024]{3,2,1,0:T(8,128)(2,1)} %attend_back.3), calls=%async_computation.9 | async-start | bytes 3145728 | tf_op jit(solution)/shard_map/all_to_all | solution.py:1068
  666.8 89.4 %reduce-scatter.9.cloned.1.call-start = ((), (), s32[]{:S(2)}) async-start(), calls=%async_computation.16 | async-start | bytes 2621440 | tf_op jit(solution)/shard_map/reduce_scatter | solution.py:1000
  703.0 79.0 %reduce-scatter.11.cloned.1.call-start = ((), (), s32[]{:S(2)}) async-start(), calls=%async_computation.17 | async-start | bytes 1310720 | tf_op jit(solution)/shard_map/reduce_scatter | solution.py:1000
  756.2 74.7 %all-gather.21.cloned.1.call-start = ((), (), s32[]{:S(2)}) async-start(), calls=%async_computation.19 | async-start | bytes 2621440 | tf_op jit(solution)/shard_map/all_gather | solution.py:1003
  756.8 102.6 %all-gather.19.cloned.1.call-start = ((), (), s32[]{:S(2)}) async-start(), calls=%async_computation.18 | async-start | bytes 1310720 | tf_op jit(solution)/shard_map/all_gather | solution.py:1003
  (134 other events, 1695.1 us)
Sparse Core Ops, SparseCore 0:
  52.3 34.5 all-gather.22
  121.5 31.9 all-gather.24
  183.2 25.0 all-gather.26
  228.8 33.6 all-gather.28
  263.8 33.1 all-gather.30
  502.5 41.8 reduce-scatter.4
  548.4 44.0 all-gather.14
  597.1 34.0 reduce-scatter.6
  633.9 26.6 all-gather.16
  703.1 42.2 reduce-scatter.8
  756.3 25.6 reduce-scatter.10
  783.4 47.4 all-gather.20
  832.5 26.8 all-gather.18

commit v2 on v1

--- a/solution.py
+++ b/solution.py
@@ -36,10 +36,10 @@
 def qkv_kernel(perm, cols, *refs, n_x, n_w):
     xs, bias_ref = refs[:n_x], refs[n_x]
     w_refs = refs[n_x + 1 : n_x + 1 + n_w]
-    out_ref = refs[n_x + 1 + n_w]
+    out_ref = refs[-1]
     x_ref = xs[0]
     if n_x > 1:
-        x_ref = refs[n_x + 2 + n_w]
+        out_ref, x_ref = refs[-2:]
         for i in range(n_x):
 
             @pl.when(pl.program_id(0) == i)
@@ -67,33 +67,40 @@
             out_ref[h, c] = turned[h * HEAD_DIM : (h + 1) * HEAD_DIM]
 
 
-def project(xs, weights, cols, bias, perm, piece):
+def project(xs, weights, cols, bias, perm, piece, base, rows, kept):
     width = xs[0].shape[1]
-    rows = sum(x.shape[0] for x in xs)
+    count = sum(x.shape[0] for x in xs) // piece
     hw = weights[0].shape[-1]
     heads = hw // HEAD_DIM
     out_shape = [jax.ShapeDtypeStruct((heads, 3, HEAD_DIM, rows), BF16)]
-    out_specs = [pl.BlockSpec((heads, 3, HEAD_DIM, piece), lambda r, p, c: (0, 0, 0, p[r]))]
+    out_specs = [
+        pl.BlockSpec((heads, 3, HEAD_DIM, piece), lambda r, p, c: (0, 0, 0, p[r + base]))
+    ]
     x_specs = [pl.BlockSpec((piece, width), lambda r, p, c: (r, 0))]
     if len(xs) > 1:
         x_specs = [pl.BlockSpec((piece, width), lambda r, p, c: (0, 0))] * len(xs)
         out_shape.append(jax.ShapeDtypeStruct((rows, width), BF16))
-        out_specs.append(pl.BlockSpec((piece, width), lambda r, p, c: (p[r], 0)))
+        out_specs.append(pl.BlockSpec((piece, width), lambda r, p, c: (p[r + base], 0)))
+    first = 3 + len(xs) + len(weights)
     return pl.pallas_call(
         functools.partial(qkv_kernel, n_x=len(xs), n_w=len(weights)),
         grid_spec=pltpu.PrefetchScalarGridSpec(
             num_scalar_prefetch=2,
-            grid=(rows // piece,),
+            grid=(count,),
             in_specs=x_specs
             + [pl.BlockSpec(bias.shape, lambda r, p, c: (0, 0))]
-            + [pl.BlockSpec(w.shape, lambda r, p, c: (0, 0, 0, 0)) for w in weights],
+            + [pl.BlockSpec(w.shape, lambda r, p, c: (0, 0, 0, 0)) for w in weights]
+            + [pl.BlockSpec(memory_space=pl.ANY)] * len(kept),
             out_specs=out_specs,
         ),
         out_shape=out_shape,
+        input_output_aliases={first + i: i for i in range(len(kept))},
         compiler_params=params(),
-        cost_estimate=cost(2 * rows * width * 3 * hw, 2 * rows * width * 2 + 6 * width * hw),
+        cost_estimate=pl.CostEstimate(
+            flops=8 * count * piece * width * 3 * hw, bytes_accessed=1, transcendentals=0
+        ),
         name="project",
-    )(perm, cols, *xs, bias, *weights)
+    )(perm, cols, *xs, bias, *weights, *kept)
 
 
 def back_kernel(perm, cols, *refs, n_w):
@@ -506,6 +513,15 @@
     return total
 
 
+def row_blocks(count, rows, width):
+    block = rows
+    return (rows // block,), [pl.BlockSpec((block, width), lambda r: (r, 0))] * count
+
+
+def all_of(shape):
+    return pl.BlockSpec(shape, lambda r: (0, 0))
+
+
 def norm_kernel(vec, *refs, n_in):
     summed_ref, out_ref, low_ref = refs[n_in:]
     summed = add_up(refs[:n_in]) + vec[4:5, :]
@@ -519,10 +535,12 @@
 def second_norm(vec, terms):
     shape = terms[0].shape
     big = jax.ShapeDtypeStruct(shape, F32)
+    grid, specs = row_blocks(len(terms) + 3, *shape)
     return pl.pallas_call(
         functools.partial(norm_kernel, n_in=len(terms)),
-        in_specs=[VMEM] * (1 + len(terms)),
-        out_specs=[VMEM] * 3,
+        grid=grid,
+        in_specs=[all_of(vec.shape)] + specs[3:],
+        out_specs=specs[:3],
         out_shape=[big, big, jax.ShapeDtypeStruct(shape, BF16)],
         compiler_params=params(),
         cost_estimate=cost(20 * shape[0] * shape[1], 20 * shape[0] * shape[1]),
@@ -535,9 +553,14 @@
     d_summed = norm_back(xhat, rstd, d_out, vec[1:2, :])
     d_ref[...] = d_summed
     low_ref[...] = d_summed.astype(BF16)
-    sum_ref[0:1, :] = column(d_out * xhat)
-    sum_ref[1:2, :] = column(d_out)
-    sum_ref[2:3, :] = column(d_summed)
+
+    @pl.when(pl.program_id(0) == 0)
+    def _():
+        sum_ref[...] = jnp.zeros_like(sum_ref)
+
+    sum_ref[0:1, :] += column(d_out * xhat)
+    sum_ref[1:2, :] += column(d_out)
+    sum_ref[2:3, :] += column(d_summed)
     return xhat
 
 
@@ -552,10 +575,12 @@
 def last_norm(vec, d_out, terms):
     rows, width = terms[0].shape
     low = jax.ShapeDtypeStruct((rows, width), BF16)
+    grid, specs = row_blocks(len(terms) + 4, rows, width)
     return pl.pallas_call(
         functools.partial(last_kernel, n_in=len(terms)),
-        in_specs=[VMEM] * (2 + len(terms)),
-        out_specs=[VMEM] * 4,
+        grid=grid,
+        in_specs=[all_of(vec.shape)] + specs[3:],
+        out_specs=specs[:3] + [all_of((3, width))],
         out_shape=[
             low,
             jax.ShapeDtypeStruct((rows, width), F32),
@@ -575,10 +600,12 @@
 
 def second_back(vec, summed, terms):
     rows, width = summed.shape
+    grid, specs = row_blocks(len(terms) + 3, rows, width)
     return pl.pallas_call(
         functools.partial(second_back_kernel, n_in=len(terms)),
-        in_specs=[VMEM] * (2 + len(terms)),
-        out_specs=[VMEM] * 3,
+        grid=grid,
+        in_specs=[all_of(vec.shape)] + specs[2:],
+        out_specs=specs[:2] + [all_of((3, width))],
         out_shape=[
             jax.ShapeDtypeStruct((rows, width), F32),
             jax.ShapeDtypeStruct((rows, width), BF16),
@@ -668,8 +695,8 @@
 def up_kernel(*refs, n, fc):
     xs = refs[:n]
     up, bias, down = refs[n : n + 3]
-    outs = refs[n + 3 : 2 * n + 3]
-    cat_ref, act_ref, slope_ref = refs[2 * n + 3 :]
+    outs = refs[-3 - n : -3]
+    cat_ref, act_ref, slope_ref = refs[-3:]
     r = pl.program_id(0)
     for i in range(n):
 
@@ -697,20 +724,18 @@
                 outs[i][:, s * deep : (s + 1) * deep] = out[s]
 
 
-def ff_specs(n, piece, width, hidden):
+def ff_specs(n, piece, width, hidden, base):
     whole = pl.BlockSpec((piece, width), lambda r: (0, 0))
-    flat = pl.BlockSpec((piece, width), lambda r: (r, 0))
-    tall = pl.BlockSpec((piece, hidden), lambda r: (r, 0))
-    shapes = [jax.ShapeDtypeStruct((piece, width), BF16)] * n
-    shapes += [jax.ShapeDtypeStruct((n * piece, w), BF16) for w in (width, hidden)]
-    return whole, flat, tall, shapes
-
-
-def feed_forward(xs, up, bias, down, fc):
+    flat = pl.BlockSpec((piece, width), lambda r: (r + base, 0))
+    tall = pl.BlockSpec((piece, hidden), lambda r: (r + base, 0))
+    return whole, flat, tall
+
+
+def feed_forward(xs, up, bias, down, fc, base, rows, kept):
     n = len(xs)
     piece, width = xs[0].shape
     hidden = up.shape[2]
-    whole, flat, tall, shapes = ff_specs(n, piece, width, hidden)
+    whole, flat, tall = ff_specs(n, piece, width, hidden, base)
     got = pl.pallas_call(
         functools.partial(up_kernel, n=n, fc=fc),
         grid=(n,),
@@ -719,23 +744,26 @@
             pl.BlockSpec(up.shape, lambda r: (0, 0, 0)),
             pl.BlockSpec((1, hidden), lambda r: (0, 0)),
             pl.BlockSpec(down.shape, lambda r: (0, 0, 0)),
-        ],
+        ]
+        + [pl.BlockSpec(memory_space=pl.ANY)] * len(kept),
         out_specs=[whole] * n + [flat, tall, tall],
-        out_shape=shapes + [shapes[-1]],
+        out_shape=[jax.ShapeDtypeStruct((piece, width), BF16)] * n
+        + [jax.ShapeDtypeStruct((rows, w), BF16) for w in (width, hidden, hidden)],
+        input_output_aliases={n + 3 + i: n + i for i in range(len(kept))},
         compiler_params=params(),
-        cost_estimate=cost(
-            4 * n * piece * width * hidden, 12 * n * piece * width + 4 * width * hidden
+        cost_estimate=pl.CostEstimate(
+            flops=16 * n * piece * width * hidden, bytes_accessed=1, transcendentals=0
         ),
         name="feed_forward",
-    )(*xs, up, bias, down)
-    return got[:n], got[n], got[n + 1], got[n + 2]
+    )(*xs, up, bias, down, *kept)
+    return list(got[:n]), list(got[n:])
 
 
 def down_kernel(*refs, n, fc):
     ds = refs[:n]
     slope_ref, up, down = refs[n : n + 3]
-    outs = refs[n + 3 : 2 * n + 3]
-    cat_ref, du_ref, sum_ref = refs[2 * n + 3 :]
+    outs = refs[-3 - n : -3]
+    cat_ref, du_ref, sum_ref = refs[-3:]
     r = pl.program_id(0)
     for i in range(n):
 
@@ -766,11 +794,11 @@
                 outs[i][:, s * deep : (s + 1) * deep] = out[s]
 
 
-def feed_back(ds, slope, up, down, fc):
+def feed_back(ds, slope, up, down, fc, base, kept, filler):
     n = len(ds)
     piece, width = ds[0].shape
-    hidden = up.shape[2]
-    whole, flat, tall, shapes = ff_specs(n, piece, width, hidden)
+    rows, hidden = slope.shape
+    whole, flat, tall = ff_specs(n, piece, width, hidden, base)
     got = pl.pallas_call(
         functools.partial(down_kernel, n=n, fc=fc),
         grid=(n,),
@@ -779,16 +807,22 @@
             tall,
             pl.BlockSpec(up.shape, lambda r: (0, 0, 0)),
             pl.BlockSpec(down.shape, lambda r: (0, 0, 0)),
-        ],
+        ]
+        + [pl.BlockSpec(memory_space=pl.ANY)] * len(kept),
         out_specs=[whole] * n + [flat, tall, pl.BlockSpec((1, hidden), lambda r: (0, 0))],
-        out_shape=shapes + [jax.ShapeDtypeStruct((1, hidden), F32)],
+        out_shape=[jax.ShapeDtypeStruct((piece, width), BF16)] * n
+        + [jax.ShapeDtypeStruct((rows, w), BF16) for w in (width, hidden)]
+        + [jax.ShapeDtypeStruct((1, hidden), F32)],
+        input_output_aliases={n + 3 + i: n + i for i in range(len(kept))},
         compiler_params=params(),
-        cost_estimate=cost(
-            4 * n * piece * width * hidden, 12 * n * piece * width + 4 * width * hidden
+        cost_estimate=pl.CostEstimate(
+            flops=16 * n * piece * width * hidden if filler else 1,
+            bytes_accessed=1,
+            transcendentals=0,
         ),
         name="feed_back",
-    )(*ds, slope, up, down)
-    return got[:n], got[n], got[n + 1], got[n + 2]
+    )(*ds, slope, up, down, *kept)
+    return list(got[:n]), list(got[n : n + 2]), got[n + 2]
 
 
 def place_kernel(perm, *refs):
@@ -822,12 +856,22 @@
     refs[-1][...] = refs[-2][...].astype(F32)
 
 
-def store(buffer, joined, first, rows, width, layer, layers):
-    chunk = joined.shape[1]
-    block = math.gcd(math.gcd(rows, 256), first)
-    ins = [
-        pl.BlockSpec((block, chunk), lambda i, j: ((first + j * rows) // block + i, 0)),
-    ]
+def store(buffer, joined, first, rows, width, layer, layers, runs):
+    wide = joined.shape[1]
+    chunk = min(wide, width)
+    own, whole, start = runs
+    stride = rows if width >= wide else rows * width // wide
+    block = math.gcd(math.gcd(math.gcd(stride, 256), first), math.gcd(own, start))
+
+    def place_of(i, j):
+        row = j * rows + i * block
+        side = 0
+        if width < wide:
+            row, side = i * block % stride, i * block // stride
+        row = first + row
+        return ((row // own * whole + start + row % own) // block, side)
+
+    ins = [pl.BlockSpec((block, chunk), place_of)]
     args = [joined]
     alias = {}
     if buffer is not None:
@@ -912,13 +956,14 @@
         first = [w_in[0:1]]
         for bit in range(1, n_shard):
             first.append(swap(w_in[0:1], SHARD, n_shard, bit))
-        segs = [segment_ids[0]]
-        for bit in range(1, n_context):
-            segs.append(swap(segment_ids[0], CONTEXT, n_context, bit))
         tables = jnp.concatenate([row_gains, row_bias], axis=1)
         w_in = [w_in[layer] for layer in range(layers)]
         up_weight = [up_weight[layer] for layer in range(layers)]
         down_weight = [down_weight[layer] for layer in range(layers)]
+        up_weight, segment_ids = lax.optimization_barrier((up_weight, segment_ids))
+        segs = [segment_ids[0]]
+        for bit in range(1, n_context):
+            segs.append(swap(segment_ids[0], CONTEXT, n_context, bit))
         first, segs, tables, merge_weight, up_weight, down_weight, w_in = (
             lax.optimization_barrier(
                 (first, segs, tables, merge_weight, up_weight, down_weight, w_in)
@@ -941,11 +986,19 @@
         x_nat = hidden_in
         saved = []
         for layer in range(layers):
-            perm = order if layer == 0 else relative
-            got = list(project(xs, w_qkv[layer], cols[layer], head_bias[layer], perm, piece))
+            args = (w_qkv[layer], cols[layer], head_bias[layer])
             if layer == 0:
-                got[0], parts, tabs, up_weight, down_weight, w_in = lax.optimization_barrier(
-                    (got[0], parts, tabs, up_weight, down_weight, w_in)
+                got = list(project(xs, *args, order, piece, 0, rows, []))
+            else:
+                near = [x_low, swap(x_low, "tensor", n_tensor, 1)]
+                far = swap(x_low, "tensor", n_tensor, 2)
+                got = list(project(near, *args, relative, piece, 0, rows, []))
+                far, got = lax.optimization_barrier((far, got))
+                far = [far, swap(far, "tensor", n_tensor, 1)]
+                got = list(project(far, *args, relative, piece, 2, rows, got))
+            if layer == 0:
+                got[0], up_weight, down_weight, w_in = lax.optimization_barrier(
+                    (got[0], up_weight, down_weight, w_in)
                 )
                 pair = jnp.stack(parts)
                 far = swap(pair, "tensor", n_tensor, 2)
@@ -971,14 +1024,20 @@
             mixed, normed, low = merge_norm(
                 mine, w_merge, layer, x_own, vec[layer], relative, cols_rel
             )
-            blocks, x1, act, slope = feed_forward(
-                spread(low, n_tensor), w_up[layer], up_bias[layer : layer + 1], w_down[layer], 512
-            )
+            ff_args = (w_up[layer], up_bias[layer : layer + 1], w_down[layer], 512)
+            far = swap(low, "tensor", n_tensor, 2)
+            near = [low, swap(low, "tensor", n_tensor, 1)]
+            blocks, kept = feed_forward(near, *ff_args, 0, rows, [])
+            far, kept = lax.optimization_barrier((far, kept))
+            far = [far, swap(far, "tensor", n_tensor, 1)]
+            got, kept = feed_forward(far, *ff_args, 2, rows, kept)
+            blocks += got
+            x1, act, slope = kept
             terms = [normed] + collect(blocks, n_tensor)
             keep = [x_nat, qkv, ctx, lse, mine, mixed, x1, act, slope]
             if layer + 1 < layers:
+                terms, w_qkv[1] = lax.optimization_barrier((terms, w_qkv[1]))
                 summed, x_own, x_low = second_norm(vec[layer], terms)
-                xs = spread(x_low, n_tensor)
                 keep.append(summed)
             else:
                 out_low, d_summed, d_low, sums = last_norm(vec[layer], d_last, terms)
@@ -1006,12 +1065,15 @@
             return [value[:, i : i + wide] for i in range(0, value.shape[1], wide)]
 
         def join_wide(g_down, g_up):
-            return jnp.concatenate([g_down] + chunks(g_up, g_down.shape[1]), axis=0)
+            return jnp.concatenate(g_down + chunks(g_up, deep), axis=0)
 
         def join_narrow(g_qkv, g_merge):
             flat = g_qkv.reshape(-1, g_qkv.shape[2])
-            wide = min(flat.shape[1], g_merge.shape[1])
-            return jnp.concatenate(chunks(flat, wide) + chunks(g_merge, wide), axis=0)
+            if deep > flat.shape[1]:
+                part = flat.shape[0] * flat.shape[1] // deep
+                sides = [flat[i : i + part] for i in range(0, flat.shape[0], part)]
+                flat = jnp.concatenate(sides, axis=1)
+            return jnp.concatenate(chunks(flat, deep) + [g_merge], axis=0)
 
         tie = lax.optimization_barrier
         grads = [None] * layers
@@ -1025,10 +1087,20 @@
             x_nat, qkv, ctx, lse, mine, mixed, x1, act, slope = saved[layer][:9]
             if not last:
                 d_summed, d_low, sums = second_back(vec[layer], saved[layer][9], terms)
-            blocks, wide = tie((spread(d_low, n_tensor), wide))
+            ff_args = (slope, w_up[layer], w_down[layer], 512)
+            far = swap(d_low, "tensor", n_tensor, 2)
+            near = [d_low, swap(d_low, "tensor", n_tensor, 1)]
             if not last:
+                near, wide = tie((near, jnp.concatenate(wide, axis=0)))
                 wide = context_gather(wide)
-            blocks, dy, du, g_hidden = feed_back(blocks, slope, w_up[layer], w_down[layer], 512)
+            blocks, kept, g_hidden = feed_back(near, *ff_args, 0, [], last)
+            far, kept = tie((far, kept))
+            far = [far, swap(far, "tensor", n_tensor, 1)]
+            got, kept, part = feed_back(far, *ff_args, 2, kept, last)
+            blocks += got
+            blocks, late = tie((blocks, late))
+            g_hidden = g_hidden + part
+            dy, du = kept
 
             def down_part(i, act=act, dy=dy):
                 return dot(act, lax.dynamic_slice_in_dim(dy, i * deep, deep, 1), 0, 0)
@@ -1038,7 +1110,7 @@
 
             terms = [d_summed] + collect(blocks, n_tensor)
             down_send, up_send = send_parts(down_part), send_parts(up_part)
-            terms, down_send, up_send, late, wide = tie((terms, down_send, up_send, late, wide))
+            terms, down_send, up_send, wide = tie((terms, down_send, up_send, wide))
             down_got, up_got = exchange(down_send), exchange(up_send)
             d_mixed, d_low, sums_one, d_mine = first_back(
                 vec[layer], mixed, w_merge, layer, terms, relative, cols_rel
@@ -1052,23 +1124,29 @@
             for r in range(n_tensor):
                 part = lax.dynamic_slice_in_dim(mine, relative[r] * deep_t, deep_t, 0)
                 g_blocks.append(dot(part, d_low, 1, 0).astype(BF16))
-            d_ctx, g_blocks, narrow, down_got, out_low = tie(
-                (d_ctx, g_blocks, narrow, down_got, out_low)
+            g_down = settle(down_part, down_got) if last else ()
+            d_ctx, g_blocks, narrow, down_got, g_down, out_low = tie(
+                (d_ctx, g_blocks, narrow, down_got, g_down, out_low)
             )
             if last:
                 out_low = [out_low, swap(out_low, "tensor", n_tensor, 2)]
+                g_down = context_scatter(g_down)
             else:
                 narrow = context_gather(narrow)
             d_heads = attend_back(
                 qkv, doc, tiles_back, lse, ctx, d_ctx, piece, BQ_BACK, BK_BACK, UNROLL_BACK
             )
-            d_heads, down_got, up_got, g_blocks, out_low, narrow = tie(
-                (d_heads, down_got, up_got, g_blocks, out_low, narrow)
+            d_heads, down_got, up_got, g_blocks, g_down, out_low, narrow = tie(
+                (d_heads, down_got, up_got, g_blocks, g_down, out_low, narrow)
             )
             d_heads = lax.all_to_all(d_heads, CONTEXT, 0, 0, tiled=True)
             g_terms = collect(g_blocks, n_tensor)
             g_merge = sum(term.astype(F32) for term in g_terms).astype(BF16)
-            new_wide = join_wide(settle(down_part, down_got), settle(up_part, up_got))
+            g_up = settle(up_part, up_got)
+            if last:
+                new_wide = join_wide([], g_up)
+            else:
+                new_wide = join_wide([settle(down_part, down_got)], g_up)
             if last:
                 near = [swap(v, "tensor", n_tensor, 1) for v in out_low]
                 out_low = [out_low[0], near[0], out_low[1], near[1]]
@@ -1077,6 +1155,8 @@
                 (d_heads, new_wide, g_merge, narrow, hidden_out)
             )
             new_wide = context_scatter(new_wide)
+            if last:
+                new_wide = [g_down, new_wide]
             got = project_back(d_heads, w_qkv[layer], cols[layer], relative, piece, width)
             d_x, d_proj, g_heads = got[:n_tensor], got[n_tensor], got[n_tensor + 1]
 
@@ -1089,7 +1169,9 @@
 
             qkv_send, merge_send = send_parts(qkv_part), send_parts(merge_part)
             terms = [d_mixed] + collect(d_x, n_tensor)
-            terms, qkv_send, merge_send = tie((terms, qkv_send, merge_send))
+            if layer > 0:
+                terms, qkv_send, merge_send = tie((terms, qkv_send, merge_send))
+
             if not last:
                 grads[layer + 1] = (wide, narrow)
             late = (exchange(qkv_send), exchange(merge_send))
@@ -1100,29 +1182,44 @@
         total = terms[0]
         for term in terms[1:]:
             total = total + term.astype(F32)
-        blocks, wide = tie((spread(total.astype(BF16), n_tensor), wide))
         narrow = join_narrow(settle(makers[0], late[0]), settle(makers[1], late[1]))
-        wide, narrow = tie((wide, narrow))
-        grads[0] = (context_gather(wide), context_gather(context_scatter(narrow)))
-        input_grad = place(blocks, relative, F32)
-        hw = width // n_tensor
-        hidden = up_bias.shape[1]
-        g_down = g_up = g_qkv = g_merge = None
-        for layer in reversed(range(layers)):
-            wide, narrow = grads[layer]
-            g_down = store(g_down, wide, 0, hidden, deep, layer, layers)
-            g_up = store(g_up, wide, hidden, deep, hidden, layer, layers)
-            g_qkv = store(g_qkv, narrow, 0, 3 * deep, hw, layer, layers)
-            g_merge = store(
-                g_merge, narrow, narrow.shape[0] - hw * deep // narrow.shape[1], hw, deep, layer, layers
-            )
-        g_qkv = g_qkv.reshape(layers, 3, deep, -1)
-
+        total, wide, narrow = tie((total.astype(BF16), wide, narrow))
+        blocks = spread(total, n_tensor)
         table = sum_all(jnp.concatenate(rowsums, axis=0), "tensor", n_tensor)
         side = jnp.concatenate(sides).reshape(-1, width)
         packed = jnp.concatenate([table, side], axis=0)
         packed = sum_all(packed, SHARD, n_shard)
         packed = sum_all(packed, CONTEXT, n_context)
+        narrow = context_scatter(narrow)
+        wide, narrow, blocks, packed = tie((wide, narrow, blocks, packed))
+        grads[0] = context_gather(jnp.concatenate([wide, narrow], axis=0))
+        input_grad = place(blocks, relative, F32)
+        hw = width // n_tensor
+        hidden = up_bias.shape[1]
+        g_down = g_up = g_qkv = g_merge = None
+        n_qkv = 3 * deep * hw // deep
+        n_narrow = n_qkv + hw
+        run_w, run_n = 2 * hidden // n_context, n_narrow // n_context
+        for layer in reversed(range(layers)):
+            if layer == 0:
+                wide = narrow = grads[0]
+                runs_d = runs_u = (run_w, run_w + run_n, 0)
+                runs_n = (run_n, run_w + run_n, run_w)
+                second = hidden
+            else:
+                wide, narrow = grads[layer]
+                runs_d = runs_u = runs_n = (1 << 20, 0, 0)
+                second = hidden
+                if layer + 1 == layers:
+                    run = hidden // n_context
+                    runs_d, runs_u, second = (run, 2 * run, 0), (run, 2 * run, run), 0
+                runs_n = (n_narrow, 0, 0)
+            g_down = store(g_down, wide, 0, hidden, deep, layer, layers, runs_d)
+            g_up = store(g_up, wide, second, deep, hidden, layer, layers, runs_u)
+            g_qkv = store(g_qkv, narrow, 0, 3 * deep, hw, layer, layers, runs_n)
+            g_merge = store(g_merge, narrow, n_qkv, hw, deep, layer, layers, runs_n)
+        g_qkv = g_qkv.reshape(layers, 3, deep, -1)
+
         table = packed[: layers * 6].reshape(layers, 6, width)
         table = lax.dynamic_slice_in_dim(table, me_s * deep, deep, 2)
         side = packed[layers * 6 :].reshape(layers, -1)

time: 881 us -> 836 us (0.949)
  waiting for transfers between devices: 414 us -> 367 us
  Pallas kernels: 240 us -> 257 us
    all_to_all x2, waiting for transfers between devices: 22.9 us -> 2.08 us  [shards(): d_ctx = lax.all_to_all(pieces, ('tensor', CONTEXT), 0, 0, tiled=True)]
    all_to_all x2, waiting for transfers between devices: 65.5 us -> 47.7 us  [shards(): qkv = lax.all_to_all(got[0], CONTEXT, 0, 0, tiled=True)]
    ppermute x67, waiting for transfers between devices: 217 us -> 200 us  [swap(): return lax.ppermute(value, axis, [(i, i ^ bit) for i in range(count)])]
    all_gather x1, waiting for transfers between devices: 0.01 us -> 9.16 us  [shards(): w_qkv.append([lax.all_gather(w_in[i], SHARD, axis=0, tiled=False)])]
    all_gather x4 -> x3, waiting for transfers between devices: 40.8 us -> 48.7 us  [context_gather(): return lax.all_gather(value, CONTEXT, axis=0, tiled=True)]
    reduce_scatter x4 -> x5, waiting for transfers between devices: 25.2 us -> 17.7 us  [context_scatter(): return lax.psum_scatter(value, CONTEXT, scatter_dimension=0, tiled=True)]
    pallas_call x2 -> x4, Pallas kernels: 30.3 us -> 37.1 us  [feed_forward(): pl.pallas_call(functools.partial(up_kernel, n=n, fc=fc), grid=(n,), in_sp...]
    pallas_call x2 -> x4, Pallas kernels: 21.4 us -> 28 us  [feed_back(): pl.pallas_call(functools.partial(down_kernel, n=n, fc=fc), grid=(n,), in_...]
  transfers between devices with their start and end apart: 87 -> 87, of which waited for: 43 -> 50; matrix products, arithmetic and copies ran while one was open for 10% -> 10% of each run, Pallas kernels for 21% -> 26%
where the time goes in v2:
time: 836 us; the launch traced here: 833 us
  waiting for transfers between devices  367 us (44%)
  Pallas kernels  257 us (31%)
  starting transfers between devices  69.1 us (8%)
  matrix products  44.5 us (5%)
  other arithmetic  30.4 us (4%)
  local copies, waits for them, and re-layouts  27.3 us (3%)
  between operations  19.2 us (2%)
  blocking collectives  19.1 us (2%)
    ppermute x67, waiting for transfers between devices, swap(): return lax.ppermute(value, axis, [(i, i ^ bit) for i in range(count)])  200 us
    pallas_call x2, Pallas kernels, attend_back(): pl.pallas_call(functools.partial(attend_back_kernel, bq=bq, bk=bk, seq=se...  54 us
    pallas_call x2, Pallas kernels, attend(): pl.pallas_call(functools.partial(attend_kernel, bq=bq, bk=bk, seq=seq, ch...  50.1 us
    all_gather x3, waiting for transfers between devices, context_gather(): return lax.all_gather(value, CONTEXT, axis=0, tiled=True)  48.7 us
    all_to_all x2, waiting for transfers between devices, shards(): qkv = lax.all_to_all(got[0], CONTEXT, 0, 0, tiled=True)  47.7 us
    dot_general x16, matrix products, dot(): lax.dot_general(a, b, (((ca,), (cb,)), ((), ())), preferred_element_type=...  38 us
    ppermute x67, starting transfers between devices, swap(): return lax.ppermute(value, axis, [(i, i ^ bit) for i in range(count)])  37.9 us
    pallas_call x4, Pallas kernels, feed_forward(): pl.pallas_call(functools.partial(up_kernel, n=n, fc=fc), grid=(n,), in_sp...  37.1 us
  transfers between devices with their start and end apart: 87, of which 50 were waited for; matrix products, arithmetic and copies ran while one was open for 10% of the time, Pallas kernels for 26%

profile of v2, /device:TPU:0, one launch (start us, length us, event | category | flops | bytes accessed | tf_op | source)
XLA Modules:
  0.0 833.2 jit_solution(1128084318156948675)
XLA Ops:
  44.8 18.5 %collective-permute-done.5 = bf16[2,256,512]{2,1,0:T(8,128)(2,1)S(1)} collective-permute-done((bf16[2,256,512]{2,1,0:T(8,128)(2,1)S(1)}, bf16[2,256,512]{2,1,0:T(8,128)(2,1)S(1)}, u32[]{:S(2)}, u32[]{:S(2)}) %collective-permute-start.5) | collective-permute-done | bytes 524320 | tf_op jit(solution)/shard_map/ppermute | solution.py:895
  68.1 10.7 %all-to-all-done.qkv = bf16[4,3,64,1024]{3,2,1,0:T(8,128)(2,1)} async-done(((bf16[4,3,64,1024]{3,2,1,0:T(8,128)(2,1)}), bf16[4,3,64,1024]{3,2,1,0:T(8,128)(2,1)}, u32[]{:S(2)}, u32[]{:S(2)}) %all-to-all-start) | async-done | bytes 1572896 | tf_op jit(solution)/shard_map/all_to_all | solution.py:1016
  78.7 35.1 %attend.2 = (bf16[16,64,256]{2,1,0:T(8,128)(2,1)S(1)}, f32[16,64,256]{2,1,0:T(8,128)S(1)}, f32[1,4096]{1,0:T(1,128)S(1)}) custom-call(s32[397]{0:T(512)S(1)} %pad_add_fusion.2.tiles, bf16[4,3,64,1024]{3,2,1,0:T(8,128)(2,1)} %all-to-all-done.qkv, s32[1,4096]{1,0:T(1,128)S(1)} %bitcast.99, s32[1,4096]{1,0:T(1,128)S(1)} %sub.94.length), custom_call_target="tpu_custom_call" | custom-call | flops 1 | bytes 1 | tf_op jit(solution)/shard_map/attend/pallas_call | solution.py:278
  126.0 9.1 %all-to-all-done.1 = bf16[16,64,256]{2,1,0:T(8,128)(2,1)} async-done(((bf16[16,64,256]{2,1,0:T(8,128)(2,1)}), bf16[16,64,256]{2,1,0:T(8,128)(2,1)}, u32[]{:S(2)}, u32[]{:S(2)}) %all-to-all-start.1) | async-done | bytes 524320 | tf_op jit(solution)/shard_map/all_to_all | solution.py:1022
  142.5 9.2 %feed_forward.4 = (bf16[256,1024]{1,0:T(8,128)(2,1)}, bf16[256,1024]{1,0:T(8,128)(2,1)}, bf16[1024,1024]{1,0:T(8,128)(2,1)}, bf16[1024,1024]{1,0:T(8,128)(2,1)}, bf16[1024,1024]{1,0:T(8,128)(2,1)}) custom-call(bf16[256,1024]{1,0:T(8,128)(2,1)} %get-tuple-element.250.refs_0_, bf16[256,1024]{1,0:T(8,128)(2,1)} %collective-permute-done.9.refs_1_, ...), custom_call_target="tpu_custom_call" | custom-call | flops 8589934592 | bytes 1 | tf_op jit(solution)/shard_map/feed_forward/pallas_call | solution.py:739
  157.8 9.5 %feed_forward.5 = (bf16[256,1024]{1,0:T(8,128)(2,1)}, bf16[256,1024]{1,0:T(8,128)(2,1)}, bf16[1024,1024]{1,0:T(8,128)(2,1)}, bf16[1024,1024]{1,0:T(8,128)(2,1)}, bf16[1024,1024]{1,0:T(8,128)(2,1)}) custom-call(bf16[256,1024]{1,0:T(8,128)(2,1)} %collective-permute-done.11.refs_0_, ...), custom_call_target="tpu_custom_call", output_to_operand_aliasing={{2}: (5, {}), {3}: (6, {}), {4}: (7, {})} | custom-call | flops 8589934592 | bytes 1 | tf_op jit(solution)/shard_map/feed_forward/pallas_call | solution.py:739
  171.6 9.2 %all-gather.24.cloned.1.call-done = bf16[6,512,256]{2,1,0:T(8,128)(2,1)} async-done(((bf16[3,512,256]{2,1,0:T(8,128)(2,1)}), bf16[6,512,256]{2,1,0:T(8,128)(2,1)}) %all-gather.24.cloned.1.call-update) | async-done | bytes 1572880 | tf_op jit(solution)/shard_map/all_gather | solution.py:1010
  216.4 37.0 %all-to-all-done.2.qkv = bf16[4,3,64,1024]{3,2,1,0:T(8,128)(2,1)} async-done(((bf16[4,3,64,1024]{3,2,1,0:T(8,128)(2,1)}), bf16[4,3,64,1024]{3,2,1,0:T(8,128)(2,1)}, u32[]{:S(2)}, u32[]{:S(2)}) %all-to-all-start.2) | async-done | bytes 1572896 | tf_op jit(solution)/shard_map/all_to_all | solution.py:1016
  253.4 14.9 %attend.3 = (bf16[16,64,256]{2,1,0:T(8,128)(2,1)S(1)}, f32[16,64,256]{2,1,0:T(8,128)S(1)}, f32[1,4096]{1,0:T(1,128)S(1)}) custom-call(s32[397]{0:T(512)S(1)} %pad_add_fusion.2.tiles, bf16[4,3,64,1024]{3,2,1,0:T(8,128)(2,1)} %all-to-all-done.2.qkv, s32[1,4096]{1,0:T(1,128)S(1)} %bitcast.100, s32[1,4096]{1,0:T(1,128)S(1)} %sub.94.length), custom_call_target="tpu_custom_call" | custom-call | flops 1 | bytes 1 | tf_op jit(solution)/shard_map/attend/pallas_call | solution.py:278
  269.4 19.1 %all_to_all.40 = bf16[16,64,256]{2,1,0:T(8,128)(2,1)} all-to-all(bf16[16,64,256]{2,1,0:T(8,128)(2,1)S(1)} %get-tuple-element.278), channel_id=1, replica_groups=mesh['shard'=2,'context'=4,'tensor'=4] {'tensor','context'}, dimensions={0} | all-to-all | bytes 1048576 | tf_op jit(solution)/shard_map/all_to_all | solution.py:1022
  295.8 9.2 %feed_forward.6 = (bf16[256,1024]{1,0:T(8,128)(2,1)}, bf16[256,1024]{1,0:T(8,128)(2,1)}, bf16[1024,1024]{1,0:T(8,128)(2,1)}, bf16[1024,1024]{1,0:T(8,128)(2,1)}, bf16[1024,1024]{1,0:T(8,128)(2,1)}) custom-call(bf16[256,1024]{1,0:T(8,128)(2,1)} %get-tuple-element.282.refs_0_, bf16[256,1024]{1,0:T(8,128)(2,1)} %collective-permute-done.18.refs_1_, ...), custom_call_target="tpu_custom_call" | custom-call | flops 8589934592 | bytes 1 | tf_op jit(solution)/shard_map/feed_forward/pallas_call | solution.py:739
  311.1 9.2 %feed_forward.7 = (bf16[256,1024]{1,0:T(8,128)(2,1)}, bf16[256,1024]{1,0:T(8,128)(2,1)}, bf16[1024,1024]{1,0:T(8,128)(2,1)}, bf16[1024,1024]{1,0:T(8,128)(2,1)}, bf16[1024,1024]{1,0:T(8,128)(2,1)}) custom-call(bf16[256,1024]{1,0:T(8,128)(2,1)} %collective-permute-done.20.refs_0_, ...), custom_call_target="tpu_custom_call", output_to_operand_aliasing={{2}: (5, {}), {3}: (6, {}), {4}: (7, {})} | custom-call | flops 8589934592 | bytes 1 | tf_op jit(solution)/shard_map/feed_forward/pallas_call | solution.py:739
  325.1 12.6 %collective-permute-done.23.refs_3_ = bf16[256,1024]{1,0:T(8,128)(2,1)S(1)} collective-permute-done((bf16[256,1024]{1,0:T(8,128)(2,1)S(1)}, bf16[256,1024]{1,0:T(8,128)(2,1)S(1)}, u32[]{:S(2)}, u32[]{:S(2)}) %collective-permute-start.23) | collective-permute-done | bytes 524320 | tf_op jit(solution)/shard_map/ppermute | solution.py:895
  418.3 27.0 %attend_back.2 = bf16[4,3,64,1024]{3,2,1,0:T(8,128)(2,1)} custom-call(s32[781]{0:T(1024)S(1)} %pad_add_fusion.1.tiles, bf16[4,3,64,1024]{3,2,1,0:T(8,128)(2,1)} %all-to-all-done.2.qkv, s32[1,4096]{1,0:T(1,128)S(1)} %bitcast.101, s32[1,4096]{1,0:T(1,128)S(1)} %sub.94.length, f32[1,4096]{1,0:T(1,128)S(1)} %get-tuple-element.321.lse, ...), custom_call_target="tpu_custom_call" | custom-call | flops 1 | bytes 1 | tf_op jit(solution)/shard_map/attend_back/pallas_call | solution.py:389
  469.9 17.2 %all-to-all-done.5.refs_0_ = bf16[4,3,64,1024]{3,2,1,0:T(8,128)(2,1)} async-done(((bf16[4,3,64,1024]{3,2,1,0:T(8,128)(2,1)}), bf16[4,3,64,1024]{3,2,1,0:T(8,128)(2,1)}, u32[]{:S(2)}, u32[]{:S(2)}) %all-to-all-start.5) | async-done | bytes 1572896 | tf_op jit(solution)/shard_map/all_to_all | solution.py:1142
  501.7 11.1 %collective-permute-done.40.refs_3_ = bf16[256,1024]{1,0:T(8,128)(2,1)S(1)} collective-permute-done((bf16[256,1024]{1,0:T(8,128)(2,1)S(1)}, bf16[256,1024]{1,0:T(8,128)(2,1)S(1)}, u32[]{:S(2)}, u32[]{:S(2)}) %collective-permute-start.40) | collective-permute-done | bytes 524320 | tf_op jit(solution)/shard_map/ppermute | solution.py:895
  583.0 17.7 %reduce-scatter.10.cloned.1.call-done = bf16[256,512]{1,0:T(8,128)(2,1)} async-done(((bf16[1024,512]{1,0:T(8,128)(2,1)}), bf16[256,512]{1,0:T(8,128)(2,1)}) %reduce-scatter.10.cloned.1.call-update) | async-done | bytes 262160 | tf_op jit(solution)/shard_map/reduce_scatter | solution.py:1059
  604.1 27.0 %attend_back.3 = bf16[4,3,64,1024]{3,2,1,0:T(8,128)(2,1)} custom-call(s32[781]{0:T(1024)S(1)} %pad_add_fusion.1.tiles, bf16[4,3,64,1024]{3,2,1,0:T(8,128)(2,1)} %all-to-all-done.qkv, s32[1,4096]{1,0:T(1,128)S(1)} %bitcast.102, s32[1,4096]{1,0:T(1,128)S(1)} %sub.94.length, f32[1,4096]{1,0:T(1,128)S(1)} %get-tuple-element.240.lse, ...), custom_call_target="tpu_custom_call" | custom-call | flops 1 | bytes 1 | tf_op jit(solution)/shard_map/attend_back/pallas_call | solution.py:389
  645.3 11.1 %collective-permute-done.53 = bf16[256,1024]{1,0:T(8,128)(2,1)} collective-permute-done((bf16[256,1024]{1,0:T(8,128)(2,1)S(1)}, bf16[256,1024]{1,0:T(8,128)(2,1)}, u32[]{:S(2)}, u32[]{:S(2)}) %collective-permute-start.53) | collective-permute-done | bytes 524320 | tf_op jit(solution)/shard_map/ppermute | solution.py:895
  657.9 14.2 %all-to-all-done.7.refs_0_ = bf16[4,3,64,1024]{3,2,1,0:T(8,128)(2,1)} async-done(((bf16[4,3,64,1024]{3,2,1,0:T(8,128)(2,1)}), bf16[4,3,64,1024]{3,2,1,0:T(8,128)(2,1)}, u32[]{:S(2)}, u32[]{:S(2)}) %all-to-all-start.7) | async-done | bytes 1572896 | tf_op jit(solution)/shard_map/all_to_all | solution.py:1142
  685.0 21.7 %collective-permute-done.58 = bf16[256,512]{1,0:T(8,128)(2,1)S(1)} collective-permute-done((bf16[256,512]{1,0:T(8,128)(2,1)S(1)}, bf16[256,512]{1,0:T(8,128)(2,1)S(1)}, u32[]{:S(2)}, u32[]{:S(2)}) %collective-permute-start.58) | collective-permute-done | bytes 262176 | tf_op jit(solution)/shard_map/ppermute | solution.py:895
  711.0 8.2 collective-permute-done.56
  724.9 8.9 %collective-permute-done.63 = f32[12,1024]{1,0:T(8,128)S(1)} collective-permute-done((f32[12,1024]{1,0:T(8,128)S(1)}, f32[12,1024]{1,0:T(8,128)S(1)}, u32[]{:S(2)}, u32[]{:S(2)}) %collective-permute-start.63) | collective-permute-done | bytes 49184 | tf_op jit(solution)/shard_map/ppermute | solution.py:895
  769.0 48.7 %all-gather.18.cloned.1.call-done.refs_1_ = bf16[3072,512]{1,0:T(8,128)(2,1)} async-done(((bf16[768,512]{1,0:T(8,128)(2,1)}), bf16[3072,512]{1,0:T(8,128)(2,1)}) %all-gather.18.cloned.1.call-update) | async-done | bytes 3145744 | tf_op jit(solution)/shard_map/all_gather | solution.py:1062
  (454 shorter events, 397.7 us)
Async XLA Ops:
  7.2 134.5 %all-gather.20.cloned.1.call-start = ((), (), s32[]{:S(2)}) async-start(), calls=%async_computation.21 | async-start | bytes 3145728 | tf_op jit(solution)/shard_map/all_gather | solution.py:1012
  37.3 41.4 %all-to-all-start = ((bf16[4,3,64,1024]{3,2,1,0:T(8,128)(2,1)}), bf16[4,3,64,1024]{3,2,1,0:T(8,128)(2,1)}, u32[]{:S(2)}, u32[]{:S(2)}) async-start(bf16[4,3,64,1024]{3,2,1,0:T(8,128)(2,1)} %project.3), calls=%async_computation | async-start | bytes 3145728 | tf_op jit(solution)/shard_map/all_to_all | solution.py:1016
  42.5 99.2 %all-gather.22.cloned.1.call-start = ((), (), s32[]{:S(2)}) async-start(), calls=%async_computation.22 | async-start | bytes 3145728 | tf_op jit(solution)/shard_map/all_gather | solution.py:1013
  64.5 50.2 %collective-permute-start.6 = (bf16[2,2,256,512]{3,2,1,0:T(8,128)(2,1)}, bf16[2,2,256,512]{3,2,1,0:T(8,128)(2,1)}, u32[]{:S(2)}, u32[]{:S(2)}) collective-permute-start(bf16[2,2,256,512]{3,2,1,0:T(8,128)(2,1)} %pad_maximum_fusion.1.refs_0_), channel_id=1, source_target_pairs={{0,2},{1,3},{2,0},{3,1},{4,6},{5,7},{6,4},{7,5},{8,10},{9,11},{10,... | collective-permute-start | bytes 3145736 | tf_op jit(solution)/shard_map/ppermute | solution.py:895
  119.5 61.4 %all-gather.24.cloned.1.call-start = ((), (), s32[]{:S(2)}) async-start(), calls=%async_computation.23 | async-start | bytes 2359296 | tf_op jit(solution)/shard_map/all_gather | solution.py:1010
  155.5 138.8 %all-gather.26.cloned.1.call-start = ((), (), s32[]{:S(2)}) async-start(), calls=%async_computation.24 | async-start | bytes 3145728 | tf_op jit(solution)/shard_map/all_gather | solution.py:1012
  211.4 42.0 %all-to-all-start.2 = ((bf16[4,3,64,1024]{3,2,1,0:T(8,128)(2,1)}), bf16[4,3,64,1024]{3,2,1,0:T(8,128)(2,1)}, u32[]{:S(2)}, u32[]{:S(2)}) async-start(bf16[4,3,64,1024]{3,2,1,0:T(8,128)(2,1)} %get-tuple-element.277), calls=%async_computation.2 | async-start | bytes 3145728 | tf_op jit(solution)/shard_map/all_to_all | solution.py:1016
  215.8 78.6 %all-gather.28.cloned.1.call-start = ((), (), s32[]{:S(2)}) async-start(), calls=%async_computation.25 | async-start | bytes 3145728 | tf_op jit(solution)/shard_map/all_gather | solution.py:1013
  397.8 47.6 %reduce-scatter.6.cloned.1.call-start = ((), (), s32[]{:S(2)}) async-start(), calls=%async_computation.13 | async-start | bytes 1310720 | tf_op jit(solution)/shard_map/reduce_scatter | solution.py:1059
  413.5 31.9 %collective-permute-start.31 = (bf16[512,1024]{1,0:T(8,128)(2,1)}, bf16[512,1024]{1,0:T(8,128)(2,1)}, u32[]{:S(2)}, u32[]{:S(2)}) collective-permute-start(bf16[512,1024]{1,0:T(8,128)(2,1)} %convolution_convert_fusion.2), channel_id=1, source_target_pairs={{0,16},{16,0},{1,17},{17,1},{2,18},{18,2},{3,19},{19,3},{4,20},{20... | collective-permute-start | bytes 3145736 | tf_op jit(solution)/shard_map/ppermute | solution.py:895
  415.7 29.7 %collective-permute-start.32 = (bf16[256,1024]{1,0:T(8,128)(2,1)}, bf16[256,1024]{1,0:T(8,128)(2,1)}, u32[]{:S(2)}, u32[]{:S(2)}) collective-permute-start(bf16[256,1024]{1,0:T(8,128)(2,1)} %get-tuple-element.341.refs_0_), channel_id=1, source_target_pairs={{0,2},{1,3},{2,0},{3,1},{4,6},{5,7},{6,4},{7,5},{8,10},{9,11},{10,... | collective-permute-start | bytes 1572872 | tf_op jit(solution)/shard_map/ppermute | solution.py:895
  445.4 41.8 %all-to-all-start.5 = ((bf16[4,3,64,1024]{3,2,1,0:T(8,128)(2,1)}), bf16[4,3,64,1024]{3,2,1,0:T(8,128)(2,1)}, u32[]{:S(2)}, u32[]{:S(2)}) async-start(bf16[4,3,64,1024]{3,2,1,0:T(8,128)(2,1)} %attend_back.2), calls=%async_computation.6 | async-start | bytes 3145728 | tf_op jit(solution)/shard_map/all_to_all | solution.py:1142
  449.9 67.9 %reduce-scatter.8.cloned.1.call-start = ((), (), s32[]{:S(2)}) async-start(), calls=%async_computation.14 | async-start | bytes 1310720 | tf_op jit(solution)/shard_map/reduce_scatter | solution.py:1059
  487.2 77.4 %all-gather.14.cloned.1.call-start = ((), (), s32[]{:S(2)}) async-start(), calls=%async_computation.15 | async-start | bytes 2621440 | tf_op jit(solution)/shard_map/all_gather | solution.py:1062
  519.9 80.8 %reduce-scatter.10.cloned.1.call-start = ((), (), s32[]{:S(2)}) async-start(), calls=%async_computation.16 | async-start | bytes 1310720 | tf_op jit(solution)/shard_map/reduce_scatter | solution.py:1059
  564.6 37.8 %collective-permute-start.49 = (bf16[1024,512]{1,0:T(8,128)(2,1)S(1)}, bf16[1024,512]{1,0:T(8,128)(2,1)}, u32[]{:S(2)}, u32[]{:S(2)}) collective-permute-start(bf16[1024,512]{1,0:T(8,128)(2,1)S(1)} %convolution_convert_fusion.1), channel_id=1, source_target_pairs={{0,16},{16,0},{1,17},{17,1},{2,18},{18,2},{3,19},{19,3},{4,20},{20... | collective-permute-start | bytes 3145736 | tf_op jit(solution)/shard_map/ppermute | solution.py:895
  570.7 31.7 %all-to-all-start.6 = ((bf16[16,64,256]{2,1,0:T(8,128)(2,1)}), bf16[16,64,256]{2,1,0:T(8,128)(2,1)S(1)}, u32[]{:S(2)}, u32[]{:S(2)}) async-start(bf16[16,64,256]{2,1,0:T(8,128)(2,1)} %bitcast.123), calls=%async_computation.8 | async-start | bytes 1048576 | tf_op jit(solution)/shard_map/all_to_all | solution.py:1122
  574.4 56.7 %all-gather.16.cloned.1.call-start = ((), (), s32[]{:S(2)}) async-start(), calls=%async_computation.17 | async-start | bytes 1310720 | tf_op jit(solution)/shard_map/all_gather | solution.py:1062
  602.4 28.6 %collective-permute-start.50 = (bf16[512,1024]{1,0:T(8,128)(2,1)}, bf16[512,1024]{1,0:T(8,128)(2,1)}, u32[]{:S(2)}, u32[]{:S(2)}) collective-permute-start(bf16[512,1024]{1,0:T(8,128)(2,1)} %convolution_convert_fusion), channel_id=1, source_target_pairs={{0,16},{16,0},{1,17},{17,1},{2,18},{18,2},{3,19},{19,3},{4,20},{20... | collective-permute-start | bytes 3145736 | tf_op jit(solution)/shard_map/ppermute | solution.py:895
  631.1 41.1 %all-to-all-start.7 = ((bf16[4,3,64,1024]{3,2,1,0:T(8,128)(2,1)}), bf16[4,3,64,1024]{3,2,1,0:T(8,128)(2,1)}, u32[]{:S(2)}, u32[]{:S(2)}) async-start(bf16[4,3,64,1024]{3,2,1,0:T(8,128)(2,1)} %attend_back.3), calls=%async_computation.10 | async-start | bytes 3145728 | tf_op jit(solution)/shard_map/all_to_all | solution.py:1142
  635.5 85.7 %reduce-scatter.12.cloned.1.call-start = ((), (), s32[]{:S(2)}) async-start(), calls=%async_computation.18 | async-start | bytes 2621440 | tf_op jit(solution)/shard_map/reduce_scatter | solution.py:1059
  672.2 80.0 %reduce-scatter.14.cloned.1.call-start = ((), (), s32[]{:S(2)}) async-start(), calls=%async_computation.19 | async-start | bytes 1310720 | tf_op jit(solution)/shard_map/reduce_scatter | solution.py:1059
  684.8 26.2 %collective-permute-start.54 = (bf16[256,1024]{1,0:T(8,128)(2,1)}, bf16[256,1024]{1,0:T(8,128)(2,1)}, u32[]{:S(2)}, u32[]{:S(2)}) collective-permute-start(bf16[256,1024]{1,0:T(8,128)(2,1)} %get-tuple-element.412), channel_id=1, source_target_pairs={{0,1},{1,0},{2,3},{3,2},{4,5},{5,4},{6,7},{7,6},{8,9},{9,8},{10,11... | collective-permute-start | bytes 1572872 | tf_op jit(solution)/shard_map/ppermute | solution.py:895
  721.3 96.5 %all-gather.18.cloned.1.call-start = ((), (), s32[]{:S(2)}) async-start(), calls=%async_computation.20 | async-start | bytes 3932160 | tf_op jit(solution)/shard_map/all_gather | solution.py:1062
  (133 other events, 1536.5 us)
Sparse Core Ops, SparseCore 0:
  37.4 40.3 all-gather.19
  80.0 34.2 all-gather.21
  155.7 25.0 all-gather.23
  203.9 30.7 all-gather.25
  236.1 33.1 all-gather.27
  413.6 26.3 reduce-scatter.5
  487.3 24.6 reduce-scatter.7
  520.0 43.4 all-gather.13
  566.4 34.2 reduce-scatter.9
  602.6 28.0 all-gather.15
  672.3 42.9 reduce-scatter.11
  721.4 28.0 reduce-scatter.13
  754.4 63.2 all-gather.17

commit v3 on v2

--- a/solution.py
+++ b/solution.py
@@ -697,12 +697,9 @@
     up, bias, down = refs[n : n + 3]
     outs = refs[-3 - n : -3]
     cat_ref, act_ref, slope_ref = refs[-3:]
-    r = pl.program_id(0)
+    piece = xs[0].shape[0]
     for i in range(n):
-
-        @pl.when(r == i)
-        def _():
-            cat_ref[...] = xs[i][...]
+        cat_ref[i * piece : (i + 1) * piece, :] = xs[i][...]
 
     halves, deep, hidden = up.shape
     for f in range(0, hidden, fc):
@@ -715,19 +712,16 @@
         act_ref[:, fs] = (u * phi).astype(BF16)
         slope = phi + u * (jnp.exp(-0.5 * u * u) * 0.3989422804014327)
         slope_ref[:, fs] = slope.astype(BF16)
-    out = [dot(act_ref[...], down[s], 1, 0).astype(BF16) for s in range(halves)]
-    for i in range(n):
-
-        @pl.when(r == i)
-        def _():
-            for s in range(halves):
-                outs[i][:, s * deep : (s + 1) * deep] = out[s]
+    for s in range(halves):
+        out = dot(act_ref[...], down[s], 1, 0).astype(BF16)
+        for i in range(n):
+            outs[i][:, s * deep : (s + 1) * deep] = out[i * piece : (i + 1) * piece]
 
 
 def ff_specs(n, piece, width, hidden, base):
     whole = pl.BlockSpec((piece, width), lambda r: (0, 0))
-    flat = pl.BlockSpec((piece, width), lambda r: (r + base, 0))
-    tall = pl.BlockSpec((piece, hidden), lambda r: (r + base, 0))
+    flat = pl.BlockSpec((n * piece, width), lambda r: (base // n, 0))
+    tall = pl.BlockSpec((n * piece, hidden), lambda r: (base // n, 0))
     return whole, flat, tall
 
 
@@ -738,7 +732,7 @@
     whole, flat, tall = ff_specs(n, piece, width, hidden, base)
     got = pl.pallas_call(
         functools.partial(up_kernel, n=n, fc=fc),
-        grid=(n,),
+        grid=(1,),
         in_specs=[whole] * n
         + [
             pl.BlockSpec(up.shape, lambda r: (0, 0, 0)),
@@ -764,19 +758,10 @@
     slope_ref, up, down = refs[n : n + 3]
     outs = refs[-3 - n : -3]
     cat_ref, du_ref, sum_ref = refs[-3:]
-    r = pl.program_id(0)
+    piece = ds[0].shape[0]
     for i in range(n):
-
-        @pl.when(r == i)
-        def _():
-            cat_ref[...] = ds[i][...]
-
+        cat_ref[i * piece : (i + 1) * piece, :] = ds[i][...]
     halves, deep, hidden = up.shape
-
-    @pl.when(r == 0)
-    def _():
-        sum_ref[...] = jnp.zeros_like(sum_ref)
-
     for f in range(0, hidden, fc):
         fs = slice(f, f + fc)
         d = dot(cat_ref[:, :deep], down[0, fs, :], 1, 1)
@@ -784,14 +769,11 @@
             d = d + dot(cat_ref[:, s * deep : (s + 1) * deep], down[s, fs, :], 1, 1)
         du = (d * slope_ref[:, fs].astype(F32)).astype(BF16)
         du_ref[:, fs] = du
-        sum_ref[:, fs] += column(du.astype(F32))
-    out = [dot(du_ref[...], up[s], 1, 1).astype(BF16) for s in range(halves)]
-    for i in range(n):
-
-        @pl.when(r == i)
-        def _():
-            for s in range(halves):
-                outs[i][:, s * deep : (s + 1) * deep] = out[s]
+        sum_ref[:, fs] = column(du.astype(F32))
+    for s in range(halves):
+        out = dot(du_ref[...], up[s], 1, 1).astype(BF16)
+        for i in range(n):
+            outs[i][:, s * deep : (s + 1) * deep] = out[i * piece : (i + 1) * piece]
 
 
 def feed_back(ds, slope, up, down, fc, base, kept, filler):
@@ -801,7 +783,7 @@
     whole, flat, tall = ff_specs(n, piece, width, hidden, base)
     got = pl.pallas_call(
         functools.partial(down_kernel, n=n, fc=fc),
-        grid=(n,),
+        grid=(1,),
         in_specs=[whole] * n
         + [
             tall,
@@ -852,18 +834,26 @@
     )(perm, *blocks)
 
 
-def store_kernel(*refs):
-    refs[-1][...] = refs[-2][...].astype(F32)
-
-
-def store(buffer, joined, first, rows, width, layer, layers, runs):
+def store_kernel(*refs, n):
+    for source, target in zip(refs[-2 * n : -n], refs[-n:]):
+        target[...] = source[...].astype(F32)
+
+
+def part_specs(joined, first, rows, width, runs, layer):
     wide = joined.shape[1]
     chunk = min(wide, width)
     own, whole, start = runs
     stride = rows if width >= wide else rows * width // wide
     block = math.gcd(math.gcd(math.gcd(stride, 256), first), math.gcd(own, start))
-
-    def place_of(i, j):
+    down = rows // block
+    steps = down * (width // chunk)
+
+    def spot(t):
+        t = jnp.minimum(t, steps - 1)
+        return t % down, t // down
+
+    def source(t):
+        i, j = spot(t)
         row = j * rows + i * block
         side = 0
         if width < wide:
@@ -871,24 +861,31 @@
         row = first + row
         return ((row // own * whole + start + row % own) // block, side)
 
-    ins = [pl.BlockSpec((block, chunk), place_of)]
-    args = [joined]
-    alias = {}
-    if buffer is not None:
-        ins = [pl.BlockSpec(memory_space=pl.ANY)] + ins
-        args = [buffer] + args
-        alias = {0: 0}
+    def target(t):
+        i, j = spot(t)
+        return (layer, i, j)
+
+    return (
+        steps,
+        pl.BlockSpec((block, chunk), source),
+        pl.BlockSpec((None, block, chunk), target),
+    )
+
+
+def store(buffers, items, layer, layers):
+    n = len(items)
+    parts = [part_specs(*item, layer) for item in items]
     return pl.pallas_call(
-        store_kernel,
-        grid=(rows // block, width // chunk),
-        in_specs=ins,
-        out_specs=pl.BlockSpec((None, block, chunk), lambda i, j: (layer, i, j)),
-        out_shape=jax.ShapeDtypeStruct((layers, rows, width), F32),
-        input_output_aliases=alias,
+        functools.partial(store_kernel, n=n),
+        grid=(max(part[0] for part in parts),),
+        in_specs=[pl.BlockSpec(memory_space=pl.ANY)] * len(buffers) + [p[1] for p in parts],
+        out_specs=[p[2] for p in parts],
+        out_shape=[jax.ShapeDtypeStruct((layers, item[2], item[3]), F32) for item in items],
+        input_output_aliases={i: i for i in range(len(buffers))},
         compiler_params=params(32),
-        cost_estimate=cost(rows * width, 6 * rows * width),
+        cost_estimate=cost(1, 1),
         name="store",
-    )(*args)
+    )(*buffers, *[item[0] for item in items])
 
 
 def swap(value, axis, count, bit):
@@ -1183,7 +1180,8 @@
         for term in terms[1:]:
             total = total + term.astype(F32)
         narrow = join_narrow(settle(makers[0], late[0]), settle(makers[1], late[1]))
-        total, wide, narrow = tie((total.astype(BF16), wide, narrow))
+        total = total.astype(BF16)
+        wide, narrow = tie((wide, narrow))
         blocks = spread(total, n_tensor)
         table = sum_all(jnp.concatenate(rowsums, axis=0), "tensor", n_tensor)
         side = jnp.concatenate(sides).reshape(-1, width)
@@ -1191,12 +1189,12 @@
         packed = sum_all(packed, SHARD, n_shard)
         packed = sum_all(packed, CONTEXT, n_context)
         narrow = context_scatter(narrow)
-        wide, narrow, blocks, packed = tie((wide, narrow, blocks, packed))
+        blocks, packed = tie((blocks, packed))
         grads[0] = context_gather(jnp.concatenate([wide, narrow], axis=0))
         input_grad = place(blocks, relative, F32)
         hw = width // n_tensor
         hidden = up_bias.shape[1]
-        g_down = g_up = g_qkv = g_merge = None
+        stored = []
         n_qkv = 3 * deep * hw // deep
         n_narrow = n_qkv + hw
         run_w, run_n = 2 * hidden // n_context, n_narrow // n_context
@@ -1214,10 +1212,14 @@
                     run = hidden // n_context
                     runs_d, runs_u, second = (run, 2 * run, 0), (run, 2 * run, run), 0
                 runs_n = (n_narrow, 0, 0)
-            g_down = store(g_down, wide, 0, hidden, deep, layer, layers, runs_d)
-            g_up = store(g_up, wide, second, deep, hidden, layer, layers, runs_u)
-            g_qkv = store(g_qkv, narrow, 0, 3 * deep, hw, layer, layers, runs_n)
-            g_merge = store(g_merge, narrow, n_qkv, hw, deep, layer, layers, runs_n)
+            items = [
+                (wide, 0, hidden, deep, runs_d),
+                (wide, second, deep, hidden, runs_u),
+                (narrow, 0, 3 * deep, hw, runs_n),
+                (narrow, n_qkv, hw, deep, runs_n),
+            ]
+            stored = store(stored, items, layer, layers)
+        g_down, g_up, g_qkv, g_merge = stored
         g_qkv = g_qkv.reshape(layers, 3, deep, -1)
 
         table = packed[: layers * 6].reshape(layers, 6, width)

time: 836 us -> 837 us (level)
  starting transfers between devices: 69.1 us -> 98.7 us
  Pallas kernels: 257 us -> 228 us
  waiting for transfers between devices: 367 us -> 358 us
    all_gather x3, waiting for transfers between devices: 48.7 us -> 0.01 us  [context_gather(): return lax.all_gather(value, CONTEXT, axis=0, tiled=True)]
    reduce_scatter x5, waiting for transfers between devices: 17.7 us -> 51.6 us  [context_scatter(): return lax.psum_scatter(value, CONTEXT, scatter_dimension=0, tiled=True)]
    ppermute x67, starting transfers between devices: 37.9 us -> 67.3 us  [swap(): return lax.ppermute(value, axis, [(i, i ^ bit) for i in range(count)])]
    pallas_call x2, Pallas kernels: 50.1 us -> 29.9 us  [attend(): pl.pallas_call(functools.partial(attend_kernel, bq=bq, bk=bk, seq=seq, ch...]
    all_gather x1, waiting for transfers between devices: 9.16 us -> 19.1 us  [shards(): w_qkv.append([lax.all_gather(w_in[i], SHARD, axis=0, tiled=False)])]
    pallas_call x16 -> x10, Pallas kernels: 78.8 us -> 69.1 us  [the longest x4 34.2 us: feed_forward(): pl.pallas_call(functools.partial(up_kernel, n=n, fc=fc), grid=(1,), in_sp...]
    all_to_all x1, waiting for transfers between devices: 9.1 us -> 0.01 us  [shards(): mine = lax.all_to_all(ctx_low, ('tensor', CONTEXT), 0, 0, tiled=True)]
  transfers between devices with their start and end apart: 87 -> 87, of which waited for: 50 -> 49; matrix products, arithmetic and copies ran while one was open for 10% -> 11% of each run, Pallas kernels for 26% -> 24%
where the time goes in v3:
time: 837 us; the launch traced here: 827 us
  waiting for transfers between devices  358 us (43%)
  Pallas kernels  228 us (27%)
  starting transfers between devices  98.7 us (12%)
  matrix products  44.5 us (5%)
  other arithmetic  31.1 us (4%)
  local copies, waits for them, and re-layouts  28 us (3%)
  blocking collectives  19.3 us (2%)
  between operations  19.1 us (2%)
    ppermute x67, waiting for transfers between devices, swap(): return lax.ppermute(value, axis, [(i, i ^ bit) for i in range(count)])  203 us
    ppermute x67, starting transfers between devices, swap(): return lax.ppermute(value, axis, [(i, i ^ bit) for i in range(count)])  67.3 us
    pallas_call x2, Pallas kernels, attend_back(): pl.pallas_call(functools.partial(attend_back_kernel, bq=bq, bk=bk, seq=se...  56.1 us
    reduce_scatter x5, waiting for transfers between devices, context_scatter(): return lax.psum_scatter(value, CONTEXT, scatter_dimension=0, tiled=True)  51.6 us
    all_to_all x2, waiting for transfers between devices, shards(): qkv = lax.all_to_all(got[0], CONTEXT, 0, 0, tiled=True)  47.5 us
    dot_general x16, matrix products, dot(): lax.dot_general(a, b, (((ca,), (cb,)), ((), ())), preferred_element_type=...  37.9 us
    pallas_call x4, Pallas kernels, feed_forward(): pl.pallas_call(functools.partial(up_kernel, n=n, fc=fc), grid=(1,), in_sp...  34.2 us
    all_to_all x2, waiting for transfers between devices, shards(): d_heads = lax.all_to_all(d_heads, CONTEXT, 0, 0, tiled=True)  31.8 us
  transfers between devices with their start and end apart: 87, of which 49 were waited for; matrix products, arithmetic and copies ran while one was open for 11% of the time, Pallas kernels for 24%

profile of v3, /device:TPU:0, one launch (start us, length us, event | category | flops | bytes accessed | tf_op | source)
XLA Modules:
  0.0 826.9 jit_solution(6577534546915293354)
XLA Ops:
  44.8 18.6 %collective-permute-done.5 = bf16[2,256,512]{2,1,0:T(8,128)(2,1)S(1)} collective-permute-done((bf16[2,256,512]{2,1,0:T(8,128)(2,1)S(1)}, bf16[2,256,512]{2,1,0:T(8,128)(2,1)S(1)}, u32[]{:S(2)}, u32[]{:S(2)}) %collective-permute-start.5) | collective-permute-done | bytes 524320 | tf_op jit(solution)/shard_map/ppermute | solution.py:892
  68.1 10.7 %all-to-all-done.qkv = bf16[4,3,64,1024]{3,2,1,0:T(8,128)(2,1)} async-done(((bf16[4,3,64,1024]{3,2,1,0:T(8,128)(2,1)}), bf16[4,3,64,1024]{3,2,1,0:T(8,128)(2,1)}, u32[]{:S(2)}, u32[]{:S(2)}) %all-to-all-start) | async-done | bytes 1572896 | tf_op jit(solution)/shard_map/all_to_all | solution.py:1013
  78.7 15.0 %attend.2 = (bf16[16,64,256]{2,1,0:T(8,128)(2,1)S(1)}, f32[16,64,256]{2,1,0:T(8,128)S(1)}, f32[1,4096]{1,0:T(1,128)S(1)}) custom-call(s32[397]{0:T(512)S(1)} %pad_add_fusion.2.tiles, bf16[4,3,64,1024]{3,2,1,0:T(8,128)(2,1)} %all-to-all-done.qkv, s32[1,4096]{1,0:T(1,128)S(1)} %bitcast.99, s32[1,4096]{1,0:T(1,128)S(1)} %sub.94.length), custom_call_target="tpu_custom_call" | custom-call | flops 1 | bytes 1 | tf_op jit(solution)/shard_map/attend/pallas_call | solution.py:278
  101.5 21.7 %collective-permute-start.4 = (bf16[2,6,512]{2,1,0:T(8,128)(2,1)S(1)}, bf16[2,6,512]{2,1,0:T(8,128)(2,1)S(1)}, u32[]{:S(2)}, u32[]{:S(2)}) collective-permute-start(bf16[2,6,512]{2,1,0:T(8,128)(2,1)S(1)} %pad_maximum_fusion.9), channel_id=1, source_target_pairs={{0,16},{16,0},{1,17},{17,1},{2,18},{18,2},{3,19},{19,3},{4,20},{20... | collective-permute-start | bytes 36872 | tf_op jit(solution)/shard_map/ppermute | solution.py:892
  133.1 8.5 %feed_forward.4 = (bf16[256,1024]{1,0:T(8,128)(2,1)}, bf16[256,1024]{1,0:T(8,128)(2,1)}, bf16[1024,1024]{1,0:T(8,128)(2,1)}, bf16[1024,1024]{1,0:T(8,128)(2,1)}, bf16[1024,1024]{1,0:T(8,128)(2,1)}) custom-call(bf16[256,1024]{1,0:T(8,128)(2,1)} %get-tuple-element.255.refs_0_, bf16[256,1024]{1,0:T(8,128)(2,1)} %collective-permute-done.9.refs_1_, ...), custom_call_target="tpu_custom_call" | custom-call | flops 8589934592 | bytes 1 | tf_op jit(solution)/shard_map/feed_forward/pallas_call | solution.py:733
  162.7 19.1 %all-gather.24.cloned.1.call-done = bf16[6,512,256]{2,1,0:T(8,128)(2,1)} async-done(((bf16[3,512,256]{2,1,0:T(8,128)(2,1)}), bf16[6,512,256]{2,1,0:T(8,128)(2,1)}) %all-gather.24.cloned.1.call-update) | async-done | bytes 1572880 | tf_op jit(solution)/shard_map/all_gather | solution.py:1007
  212.6 36.8 %all-to-all-done.2.qkv = bf16[4,3,64,1024]{3,2,1,0:T(8,128)(2,1)} async-done(((bf16[4,3,64,1024]{3,2,1,0:T(8,128)(2,1)}), bf16[4,3,64,1024]{3,2,1,0:T(8,128)(2,1)}, u32[]{:S(2)}, u32[]{:S(2)}) %all-to-all-start.2) | async-done | bytes 1572896 | tf_op jit(solution)/shard_map/all_to_all | solution.py:1013
  249.4 15.0 %attend.3 = (bf16[16,64,256]{2,1,0:T(8,128)(2,1)S(1)}, f32[16,64,256]{2,1,0:T(8,128)S(1)}, f32[1,4096]{1,0:T(1,128)S(1)}) custom-call(s32[397]{0:T(512)S(1)} %pad_add_fusion.2.tiles, bf16[4,3,64,1024]{3,2,1,0:T(8,128)(2,1)} %all-to-all-done.2.qkv, s32[1,4096]{1,0:T(1,128)S(1)} %bitcast.100, s32[1,4096]{1,0:T(1,128)S(1)} %sub.94.length), custom_call_target="tpu_custom_call" | custom-call | flops 1 | bytes 1 | tf_op jit(solution)/shard_map/attend/pallas_call | solution.py:278
  265.4 19.3 %all_to_all.40 = bf16[16,64,256]{2,1,0:T(8,128)(2,1)} all-to-all(bf16[16,64,256]{2,1,0:T(8,128)(2,1)S(1)} %get-tuple-element.283), channel_id=1, replica_groups=mesh['shard'=2,'context'=4,'tensor'=4] {'tensor','context'}, dimensions={0} | all-to-all | bytes 1048576 | tf_op jit(solution)/shard_map/all_to_all | solution.py:1019
  292.0 8.5 %feed_forward.6 = (bf16[256,1024]{1,0:T(8,128)(2,1)}, bf16[256,1024]{1,0:T(8,128)(2,1)}, bf16[1024,1024]{1,0:T(8,128)(2,1)}, bf16[1024,1024]{1,0:T(8,128)(2,1)}, bf16[1024,1024]{1,0:T(8,128)(2,1)}) custom-call(bf16[256,1024]{1,0:T(8,128)(2,1)} %get-tuple-element.287.refs_0_, bf16[256,1024]{1,0:T(8,128)(2,1)} %collective-permute-done.18.refs_1_, ...), custom_call_target="tpu_custom_call" | custom-call | flops 8589934592 | bytes 1 | tf_op jit(solution)/shard_map/feed_forward/pallas_call | solution.py:733
  307.3 8.5 %feed_forward.7 = (bf16[256,1024]{1,0:T(8,128)(2,1)}, bf16[256,1024]{1,0:T(8,128)(2,1)}, bf16[1024,1024]{1,0:T(8,128)(2,1)}, bf16[1024,1024]{1,0:T(8,128)(2,1)}, bf16[1024,1024]{1,0:T(8,128)(2,1)}) custom-call(bf16[256,1024]{1,0:T(8,128)(2,1)} %collective-permute-done.20.refs_0_, ...), custom_call_target="tpu_custom_call", output_to_operand_aliasing={{2}: (5, {}), {3}: (6, {}), {4}: (7, {})} | custom-call | flops 8589934592 | bytes 1 | tf_op jit(solution)/shard_map/feed_forward/pallas_call | solution.py:733
  320.7 12.6 %collective-permute-done.23.refs_3_ = bf16[256,1024]{1,0:T(8,128)(2,1)S(1)} collective-permute-done((bf16[256,1024]{1,0:T(8,128)(2,1)S(1)}, bf16[256,1024]{1,0:T(8,128)(2,1)S(1)}, u32[]{:S(2)}, u32[]{:S(2)}) %collective-permute-start.23) | collective-permute-done | bytes 524320 | tf_op jit(solution)/shard_map/ppermute | solution.py:892
  415.3 28.3 %attend_back.2 = bf16[4,3,64,1024]{3,2,1,0:T(8,128)(2,1)} custom-call(s32[781]{0:T(1024)S(1)} %pad_add_fusion.1.tiles, bf16[4,3,64,1024]{3,2,1,0:T(8,128)(2,1)} %all-to-all-done.2.qkv, s32[1,4096]{1,0:T(1,128)S(1)} %bitcast.101, s32[1,4096]{1,0:T(1,128)S(1)} %sub.94.length, f32[1,4096]{1,0:T(1,128)S(1)} %get-tuple-element.326.lse, ...), custom_call_target="tpu_custom_call" | custom-call | flops 1 | bytes 1 | tf_op jit(solution)/shard_map/attend_back/pallas_call | solution.py:389
  468.1 17.6 %all-to-all-done.5.refs_0_ = bf16[4,3,64,1024]{3,2,1,0:T(8,128)(2,1)} async-done(((bf16[4,3,64,1024]{3,2,1,0:T(8,128)(2,1)}), bf16[4,3,64,1024]{3,2,1,0:T(8,128)(2,1)}, u32[]{:S(2)}, u32[]{:S(2)}) %all-to-all-start.5) | async-done | bytes 1572896 | tf_op jit(solution)/shard_map/all_to_all | solution.py:1139
  500.2 11.2 %collective-permute-done.40.refs_3_ = bf16[256,1024]{1,0:T(8,128)(2,1)S(1)} collective-permute-done((bf16[256,1024]{1,0:T(8,128)(2,1)S(1)}, bf16[256,1024]{1,0:T(8,128)(2,1)S(1)}, u32[]{:S(2)}, u32[]{:S(2)}) %collective-permute-start.40) | collective-permute-done | bytes 524320 | tf_op jit(solution)/shard_map/ppermute | solution.py:892
  582.1 17.4 %reduce-scatter.10.cloned.1.call-done = bf16[256,512]{1,0:T(8,128)(2,1)} async-done(((bf16[1024,512]{1,0:T(8,128)(2,1)}), bf16[256,512]{1,0:T(8,128)(2,1)}) %reduce-scatter.10.cloned.1.call-update) | async-done | bytes 262160 | tf_op jit(solution)/shard_map/reduce_scatter | solution.py:1056
  602.8 27.8 %attend_back.3 = bf16[4,3,64,1024]{3,2,1,0:T(8,128)(2,1)} custom-call(s32[781]{0:T(1024)S(1)} %pad_add_fusion.1.tiles, bf16[4,3,64,1024]{3,2,1,0:T(8,128)(2,1)} %all-to-all-done.qkv, s32[1,4096]{1,0:T(1,128)S(1)} %bitcast.102, s32[1,4096]{1,0:T(1,128)S(1)} %sub.94.length, f32[1,4096]{1,0:T(1,128)S(1)} %get-tuple-element.245.lse, ...), custom_call_target="tpu_custom_call" | custom-call | flops 1 | bytes 1 | tf_op jit(solution)/shard_map/attend_back/pallas_call | solution.py:389
  644.4 11.6 %collective-permute-done.53 = bf16[256,1024]{1,0:T(8,128)(2,1)} collective-permute-done((bf16[256,1024]{1,0:T(8,128)(2,1)S(1)}, bf16[256,1024]{1,0:T(8,128)(2,1)}, u32[]{:S(2)}, u32[]{:S(2)}) %collective-permute-start.53) | collective-permute-done | bytes 524320 | tf_op jit(solution)/shard_map/ppermute | solution.py:892
  657.5 14.3 %all-to-all-done.7.refs_0_ = bf16[4,3,64,1024]{3,2,1,0:T(8,128)(2,1)} async-done(((bf16[4,3,64,1024]{3,2,1,0:T(8,128)(2,1)}), bf16[4,3,64,1024]{3,2,1,0:T(8,128)(2,1)}, u32[]{:S(2)}, u32[]{:S(2)}) %all-to-all-start.7) | async-done | bytes 1572896 | tf_op jit(solution)/shard_map/all_to_all | solution.py:1139
  684.3 22.0 %collective-permute-done.66 = bf16[256,512]{1,0:T(8,128)(2,1)S(1)} collective-permute-done((bf16[256,512]{1,0:T(8,128)(2,1)S(1)}, bf16[256,512]{1,0:T(8,128)(2,1)S(1)}, u32[]{:S(2)}, u32[]{:S(2)}) %collective-permute-start.66) | collective-permute-done | bytes 262176 | tf_op jit(solution)/shard_map/ppermute | solution.py:892
  714.4 28.9 %reduce-scatter.14.cloned.1.call-done = bf16[256,512]{1,0:T(8,128)(2,1)} async-done(((bf16[1024,512]{1,0:T(8,128)(2,1)}), bf16[256,512]{1,0:T(8,128)(2,1)}) %reduce-scatter.14.cloned.1.call-update) | async-done | bytes 262160 | tf_op jit(solution)/shard_map/reduce_scatter | solution.py:1056
  749.2 12.5 %collective-permute-done.56 = bf16[256,1024]{1,0:T(8,128)(2,1)S(1)} collective-permute-done((bf16[256,1024]{1,0:T(8,128)(2,1)S(1)}, bf16[256,1024]{1,0:T(8,128)(2,1)S(1)}, u32[]{:S(2)}, u32[]{:S(2)}) %collective-permute-start.56) | collective-permute-done | bytes 524320 | tf_op jit(solution)/shard_map/ppermute | solution.py:892
  767.9 11.3 %collective-permute-done.61 = f32[12,1024]{1,0:T(8,128)S(1)} collective-permute-done((f32[12,1024]{1,0:T(8,128)S(1)}, f32[12,1024]{1,0:T(8,128)S(1)}, u32[]{:S(2)}, u32[]{:S(2)}) %collective-permute-start.61) | collective-permute-done | bytes 49184 | tf_op jit(solution)/shard_map/ppermute | solution.py:892
  784.3 9.2 %collective-permute-done.63 = f32[15,1024]{1,0:T(8,128)S(1)} collective-permute-done((f32[15,1024]{1,0:T(8,128)S(1)}, f32[15,1024]{1,0:T(8,128)S(1)}, u32[]{:S(2)}, u32[]{:S(2)}) %collective-permute-start.63) | collective-permute-done | bytes 61472 | tf_op jit(solution)/shard_map/ppermute | solution.py:892
  (448 shorter events, 401.5 us)
Async XLA Ops:
  7.2 125.9 %all-gather.20.cloned.1.call-start = ((), (), s32[]{:S(2)}) async-start(), calls=%async_computation.21 | async-start | bytes 3145728 | tf_op jit(solution)/shard_map/all_gather | solution.py:1009
  37.3 41.4 %all-to-all-start = ((bf16[4,3,64,1024]{3,2,1,0:T(8,128)(2,1)}), bf16[4,3,64,1024]{3,2,1,0:T(8,128)(2,1)}, u32[]{:S(2)}, u32[]{:S(2)}) async-start(bf16[4,3,64,1024]{3,2,1,0:T(8,128)(2,1)} %project.3), calls=%async_computation | async-start | bytes 3145728 | tf_op jit(solution)/shard_map/all_to_all | solution.py:1013
  42.5 90.6 %all-gather.22.cloned.1.call-start = ((), (), s32[]{:S(2)}) async-start(), calls=%async_computation.22 | async-start | bytes 3145728 | tf_op jit(solution)/shard_map/all_gather | solution.py:1010
  94.5 31.1 %collective-permute-start.7 = (bf16[2,2,256,512]{3,2,1,0:T(8,128)(2,1)}, bf16[2,2,256,512]{3,2,1,0:T(8,128)(2,1)}, u32[]{:S(2)}, u32[]{:S(2)}) collective-permute-start(bf16[2,2,256,512]{3,2,1,0:T(8,128)(2,1)} %pad_maximum_fusion.1.refs_0_), channel_id=1, source_target_pairs={{0,1},{1,0},{2,3},{3,2},{4,5},{5,4},{6,7},{7,6},{8,9},{9,8},{10,11... | collective-permute-start | bytes 3145736 | tf_op jit(solution)/shard_map/ppermute | solution.py:892
  94.5 31.1 %collective-permute-start.8 = (bf16[2,2,256,512]{3,2,1,0:T(8,128)(2,1)}, bf16[2,2,256,512]{3,2,1,0:T(8,128)(2,1)}, u32[]{:S(2)}, u32[]{:S(2)}) collective-permute-start(bf16[2,2,256,512]{3,2,1,0:T(8,128)(2,1)} %collective-permute-done.6.refs_2_), channel_id=1, source_target_pairs={{0,1},{1,0},{2,3},{3,2},{4,5},{5,4},{6,7},{7,6},{8,9},{9,8},{10,11... | collective-permute-start | bytes 3145736 | tf_op jit(solution)/shard_map/ppermute | solution.py:892
  95.0 30.6 %all-to-all-start.1 = ((bf16[16,64,256]{2,1,0:T(8,128)(2,1)}), bf16[16,64,256]{2,1,0:T(8,128)(2,1)}, u32[]{:S(2)}, u32[]{:S(2)}) async-start(bf16[16,64,256]{2,1,0:T(8,128)(2,1)} %copy-done.7), calls=%async_computation.1 | async-start | bytes 1048576 | tf_op jit(solution)/shard_map/all_to_all | solution.py:1019
  99.3 82.5 %all-gather.24.cloned.1.call-start = ((), (), s32[]{:S(2)}) async-start(), calls=%async_computation.23 | async-start | bytes 2359296 | tf_op jit(solution)/shard_map/all_gather | solution.py:1007
  146.0 144.6 %all-gather.26.cloned.1.call-start = ((), (), s32[]{:S(2)}) async-start(), calls=%async_computation.24 | async-start | bytes 3145728 | tf_op jit(solution)/shard_map/all_gather | solution.py:1009
  207.4 42.0 %all-to-all-start.2 = ((bf16[4,3,64,1024]{3,2,1,0:T(8,128)(2,1)}), bf16[4,3,64,1024]{3,2,1,0:T(8,128)(2,1)}, u32[]{:S(2)}, u32[]{:S(2)}) async-start(bf16[4,3,64,1024]{3,2,1,0:T(8,128)(2,1)} %get-tuple-element.282), calls=%async_computation.2 | async-start | bytes 3145728 | tf_op jit(solution)/shard_map/all_to_all | solution.py:1013
  212.0 78.6 %all-gather.28.cloned.1.call-start = ((), (), s32[]{:S(2)}) async-start(), calls=%async_computation.25 | async-start | bytes 3145728 | tf_op jit(solution)/shard_map/all_gather | solution.py:1010
  396.8 46.8 %reduce-scatter.6.cloned.1.call-start = ((), (), s32[]{:S(2)}) async-start(), calls=%async_computation.13 | async-start | bytes 1310720 | tf_op jit(solution)/shard_map/reduce_scatter | solution.py:1056
  412.4 31.1 %collective-permute-start.31 = (bf16[512,1024]{1,0:T(8,128)(2,1)}, bf16[512,1024]{1,0:T(8,128)(2,1)}, u32[]{:S(2)}, u32[]{:S(2)}) collective-permute-start(bf16[512,1024]{1,0:T(8,128)(2,1)} %convolution_convert_fusion.2), channel_id=1, source_target_pairs={{0,16},{16,0},{1,17},{17,1},{2,18},{18,2},{3,19},{19,3},{4,20},{20... | collective-permute-start | bytes 3145736 | tf_op jit(solution)/shard_map/ppermute | solution.py:892
  412.6 30.9 %collective-permute-start.32 = (bf16[256,1024]{1,0:T(8,128)(2,1)}, bf16[256,1024]{1,0:T(8,128)(2,1)}, u32[]{:S(2)}, u32[]{:S(2)}) collective-permute-start(bf16[256,1024]{1,0:T(8,128)(2,1)} %get-tuple-element.346.refs_0_), channel_id=1, source_target_pairs={{0,2},{1,3},{2,0},{3,1},{4,6},{5,7},{6,4},{7,5},{8,10},{9,11},{10,... | collective-permute-start | bytes 1572872 | tf_op jit(solution)/shard_map/ppermute | solution.py:892
  443.6 42.1 %all-to-all-start.5 = ((bf16[4,3,64,1024]{3,2,1,0:T(8,128)(2,1)}), bf16[4,3,64,1024]{3,2,1,0:T(8,128)(2,1)}, u32[]{:S(2)}, u32[]{:S(2)}) async-start(bf16[4,3,64,1024]{3,2,1,0:T(8,128)(2,1)} %attend_back.2), calls=%async_computation.6 | async-start | bytes 3145728 | tf_op jit(solution)/shard_map/all_to_all | solution.py:1139
  448.1 68.2 %reduce-scatter.8.cloned.1.call-start = ((), (), s32[]{:S(2)}) async-start(), calls=%async_computation.14 | async-start | bytes 1310720 | tf_op jit(solution)/shard_map/reduce_scatter | solution.py:1056
  485.7 77.3 %all-gather.14.cloned.1.call-start = ((), (), s32[]{:S(2)}) async-start(), calls=%async_computation.15 | async-start | bytes 2621440 | tf_op jit(solution)/shard_map/all_gather | solution.py:1059
  518.5 81.0 %reduce-scatter.10.cloned.1.call-start = ((), (), s32[]{:S(2)}) async-start(), calls=%async_computation.16 | async-start | bytes 1310720 | tf_op jit(solution)/shard_map/reduce_scatter | solution.py:1056
  563.1 38.4 %collective-permute-start.49 = (bf16[1024,512]{1,0:T(8,128)(2,1)S(1)}, bf16[1024,512]{1,0:T(8,128)(2,1)}, u32[]{:S(2)}, u32[]{:S(2)}) collective-permute-start(bf16[1024,512]{1,0:T(8,128)(2,1)S(1)} %convolution_convert_fusion.1), channel_id=1, source_target_pairs={{0,16},{16,0},{1,17},{17,1},{2,18},{18,2},{3,19},{19,3},{4,20},{20... | collective-permute-start | bytes 3145736 | tf_op jit(solution)/shard_map/ppermute | solution.py:892
  569.8 31.6 %all-to-all-start.6 = ((bf16[16,64,256]{2,1,0:T(8,128)(2,1)}), bf16[16,64,256]{2,1,0:T(8,128)(2,1)S(1)}, u32[]{:S(2)}, u32[]{:S(2)}) async-start(bf16[16,64,256]{2,1,0:T(8,128)(2,1)} %bitcast.123), calls=%async_computation.8 | async-start | bytes 1048576 | tf_op jit(solution)/shard_map/all_to_all | solution.py:1119
  573.5 57.1 %all-gather.16.cloned.1.call-start = ((), (), s32[]{:S(2)}) async-start(), calls=%async_computation.17 | async-start | bytes 1310720 | tf_op jit(solution)/shard_map/all_gather | solution.py:1059
  630.6 41.1 %all-to-all-start.7 = ((bf16[4,3,64,1024]{3,2,1,0:T(8,128)(2,1)}), bf16[4,3,64,1024]{3,2,1,0:T(8,128)(2,1)}, u32[]{:S(2)}, u32[]{:S(2)}) async-start(bf16[4,3,64,1024]{3,2,1,0:T(8,128)(2,1)} %attend_back.3), calls=%async_computation.10 | async-start | bytes 3145728 | tf_op jit(solution)/shard_map/all_to_all | solution.py:1139
  635.0 79.1 %reduce-scatter.12.cloned.1.call-start = ((), (), s32[]{:S(2)}) async-start(), calls=%async_computation.18 | async-start | bytes 2621440 | tf_op jit(solution)/shard_map/reduce_scatter | solution.py:1056
  671.8 71.5 %reduce-scatter.14.cloned.1.call-start = ((), (), s32[]{:S(2)}) async-start(), calls=%async_computation.19 | async-start | bytes 1310720 | tf_op jit(solution)/shard_map/reduce_scatter | solution.py:1056
  714.1 100.0 %all-gather.18.cloned.1.call-start = ((), (), s32[]{:S(2)}) async-start(), calls=%async_computation.20 | async-start | bytes 3932160 | tf_op jit(solution)/shard_map/all_gather | solution.py:1059
  (133 other events, 1797.1 us)
Sparse Core Ops, SparseCore 0:
  37.4 40.3 all-gather.19
  80.0 34.2 all-gather.21
  146.2 35.5 all-gather.23
  200.1 34.9 all-gather.25
  236.5 33.1 all-gather.27
  412.6 24.9 reduce-scatter.5
  485.8 24.8 reduce-scatter.7
  518.6 43.6 all-gather.13
  565.2 34.2 reduce-scatter.9
  601.6 27.7 all-gather.15
  671.9 42.1 reduce-scatter.11
  716.8 26.4 reduce-scatter.13
  745.5 64.8 all-gather.17

commit v4 on v3

--- a/solution.py
+++ b/solution.py
@@ -920,8 +920,8 @@
     return value
 
 
-BQ, BK, UNROLL = 256, 512, 4
-BQ_BACK, BK_BACK, UNROLL_BACK = 256, 256, 4
+BQ, BK, UNROLL = 256, 512, 6
+BQ_BACK, BK_BACK, UNROLL_BACK = 256, 256, 6
 
 
 def build(n_shard, n_context, n_tensor):

time: 837 us -> 814 us (0.973)
  Pallas kernels: 228 us -> 212 us
  starting transfers between devices: 98.7 us -> 90 us
    pallas_call x2, Pallas kernels: 56.1 us -> 46.1 us  [attend_back(): pl.pallas_call(functools.partial(attend_back_kernel, bq=bq, bk=bk, seq=se...]
    ppermute x67, starting transfers between devices: 67.3 us -> 58.4 us  [swap(): return lax.ppermute(value, axis, [(i, i ^ bit) for i in range(count)])]
  transfers between devices with their start and end apart: 87 -> 87, of which waited for: 49 -> 53; matrix products, arithmetic and copies ran while one was open for 11% -> 11% of each run, Pallas kernels for 24% -> 22%
where the time goes in v4:
time: 814 us; the launch traced here: 804 us
  waiting for transfers between devices  360 us (44%)
  Pallas kernels  212 us (26%)
  starting transfers between devices  90 us (11%)
  matrix products  44.5 us (5%)
  other arithmetic  31.1 us (4%)
  local copies, waits for them, and re-layouts  28 us (3%)
  between operations  19.4 us (2%)
  blocking collectives  18.9 us (2%)
    ppermute x67, waiting for transfers between devices, swap(): return lax.ppermute(value, axis, [(i, i ^ bit) for i in range(count)])  200 us
    ppermute x67, starting transfers between devices, swap(): return lax.ppermute(value, axis, [(i, i ^ bit) for i in range(count)])  58.4 us
    reduce_scatter x5, waiting for transfers between devices, context_scatter(): return lax.psum_scatter(value, CONTEXT, scatter_dimension=0, tiled=True)  52 us
    all_to_all x2, waiting for transfers between devices, shards(): qkv = lax.all_to_all(got[0], CONTEXT, 0, 0, tiled=True)  47.7 us
    pallas_call x2, Pallas kernels, attend_back(): pl.pallas_call(functools.partial(attend_back_kernel, bq=bq, bk=bk, seq=se...  46.1 us
    dot_general x16, matrix products, dot(): lax.dot_general(a, b, (((ca,), (cb,)), ((), ())), preferred_element_type=...  37.9 us
    pallas_call x4, Pallas kernels, feed_forward(): pl.pallas_call(functools.partial(up_kernel, n=n, fc=fc), grid=(1,), in_sp...  34.2 us
    all_to_all x2, waiting for transfers between devices, shards(): d_heads = lax.all_to_all(d_heads, CONTEXT, 0, 0, tiled=True)  32 us
  transfers between devices with their start and end apart: 87, of which 53 were waited for; matrix products, arithmetic and copies ran while one was open for 11% of the time, Pallas kernels for 22%

profile of v4, /device:TPU:0, one launch (start us, length us, event | category | flops | bytes accessed | tf_op | source)
XLA Modules:
  0.0 804.5 jit_solution(12833742030213698737)
XLA Ops:
  44.8 18.5 %collective-permute-done.5 = bf16[2,256,512]{2,1,0:T(8,128)(2,1)S(1)} collective-permute-done((bf16[2,256,512]{2,1,0:T(8,128)(2,1)S(1)}, bf16[2,256,512]{2,1,0:T(8,128)(2,1)S(1)}, u32[]{:S(2)}, u32[]{:S(2)}) %collective-permute-start.5) | collective-permute-done | bytes 524320 | tf_op jit(solution)/shard_map/ppermute | solution.py:892
  68.1 10.6 %all-to-all-done.qkv = bf16[4,3,64,1024]{3,2,1,0:T(8,128)(2,1)} async-done(((bf16[4,3,64,1024]{3,2,1,0:T(8,128)(2,1)}), bf16[4,3,64,1024]{3,2,1,0:T(8,128)(2,1)}, u32[]{:S(2)}, u32[]{:S(2)}) %all-to-all-start) | async-done | bytes 1572896 | tf_op jit(solution)/shard_map/all_to_all | solution.py:1013
  78.7 11.8 %attend.2 = (bf16[16,64,256]{2,1,0:T(8,128)(2,1)S(1)}, f32[16,64,256]{2,1,0:T(8,128)S(1)}, f32[1,4096]{1,0:T(1,128)S(1)}) custom-call(s32[403]{0:T(512)S(1)} %pad_add_fusion.2.tiles, bf16[4,3,64,1024]{3,2,1,0:T(8,128)(2,1)} %all-to-all-done.qkv, s32[1,4096]{1,0:T(1,128)S(1)} %bitcast.99, s32[1,4096]{1,0:T(1,128)S(1)} %sub.94.length), custom_call_target="tpu_custom_call" | custom-call | flops 1 | bytes 1 | tf_op jit(solution)/shard_map/attend/pallas_call | solution.py:278
  119.1 8.5 %feed_forward.4 = (bf16[256,1024]{1,0:T(8,128)(2,1)}, bf16[256,1024]{1,0:T(8,128)(2,1)}, bf16[1024,1024]{1,0:T(8,128)(2,1)}, bf16[1024,1024]{1,0:T(8,128)(2,1)}, bf16[1024,1024]{1,0:T(8,128)(2,1)}) custom-call(bf16[256,1024]{1,0:T(8,128)(2,1)} %get-tuple-element.255.refs_0_, bf16[256,1024]{1,0:T(8,128)(2,1)} %collective-permute-done.9.refs_1_, ...), custom_call_target="tpu_custom_call" | custom-call | flops 8589934592 | bytes 1 | tf_op jit(solution)/shard_map/feed_forward/pallas_call | solution.py:733
  134.4 8.5 %feed_forward.5 = (bf16[256,1024]{1,0:T(8,128)(2,1)}, bf16[256,1024]{1,0:T(8,128)(2,1)}, bf16[1024,1024]{1,0:T(8,128)(2,1)}, bf16[1024,1024]{1,0:T(8,128)(2,1)}, bf16[1024,1024]{1,0:T(8,128)(2,1)}) custom-call(bf16[256,1024]{1,0:T(8,128)(2,1)} %collective-permute-done.11.refs_0_, ...), custom_call_target="tpu_custom_call", output_to_operand_aliasing={{2}: (5, {}), {3}: (6, {}), {4}: (7, {})} | custom-call | flops 8589934592 | bytes 1 | tf_op jit(solution)/shard_map/feed_forward/pallas_call | solution.py:733
  147.6 13.1 %all-gather.24.cloned.1.call-done = bf16[6,512,256]{2,1,0:T(8,128)(2,1)} async-done(((bf16[3,512,256]{2,1,0:T(8,128)(2,1)}), bf16[6,512,256]{2,1,0:T(8,128)(2,1)}) %all-gather.24.cloned.1.call-update) | async-done | bytes 1572880 | tf_op jit(solution)/shard_map/all_gather | solution.py:1007
  191.9 37.0 %all-to-all-done.2.qkv = bf16[4,3,64,1024]{3,2,1,0:T(8,128)(2,1)} async-done(((bf16[4,3,64,1024]{3,2,1,0:T(8,128)(2,1)}), bf16[4,3,64,1024]{3,2,1,0:T(8,128)(2,1)}, u32[]{:S(2)}, u32[]{:S(2)}) %all-to-all-start.2) | async-done | bytes 1572896 | tf_op jit(solution)/shard_map/all_to_all | solution.py:1013
  228.9 11.8 %attend.3 = (bf16[16,64,256]{2,1,0:T(8,128)(2,1)S(1)}, f32[16,64,256]{2,1,0:T(8,128)S(1)}, f32[1,4096]{1,0:T(1,128)S(1)}) custom-call(s32[403]{0:T(512)S(1)} %pad_add_fusion.2.tiles, bf16[4,3,64,1024]{3,2,1,0:T(8,128)(2,1)} %all-to-all-done.2.qkv, s32[1,4096]{1,0:T(1,128)S(1)} %bitcast.100, s32[1,4096]{1,0:T(1,128)S(1)} %sub.94.length), custom_call_target="tpu_custom_call" | custom-call | flops 1 | bytes 1 | tf_op jit(solution)/shard_map/attend/pallas_call | solution.py:278
  241.8 18.9 %all_to_all.40 = bf16[16,64,256]{2,1,0:T(8,128)(2,1)} all-to-all(bf16[16,64,256]{2,1,0:T(8,128)(2,1)S(1)} %get-tuple-element.283), channel_id=1, replica_groups=mesh['shard'=2,'context'=4,'tensor'=4] {'tensor','context'}, dimensions={0} | all-to-all | bytes 1048576 | tf_op jit(solution)/shard_map/all_to_all | solution.py:1019
  268.0 8.5 %feed_forward.6 = (bf16[256,1024]{1,0:T(8,128)(2,1)}, bf16[256,1024]{1,0:T(8,128)(2,1)}, bf16[1024,1024]{1,0:T(8,128)(2,1)}, bf16[1024,1024]{1,0:T(8,128)(2,1)}, bf16[1024,1024]{1,0:T(8,128)(2,1)}) custom-call(bf16[256,1024]{1,0:T(8,128)(2,1)} %get-tuple-element.287.refs_0_, bf16[256,1024]{1,0:T(8,128)(2,1)} %collective-permute-done.18.refs_1_, ...), custom_call_target="tpu_custom_call" | custom-call | flops 8589934592 | bytes 1 | tf_op jit(solution)/shard_map/feed_forward/pallas_call | solution.py:733
  283.3 8.5 %feed_forward.7 = (bf16[256,1024]{1,0:T(8,128)(2,1)}, bf16[256,1024]{1,0:T(8,128)(2,1)}, bf16[1024,1024]{1,0:T(8,128)(2,1)}, bf16[1024,1024]{1,0:T(8,128)(2,1)}, bf16[1024,1024]{1,0:T(8,128)(2,1)}) custom-call(bf16[256,1024]{1,0:T(8,128)(2,1)} %collective-permute-done.20.refs_0_, ...), custom_call_target="tpu_custom_call", output_to_operand_aliasing={{2}: (5, {}), {3}: (6, {}), {4}: (7, {})} | custom-call | flops 8589934592 | bytes 1 | tf_op jit(solution)/shard_map/feed_forward/pallas_call | solution.py:733
  296.6 12.6 %collective-permute-done.23.refs_3_ = bf16[256,1024]{1,0:T(8,128)(2,1)S(1)} collective-permute-done((bf16[256,1024]{1,0:T(8,128)(2,1)S(1)}, bf16[256,1024]{1,0:T(8,128)(2,1)S(1)}, u32[]{:S(2)}, u32[]{:S(2)}) %collective-permute-start.23) | collective-permute-done | bytes 524320 | tf_op jit(solution)/shard_map/ppermute | solution.py:892
  393.3 23.2 %attend_back.2 = bf16[4,3,64,1024]{3,2,1,0:T(8,128)(2,1)} custom-call(s32[787]{0:T(1024)S(1)} %pad_add_fusion.1.tiles, bf16[4,3,64,1024]{3,2,1,0:T(8,128)(2,1)} %all-to-all-done.2.qkv, s32[1,4096]{1,0:T(1,128)S(1)} %bitcast.101, s32[1,4096]{1,0:T(1,128)S(1)} %sub.94.length, f32[1,4096]{1,0:T(1,128)S(1)} %get-tuple-element.326.lse, ...), custom_call_target="tpu_custom_call" | custom-call | flops 1 | bytes 1 | tf_op jit(solution)/shard_map/attend_back/pallas_call | solution.py:389
  441.1 17.6 %all-to-all-done.5.refs_0_ = bf16[4,3,64,1024]{3,2,1,0:T(8,128)(2,1)} async-done(((bf16[4,3,64,1024]{3,2,1,0:T(8,128)(2,1)}), bf16[4,3,64,1024]{3,2,1,0:T(8,128)(2,1)}, u32[]{:S(2)}, u32[]{:S(2)}) %all-to-all-start.5) | async-done | bytes 1572896 | tf_op jit(solution)/shard_map/all_to_all | solution.py:1139
  473.1 11.2 %collective-permute-done.40.refs_3_ = bf16[256,1024]{1,0:T(8,128)(2,1)S(1)} collective-permute-done((bf16[256,1024]{1,0:T(8,128)(2,1)S(1)}, bf16[256,1024]{1,0:T(8,128)(2,1)S(1)}, u32[]{:S(2)}, u32[]{:S(2)}) %collective-permute-start.40) | collective-permute-done | bytes 524320 | tf_op jit(solution)/shard_map/ppermute | solution.py:892
  559.7 17.1 %reduce-scatter.10.cloned.1.call-done = bf16[256,512]{1,0:T(8,128)(2,1)} async-done(((bf16[1024,512]{1,0:T(8,128)(2,1)}), bf16[256,512]{1,0:T(8,128)(2,1)}) %reduce-scatter.10.cloned.1.call-update) | async-done | bytes 262160 | tf_op jit(solution)/shard_map/reduce_scatter | solution.py:1056
  580.0 22.9 %attend_back.3 = bf16[4,3,64,1024]{3,2,1,0:T(8,128)(2,1)} custom-call(s32[787]{0:T(1024)S(1)} %pad_add_fusion.1.tiles, bf16[4,3,64,1024]{3,2,1,0:T(8,128)(2,1)} %all-to-all-done.qkv, s32[1,4096]{1,0:T(1,128)S(1)} %bitcast.102, s32[1,4096]{1,0:T(1,128)S(1)} %sub.94.length, f32[1,4096]{1,0:T(1,128)S(1)} %get-tuple-element.245.lse, ...), custom_call_target="tpu_custom_call" | custom-call | flops 1 | bytes 1 | tf_op jit(solution)/shard_map/attend_back/pallas_call | solution.py:389
  621.5 10.9 %collective-permute-done.53 = bf16[256,1024]{1,0:T(8,128)(2,1)} collective-permute-done((bf16[256,1024]{1,0:T(8,128)(2,1)S(1)}, bf16[256,1024]{1,0:T(8,128)(2,1)}, u32[]{:S(2)}, u32[]{:S(2)}) %collective-permute-start.53) | collective-permute-done | bytes 524320 | tf_op jit(solution)/shard_map/ppermute | solution.py:892
  633.8 14.4 %all-to-all-done.7.refs_0_ = bf16[4,3,64,1024]{3,2,1,0:T(8,128)(2,1)} async-done(((bf16[4,3,64,1024]{3,2,1,0:T(8,128)(2,1)}), bf16[4,3,64,1024]{3,2,1,0:T(8,128)(2,1)}, u32[]{:S(2)}, u32[]{:S(2)}) %all-to-all-start.7) | async-done | bytes 1572896 | tf_op jit(solution)/shard_map/all_to_all | solution.py:1139
  660.9 22.0 %collective-permute-done.66 = bf16[256,512]{1,0:T(8,128)(2,1)S(1)} collective-permute-done((bf16[256,512]{1,0:T(8,128)(2,1)S(1)}, bf16[256,512]{1,0:T(8,128)(2,1)S(1)}, u32[]{:S(2)}, u32[]{:S(2)}) %collective-permute-start.66) | collective-permute-done | bytes 262176 | tf_op jit(solution)/shard_map/ppermute | solution.py:892
  691.8 28.8 %reduce-scatter.14.cloned.1.call-done = bf16[256,512]{1,0:T(8,128)(2,1)} async-done(((bf16[1024,512]{1,0:T(8,128)(2,1)}), bf16[256,512]{1,0:T(8,128)(2,1)}) %reduce-scatter.14.cloned.1.call-update) | async-done | bytes 262160 | tf_op jit(solution)/shard_map/reduce_scatter | solution.py:1056
  726.5 12.5 %collective-permute-done.56 = bf16[256,1024]{1,0:T(8,128)(2,1)S(1)} collective-permute-done((bf16[256,1024]{1,0:T(8,128)(2,1)S(1)}, bf16[256,1024]{1,0:T(8,128)(2,1)S(1)}, u32[]{:S(2)}, u32[]{:S(2)}) %collective-permute-start.56) | collective-permute-done | bytes 524320 | tf_op jit(solution)/shard_map/ppermute | solution.py:892
  745.2 11.3 %collective-permute-done.61 = f32[12,1024]{1,0:T(8,128)S(1)} collective-permute-done((f32[12,1024]{1,0:T(8,128)S(1)}, f32[12,1024]{1,0:T(8,128)S(1)}, u32[]{:S(2)}, u32[]{:S(2)}) %collective-permute-start.61) | collective-permute-done | bytes 49184 | tf_op jit(solution)/shard_map/ppermute | solution.py:892
  761.6 9.2 %collective-permute-done.63 = f32[15,1024]{1,0:T(8,128)S(1)} collective-permute-done((f32[15,1024]{1,0:T(8,128)S(1)}, f32[15,1024]{1,0:T(8,128)S(1)}, u32[]{:S(2)}, u32[]{:S(2)}) %collective-permute-start.63) | collective-permute-done | bytes 61472 | tf_op jit(solution)/shard_map/ppermute | solution.py:892
  (448 shorter events, 415.3 us)
Async XLA Ops:
  7.2 111.2 %all-gather.20.cloned.1.call-start = ((), (), s32[]{:S(2)}) async-start(), calls=%async_computation.21 | async-start | bytes 3145728 | tf_op jit(solution)/shard_map/all_gather | solution.py:1009
  37.3 41.4 %all-to-all-start = ((bf16[4,3,64,1024]{3,2,1,0:T(8,128)(2,1)}), bf16[4,3,64,1024]{3,2,1,0:T(8,128)(2,1)}, u32[]{:S(2)}, u32[]{:S(2)}) async-start(bf16[4,3,64,1024]{3,2,1,0:T(8,128)(2,1)} %project.3), calls=%async_computation | async-start | bytes 3145728 | tf_op jit(solution)/shard_map/all_to_all | solution.py:1013
  42.5 75.8 %all-gather.22.cloned.1.call-start = ((), (), s32[]{:S(2)}) async-start(), calls=%async_computation.22 | async-start | bytes 3145728 | tf_op jit(solution)/shard_map/all_gather | solution.py:1010
  64.5 26.9 %collective-permute-start.6 = (bf16[2,2,256,512]{3,2,1,0:T(8,128)(2,1)}, bf16[2,2,256,512]{3,2,1,0:T(8,128)(2,1)}, u32[]{:S(2)}, u32[]{:S(2)}) collective-permute-start(bf16[2,2,256,512]{3,2,1,0:T(8,128)(2,1)} %pad_maximum_fusion.1.refs_0_), channel_id=1, source_target_pairs={{0,2},{1,3},{2,0},{3,1},{4,6},{5,7},{6,4},{7,5},{8,10},{9,11},{10,... | collective-permute-start | bytes 3145736 | tf_op jit(solution)/shard_map/ppermute | solution.py:892
  96.1 64.6 %all-gather.24.cloned.1.call-start = ((), (), s32[]{:S(2)}) async-start(), calls=%async_computation.23 | async-start | bytes 2359296 | tf_op jit(solution)/shard_map/all_gather | solution.py:1007
  132.2 134.4 %all-gather.26.cloned.1.call-start = ((), (), s32[]{:S(2)}) async-start(), calls=%async_computation.24 | async-start | bytes 3145728 | tf_op jit(solution)/shard_map/all_gather | solution.py:1009
  187.0 42.0 %all-to-all-start.2 = ((bf16[4,3,64,1024]{3,2,1,0:T(8,128)(2,1)}), bf16[4,3,64,1024]{3,2,1,0:T(8,128)(2,1)}, u32[]{:S(2)}, u32[]{:S(2)}) async-start(bf16[4,3,64,1024]{3,2,1,0:T(8,128)(2,1)} %get-tuple-element.282), calls=%async_computation.2 | async-start | bytes 3145728 | tf_op jit(solution)/shard_map/all_to_all | solution.py:1013
  191.3 75.3 %all-gather.28.cloned.1.call-start = ((), (), s32[]{:S(2)}) async-start(), calls=%async_computation.25 | async-start | bytes 3145728 | tf_op jit(solution)/shard_map/all_gather | solution.py:1010
  355.8 29.1 %collective-permute-start.30 = (bf16[1024,512]{1,0:T(8,128)(2,1)}, bf16[1024,512]{1,0:T(8,128)(2,1)}, u32[]{:S(2)}, u32[]{:S(2)}) collective-permute-start(bf16[1024,512]{1,0:T(8,128)(2,1)} %convolution_convert_fusion.3), channel_id=1, source_target_pairs={{0,16},{16,0},{1,17},{17,1},{2,18},{18,2},{3,19},{19,3},{4,20},{20... | collective-permute-start | bytes 3145736 | tf_op jit(solution)/shard_map/ppermute | solution.py:892
  374.8 41.7 %reduce-scatter.6.cloned.1.call-start = ((), (), s32[]{:S(2)}) async-start(), calls=%async_computation.13 | async-start | bytes 1310720 | tf_op jit(solution)/shard_map/reduce_scatter | solution.py:1056
  390.5 26.0 %collective-permute-start.31 = (bf16[512,1024]{1,0:T(8,128)(2,1)}, bf16[512,1024]{1,0:T(8,128)(2,1)}, u32[]{:S(2)}, u32[]{:S(2)}) collective-permute-start(bf16[512,1024]{1,0:T(8,128)(2,1)} %convolution_convert_fusion.2), channel_id=1, source_target_pairs={{0,16},{16,0},{1,17},{17,1},{2,18},{18,2},{3,19},{19,3},{4,20},{20... | collective-permute-start | bytes 3145736 | tf_op jit(solution)/shard_map/ppermute | solution.py:892
  390.7 25.8 %collective-permute-start.32 = (bf16[256,1024]{1,0:T(8,128)(2,1)}, bf16[256,1024]{1,0:T(8,128)(2,1)}, u32[]{:S(2)}, u32[]{:S(2)}) collective-permute-start(bf16[256,1024]{1,0:T(8,128)(2,1)} %get-tuple-element.346.refs_0_), channel_id=1, source_target_pairs={{0,2},{1,3},{2,0},{3,1},{4,6},{5,7},{6,4},{7,5},{8,10},{9,11},{10,... | collective-permute-start | bytes 1572872 | tf_op jit(solution)/shard_map/ppermute | solution.py:892
  416.5 42.1 %all-to-all-start.5 = ((bf16[4,3,64,1024]{3,2,1,0:T(8,128)(2,1)}), bf16[4,3,64,1024]{3,2,1,0:T(8,128)(2,1)}, u32[]{:S(2)}, u32[]{:S(2)}) async-start(bf16[4,3,64,1024]{3,2,1,0:T(8,128)(2,1)} %attend_back.2), calls=%async_computation.6 | async-start | bytes 3145728 | tf_op jit(solution)/shard_map/all_to_all | solution.py:1139
  421.0 68.2 %reduce-scatter.8.cloned.1.call-start = ((), (), s32[]{:S(2)}) async-start(), calls=%async_computation.14 | async-start | bytes 1310720 | tf_op jit(solution)/shard_map/reduce_scatter | solution.py:1056
  458.7 81.1 %all-gather.14.cloned.1.call-start = ((), (), s32[]{:S(2)}) async-start(), calls=%async_computation.15 | async-start | bytes 2621440 | tf_op jit(solution)/shard_map/all_gather | solution.py:1059
  491.4 85.3 %reduce-scatter.10.cloned.1.call-start = ((), (), s32[]{:S(2)}) async-start(), calls=%async_computation.16 | async-start | bytes 1310720 | tf_op jit(solution)/shard_map/reduce_scatter | solution.py:1056
  492.4 28.8 %collective-permute-start.44 = (bf16[3,512,256]{1,2,0:T(8,128)(2,1)}, bf16[3,512,256]{1,2,0:T(8,128)(2,1)S(1)}, u32[]{:S(2)}, u32[]{:S(2)}) collective-permute-start(bf16[3,512,256]{1,2,0:T(8,128)(2,1)} %fusion.2), channel_id=1, source_target_pairs={{0,16},{16,0},{1,17},{17,1},{2,18},{18,2},{3,19},{19,3},{4,20},{20... | collective-permute-start | bytes 2359304 | tf_op jit(solution)/shard_map/ppermute | solution.py:892
  539.8 39.1 %collective-permute-start.49 = (bf16[1024,512]{1,0:T(8,128)(2,1)S(1)}, bf16[1024,512]{1,0:T(8,128)(2,1)}, u32[]{:S(2)}, u32[]{:S(2)}) collective-permute-start(bf16[1024,512]{1,0:T(8,128)(2,1)S(1)} %convolution_convert_fusion.1), channel_id=1, source_target_pairs={{0,16},{16,0},{1,17},{17,1},{2,18},{18,2},{3,19},{19,3},{4,20},{20... | collective-permute-start | bytes 3145736 | tf_op jit(solution)/shard_map/ppermute | solution.py:892
  547.3 31.6 %all-to-all-start.6 = ((bf16[16,64,256]{2,1,0:T(8,128)(2,1)}), bf16[16,64,256]{2,1,0:T(8,128)(2,1)S(1)}, u32[]{:S(2)}, u32[]{:S(2)}) async-start(bf16[16,64,256]{2,1,0:T(8,128)(2,1)} %bitcast.123), calls=%async_computation.8 | async-start | bytes 1048576 | tf_op jit(solution)/shard_map/all_to_all | solution.py:1119
  551.0 55.7 %all-gather.16.cloned.1.call-start = ((), (), s32[]{:S(2)}) async-start(), calls=%async_computation.17 | async-start | bytes 1310720 | tf_op jit(solution)/shard_map/all_gather | solution.py:1059
  606.7 41.5 %all-to-all-start.7 = ((bf16[4,3,64,1024]{3,2,1,0:T(8,128)(2,1)}), bf16[4,3,64,1024]{3,2,1,0:T(8,128)(2,1)}, u32[]{:S(2)}, u32[]{:S(2)}) async-start(bf16[4,3,64,1024]{3,2,1,0:T(8,128)(2,1)} %attend_back.3), calls=%async_computation.10 | async-start | bytes 3145728 | tf_op jit(solution)/shard_map/all_to_all | solution.py:1139
  611.1 80.3 %reduce-scatter.12.cloned.1.call-start = ((), (), s32[]{:S(2)}) async-start(), calls=%async_computation.18 | async-start | bytes 2621440 | tf_op jit(solution)/shard_map/reduce_scatter | solution.py:1056
  648.3 72.3 %reduce-scatter.14.cloned.1.call-start = ((), (), s32[]{:S(2)}) async-start(), calls=%async_computation.19 | async-start | bytes 1310720 | tf_op jit(solution)/shard_map/reduce_scatter | solution.py:1056
  691.4 100.0 %all-gather.18.cloned.1.call-start = ((), (), s32[]{:S(2)}) async-start(), calls=%async_computation.20 | async-start | bytes 3932160 | tf_op jit(solution)/shard_map/all_gather | solution.py:1059
  (133 other events, 1741.5 us)
Sparse Core Ops, SparseCore 0:
  37.4 40.3 all-gather.19
  79.9 34.5 all-gather.21
  132.3 28.3 all-gather.23
  179.7 34.2 all-gather.25
  215.4 33.1 all-gather.27
  390.6 24.9 reduce-scatter.5
  458.8 29.2 reduce-scatter.7
  491.5 47.9 all-gather.13
  542.4 34.2 reduce-scatter.9
  579.0 27.6 all-gather.15
  648.4 42.9 reduce-scatter.11
  694.1 26.4 reduce-scatter.13
  722.8 64.8 all-gather.17
